TPU v7x, 32 devices: a whole 2x2x4 slice. The times are simulated.
32 devices in a mesh: row: 4 (over y, x), seq: 8 (over z, core).
Axes of the slice: x: 2, y: 2, z: 4, core: 2. Of those that a mesh axis runs over, the one named last changes fastest.
Arguments:
- inputs: bfloat16 [4, 1024, 768], P('row', 'seq'), may hold values from -6 to 6
- documents: int32 [4, 1024], P('row', 'seq'), may hold values from 0 to 3, never falling along the last dimension, each value on 1 to 768 neighbouring positions
- offsets: int32 [5, 12], replicated, may hold values from 0 to 11, as said below
- ln1_gain: float32 [768], replicated, may hold values from 0.1 to 1.9
- ln1_bias: float32 [768], replicated, may hold values from -0.5 to 0.5
- qkv_weight: bfloat16 [768, 2304], replicated, may hold values from -0.21875 to 0.21875
- out_weight: bfloat16 [768, 768], replicated, may hold values from -0.875 to 0.875
- ln2_gain: float32 [768], replicated, may hold values from 0.1 to 1.9
- ln2_bias: float32 [768], replicated, may hold values from -0.5 to 0.5
- up_weight: bfloat16 [768, 3072], replicated, may hold values from -0.21875 to 0.21875
- down_weight: bfloat16 [3072, 768], replicated, may hold values from -0.109375 to 0.109375
- cotangent: bfloat16 [4, 1024, 768], P('row', 'seq'), may hold values from -6 to 6
Outputs:
- outputs: bfloat16 [4, 1024, 768], P('row', 'seq')
- grad_inputs: bfloat16 [4, 1024, 768], P('row', 'seq')
- grad_ln1_gain: float32 [768], P('row')
- grad_ln1_bias: float32 [768], P('row')
- grad_qkv: float32 [768, 2304], P('row')
- grad_out: float32 [768, 768], P('row')
- grad_ln2_gain: float32 [768], P('row')
- grad_ln2_bias: float32 [768], P('row')
- grad_up: float32 [768, 3072], P('row')
- grad_down: float32 [3072, 768], P('row')
Inputs may be any that keep to these rules, and one draw needn't show every extreme that they name: Row k of offsets gives the heads' offsets for pattern k, of rate 1, 2, 4, 6, 12 (k = 0 .. 4): each offset 0 .. rate - 1 is taken by 12 / rate heads.
All inputs are finite; a program needn't handle non-finite values.
Results may differ from a plain program's by a relative error of at most 0.013.
Values may be sent and summed in bfloat16 or wider, within the bound.
No kernel may reach another device: no remote copies, remote signals or barrier semaphores. Data moves between devices by JAX's collectives and lax.ppermute only.
A program may use at most 320 MiB of HBM per device.

v0:
```python
from functools import partial

import jax
import jax.numpy as jnp
from jax import lax
from jax.sharding import PartitionSpec as P

reaches = (2048, 4096, 8192, 16384, 32768)
dilations = (1, 2, 4, 6, 12)
epsilon = 1e-05
masked_score = -1e30
far_code = 1 << 30


def partner_2(value, axis, apart):
    mask = 2**apart
    pairs = [(source, source ^ mask) for source in range(lax.axis_size(axis))]
    return lax.ppermute(value, axis, pairs)


def layer_norm(values, gain_vec, shift_vec):
    centered = values - jnp.mean(values, axis=-1, keepdims=True)
    variance = jnp.mean(centered * centered, axis=-1, keepdims=True)
    return centered * lax.rsqrt(variance + epsilon) * gain_vec + shift_vec


def gelu_exact(values):
    return jax.nn.gelu(values, approximate=False)


def take_slots(array, index_table):
    return jnp.take_along_axis(array, index_table[:, :, None], axis=0)


def head_slice(array, head_block, block_width):
    return lax.dynamic_slice_in_dim(array, head_block * block_width, block_width, 1)


def doc_starts(doc_row, positions):
    earlier = jnp.concatenate(
        [jnp.zeros((1,), jnp.int32), (doc_row[1:] != doc_row[:-1]).astype(jnp.int32)]
    )
    first_at = lax.cummax(
        jnp.where(earlier == 1, jnp.arange(doc_row.shape[0], dtype=jnp.int32), 0), axis=0
    )
    return first_at[positions]


def group_keys(offset_row, dilation, tokens, group_size, seg_start, slot_count):
    member = jnp.arange(group_size, dtype=jnp.int32)[:, None, None]
    slot_ids = jnp.arange(slot_count, dtype=jnp.int32)[None, :, None]
    first_idx = jnp.mod(offset_row[None, None, :] - member * tokens, dilation)
    raw_local = first_idx + dilation * slot_ids
    key_ok = raw_local < tokens
    key_pos = seg_start + member * tokens + jnp.minimum(raw_local, tokens - 1)
    key_code = jnp.where(key_ok, key_pos, far_code)
    return key_code.reshape(group_size * slot_count, -1)


def collect_double(pair, group_size, group_pos):
    gathered = pair
    for bit_pos in range(group_size.bit_length() - 1):
        partner = partner_2(gathered, "seq", bit_pos)
        upper_side = group_pos >> bit_pos & 1 == 1
        first_half = jnp.where(upper_side, partner, gathered)
        second_half = jnp.where(upper_side, gathered, partner)
        gathered = jnp.concatenate([first_half, second_half], 1)
    return gathered


def reduce_double(grads, group_size, group_pos):
    bit_total = group_size.bit_length() - 1
    for bit_pos in reversed(range(bit_total)):
        half_len = grads.shape[1] // 2
        lower_half = grads[:, :half_len]
        upper_half = grads[:, half_len:]
        upper_side = group_pos >> bit_pos & 1 == 1
        kept_half = jnp.where(upper_side, lower_half, upper_half)
        sent_half = jnp.where(upper_side, upper_half, lower_half)
        grads = kept_half + partner_2(sent_half.astype(jnp.bfloat16), "seq", bit_pos).astype(
            sent_half.dtype
        )
    for bit_pos in range(bit_total):
        grads = partner_2(grads.astype(jnp.bfloat16), "seq", bit_pos).astype(grads.dtype)
    return grads


def block_scores(context, head_block):
    query_slots, key_all, query_pos, query_low, key_code, block_width, score_scale = context
    query_part = head_slice(query_slots, head_block, block_width)
    key_part = head_slice(key_all, head_block, block_width)
    qpos_part = jnp.transpose(head_slice(query_pos, head_block, block_width))
    qlow_part = jnp.transpose(head_slice(query_low, head_block, block_width))
    kcode_part = jnp.transpose(head_slice(key_code, head_block, block_width))
    allowed = (kcode_part[:, None, :] <= qpos_part[:, :, None]) & (
        kcode_part[:, None, :] >= qlow_part[:, :, None]
    )
    raw_scores = (
        jnp.einsum("qhe,khe->hqk", query_part, key_part, preferred_element_type=jnp.float32)
        * score_scale
    )
    return (jnp.where(allowed, raw_scores, masked_score), query_part, key_part)


def forward_block(context, value_all, head_block):
    block_width = context[5]
    scores, query_part, key_part = block_scores(context, head_block)
    row_top = jnp.max(scores, axis=-1, keepdims=True)
    log_total = jnp.log(jnp.sum(jnp.exp(scores - row_top), axis=-1, keepdims=True)) + row_top
    probability = jnp.exp(scores - log_total).astype(jnp.bfloat16)
    value_part = head_slice(value_all, head_block, block_width)
    attended = jnp.einsum(
        "hqk,khe->qhe", probability, value_part, preferred_element_type=jnp.float32
    )
    return (attended, jnp.transpose(log_total[:, :, 0]))


def backward_block(context, value_all, lse_slots, grad_slots, lse_grad_slots, head_block):
    block_width = context[5]
    score_scale = context[6]
    scores, query_part, key_part = block_scores(context, head_block)
    lse_part = jnp.transpose(head_slice(lse_slots, head_block, block_width))
    probability = jnp.exp(scores - lse_part[:, :, None])
    grad_part = head_slice(grad_slots, head_block, block_width)
    dlse_part = jnp.transpose(head_slice(lse_grad_slots, head_block, block_width))
    value_part = head_slice(value_all, head_block, block_width)
    grad_prob = jnp.einsum(
        "qhe,khe->hqk", grad_part, value_part, preferred_element_type=jnp.float32
    )
    delta_sum = jnp.sum(probability * grad_prob, axis=-1, keepdims=True)
    grad_score = (probability * (grad_prob - delta_sum + dlse_part[:, :, None])).astype(
        jnp.bfloat16
    )
    grad_query = (
        jnp.einsum("hqk,khe->qhe", grad_score, key_part, preferred_element_type=jnp.float32)
        * score_scale
    )
    grad_key = (
        jnp.einsum("hqk,qhe->khe", grad_score, query_part, preferred_element_type=jnp.float32)
        * score_scale
    )
    grad_value = jnp.einsum(
        "hqk,qhe->khe",
        probability.astype(jnp.bfloat16),
        grad_part,
        preferred_element_type=jnp.float32,
    )
    return (grad_query, grad_key, grad_value)


def join_heads(stacked):
    moved = jnp.moveaxis(stacked, 0, 1)
    return moved.reshape(moved.shape[0], moved.shape[1] * moved.shape[2], *moved.shape[3:])


def shards(
    inputs,
    documents,
    offsets,
    ln1_gain,
    ln1_bias,
    qkv_weight,
    out_weight,
    ln2_gain,
    ln2_bias,
    up_weight,
    down_weight,
    cotangent,
):
    tokens = inputs.shape[1]
    model_dim = inputs.shape[2]
    head_count = offsets.shape[1]
    head_dim = model_dim // head_count
    seq_count = lax.axis_size("seq")
    seq_index = lax.axis_index("seq")
    row_len = tokens * seq_count
    score_scale = float(head_dim) ** (-0.5)
    doc_row = lax.all_gather(documents, "seq", axis=1, tiled=True)[0]
    source = inputs[0].astype(jnp.float32)
    normed_one, norm_one_back = jax.vjp(layer_norm, source, ln1_gain, ln1_bias)
    normed_one_low = normed_one.astype(jnp.bfloat16)
    packed = jnp.dot(normed_one_low, qkv_weight, preferred_element_type=jnp.float32).astype(
        jnp.bfloat16
    )
    queries = packed[:, :model_dim].reshape(tokens, head_count, head_dim)
    key_rows = packed[:, model_dim : 2 * model_dim].reshape(tokens, head_count, head_dim)
    value_rows = packed[:, 2 * model_dim :].reshape(tokens, head_count, head_dim)
    token_ids = jnp.arange(tokens, dtype=jnp.int32)[:, None]
    saved = []
    out_list = []
    lse_list = []
    for pattern_id in range(len(reaches)):
        dilation = dilations[pattern_id]
        span_len = min(reaches[pattern_id], row_len)
        group_size = span_len // tokens
        group_pos = seq_index % group_size
        seg_start = seq_index // group_size * span_len
        offset_row = offsets[pattern_id]
        slot_count = (tokens + dilation - 1) // dilation
        slot_ids = jnp.arange(slot_count, dtype=jnp.int32)[:, None]
        first_idx = jnp.mod(offset_row[None, :] - group_pos * tokens, dilation)
        raw_local = first_idx + dilation * slot_ids
        query_ok = raw_local < tokens
        local_idx = jnp.minimum(raw_local, tokens - 1)
        query_pos = seg_start + group_pos * tokens + local_idx
        query_low = doc_starts(doc_row, query_pos)
        query_slots = take_slots(queries, local_idx)
        pair = jnp.stack(
            [take_slots(key_rows, local_idx), take_slots(value_rows, local_idx)]
        ).reshape(2, 1, slot_count, model_dim)
        pair_all = collect_double(pair, group_size, group_pos)
        key_all = pair_all[0].reshape(group_size * slot_count, head_count, head_dim)
        value_all = pair_all[1].reshape(group_size * slot_count, head_count, head_dim)
        key_code = group_keys(offset_row, dilation, tokens, group_size, seg_start, slot_count)
        context = (query_slots, key_all, query_pos, query_low, key_code, dilation, score_scale)
        block_count = head_count // dilation
        out_blocks, lse_blocks = lax.map(
            partial(forward_block, context, value_all), jnp.arange(block_count, dtype=jnp.int32)
        )
        out_slots = join_heads(out_blocks)
        lse_slots = join_heads(lse_blocks)
        offset_diff = token_ids - first_idx
        covered = (offset_diff >= 0) & (jnp.mod(offset_diff, dilation) == 0)
        token_slot = jnp.clip(offset_diff // dilation, 0, slot_count - 1)
        out_tokens = jnp.where(covered[:, :, None], take_slots(out_slots, token_slot), 0.0)
        lse_tokens = jnp.where(
            covered, jnp.take_along_axis(lse_slots, token_slot, axis=0), masked_score
        )
        out_list.append(out_tokens)
        lse_list.append(lse_tokens)
        saved.append(
            (
                context,
                value_all,
                lse_slots,
                local_idx,
                query_ok,
                covered,
                token_slot,
                group_size,
                group_pos,
                block_count,
                slot_count,
            )
        )
    lse_stack = jnp.stack(lse_list)
    row_top = jnp.max(lse_stack, axis=0)
    log_norm = row_top + jnp.log(jnp.sum(jnp.exp(lse_stack - row_top), axis=0))
    mix_weights = jnp.exp(lse_stack - log_norm)
    mixed = jnp.sum(mix_weights[..., None] * jnp.stack(out_list), axis=0)
    attended_low = mixed.reshape(tokens, model_dim).astype(jnp.bfloat16)
    middle = source + jnp.dot(attended_low, out_weight, preferred_element_type=jnp.float32)
    normed_two, norm_two_back = jax.vjp(layer_norm, middle, ln2_gain, ln2_bias)
    normed_two_low = normed_two.astype(jnp.bfloat16)
    hidden_pre = jnp.dot(normed_two_low, up_weight, preferred_element_type=jnp.float32)
    hidden, gelu_back = jax.vjp(gelu_exact, hidden_pre)
    hidden_low = hidden.astype(jnp.bfloat16)
    result = middle + jnp.dot(hidden_low, down_weight, preferred_element_type=jnp.float32)
    grad_result = cotangent[0]
    grad_down = jnp.einsum("tf,td->fd", hidden_low, grad_result, preferred_element_type=jnp.float32)
    grad_hidden = jnp.einsum(
        "td,fd->tf", grad_result, down_weight, preferred_element_type=jnp.float32
    )
    grad_pre = gelu_back(grad_hidden)[0].astype(jnp.bfloat16)
    grad_up = jnp.einsum("td,tf->df", normed_two_low, grad_pre, preferred_element_type=jnp.float32)
    grad_normed_two = jnp.einsum(
        "tf,df->td", grad_pre, up_weight, preferred_element_type=jnp.float32
    )
    grad_middle_part, grad_ln2_gain, grad_ln2_bias = norm_two_back(grad_normed_two)
    grad_middle = grad_result.astype(jnp.float32) + grad_middle_part
    grad_branch = grad_middle.astype(jnp.bfloat16)
    grad_out = jnp.einsum(
        "td,te->de", attended_low, grad_branch, preferred_element_type=jnp.float32
    )
    grad_mixed = jnp.einsum(
        "te,de->td", grad_branch, out_weight, preferred_element_type=jnp.float32
    ).reshape(tokens, head_count, head_dim)
    grad_q_tokens = jnp.zeros((tokens, head_count, head_dim), jnp.float32)
    grad_k_tokens = jnp.zeros((tokens, head_count, head_dim), jnp.float32)
    grad_v_tokens = jnp.zeros((tokens, head_count, head_dim), jnp.float32)
    for pattern_id in range(len(reaches)):
        (
            context,
            value_all,
            lse_slots,
            local_idx,
            query_ok,
            covered,
            token_slot,
            group_size,
            group_pos,
            block_count,
            slot_count,
        ) = saved[pattern_id]
        weight_now = mix_weights[pattern_id]
        lse_grad_tokens = weight_now * jnp.sum((out_list[pattern_id] - mixed) * grad_mixed, axis=-1)
        out_grad_tokens = (weight_now[:, :, None] * grad_mixed).astype(jnp.bfloat16)
        grad_slots = jnp.where(
            query_ok[:, :, None],
            take_slots(out_grad_tokens, local_idx),
            jnp.zeros((), jnp.bfloat16),
        )
        lse_grad_slots = jnp.where(
            query_ok, jnp.take_along_axis(lse_grad_tokens, local_idx, axis=0), 0.0
        )
        query_blocks, key_blocks, value_blocks = lax.map(
            partial(backward_block, context, value_all, lse_slots, grad_slots, lse_grad_slots),
            jnp.arange(block_count, dtype=jnp.int32),
        )
        grad_query_slots = join_heads(query_blocks)
        grad_pair = jnp.stack(
            [
                join_heads(key_blocks).reshape(group_size, slot_count, model_dim),
                join_heads(value_blocks).reshape(group_size, slot_count, model_dim),
            ]
        )
        own_pair = reduce_double(grad_pair, group_size, group_pos)
        grad_key_slots = own_pair[0].reshape(slot_count, head_count, head_dim)
        grad_value_slots = own_pair[1].reshape(slot_count, head_count, head_dim)
        cover_mask = covered[:, :, None]
        grad_q_tokens = grad_q_tokens + jnp.where(
            cover_mask, take_slots(grad_query_slots, token_slot), 0.0
        )
        grad_k_tokens = grad_k_tokens + jnp.where(
            cover_mask, take_slots(grad_key_slots, token_slot), 0.0
        )
        grad_v_tokens = grad_v_tokens + jnp.where(
            cover_mask, take_slots(grad_value_slots, token_slot), 0.0
        )
    grad_packed = jnp.concatenate(
        [
            grad_q_tokens.reshape(tokens, model_dim),
            grad_k_tokens.reshape(tokens, model_dim),
            grad_v_tokens.reshape(tokens, model_dim),
        ],
        axis=1,
    ).astype(jnp.bfloat16)
    grad_qkv = jnp.einsum(
        "td,tf->df", normed_one_low, grad_packed, preferred_element_type=jnp.float32
    )
    grad_normed_one = jnp.einsum(
        "tf,df->td", grad_packed, qkv_weight, preferred_element_type=jnp.float32
    )
    grad_source_part, grad_ln1_gain, grad_ln1_bias = norm_one_back(grad_normed_one)
    grad_inputs = (grad_middle + grad_source_part).astype(jnp.bfloat16)[None]
    local_grads = (
        grad_ln1_gain,
        grad_ln1_bias,
        grad_qkv,
        grad_out,
        grad_ln2_gain,
        grad_ln2_bias,
        grad_up,
        grad_down,
    )
    row_count = lax.axis_size("row")
    flat_grads = jnp.concatenate(
        [grad_item.reshape(row_count, -1) for grad_item in local_grads], axis=1
    )
    share_len = flat_grads.shape[1]
    padded_len = -(-share_len // seq_count) * seq_count
    padded = flat_grads.reshape(-1)
    share = lax.psum_scatter(padded, ("row", "seq"), scatter_dimension=0, tiled=True)
    summed = lax.all_gather(share.astype(jnp.bfloat16), "seq", axis=0, tiled=True).astype(
        share.dtype
    )
    pieces = []
    cursor = 0
    for grad_item in local_grads:
        item_count = grad_item.size // row_count
        piece_shape = (grad_item.shape[0] // row_count,) + grad_item.shape[1:]
        pieces.append(summed[cursor : cursor + item_count].reshape(piece_shape))
        cursor = cursor + item_count
    return (
        result.astype(jnp.bfloat16)[None],
        grad_inputs,
        pieces[0],
        pieces[1],
        pieces[2],
        pieces[3],
        pieces[4],
        pieces[5],
        pieces[6],
        pieces[7],
    )


def solution(mesh):
    placed = (
        P("row", "seq", None),
        P("row", "seq"),
        P(),
        P(),
        P(),
        P(),
        P(),
        P(),
        P(),
        P(),
        P(),
        P("row", "seq", None),
    )
    return jax.shard_map(
        shards,
        mesh=mesh,
        in_specs=placed,
        out_specs=(
            P("row", "seq", None),
            P("row", "seq", None),
            P("row"),
            P("row"),
            P("row", None),
            P("row", None),
            P("row"),
            P("row"),
            P("row", None),
            P("row", None),
        ),
        check_vma=False,
    )
```

profile of v0, /device:TPU:15, one launch (start us, length us, event | category | flops | bytes accessed | tf_op | source)
XLA Modules:
  0.0 2614.5 jit_solution(9454261710031480664)
XLA Ops:
  54.6 7.4 gather_fusion.23
  62.1 7.0 gather_fusion.24
  69.0 7.0 gather_fusion.25
  122.8 7.3 gather_fusion.17
  130.1 7.2 gather_fusion.18
  137.3 7.2 gather_fusion.19
  160.7 16.4 gather_fusion.13
  177.1 16.4 gather_fusion.14
  193.5 16.5 gather_fusion.15
  248.3 9.1 all_gather.6
  334.5 9.5 gather_fusion
  396.2 16.9 gather_fusion.8
  420.5 12.9 gather_fusion.33
  457.5 14.2 while.118
  472.4 17.0 gather_fusion.7
  495.3 13.2 gather_fusion.32
  528.7 19.1 while.117
  548.4 17.0 gather_fusion.6
  571.4 13.3 gather_fusion.31
  610.2 38.5 %while.116 = (s32[]{:T(128)}, f32[6,64,2,64]{1,3,2,0:T(8,128)}, f32[6,64,2]{1,2,0:T(2,128)}, s32[6]{0:T(128)S(1)}, bf16[512,12,64]{0,2,1:T(8,128)(2,1)}, /*index...) while((s32[]{:T(128)}, f32[6,64,2,64]{1,3,2,0:T(8,128)}, ...), condition=%wide.region_11.15_spmd, body=%wide.region_8.14_spmd.sunk | while | flops 17432452 | bytes 1169099 | solution.py:217
  649.4 17.0 gather_fusion.5
  674.3 13.3 gather_fusion.30
  709.8 111.2 %while.115 = (s32[]{:T(128)}, f32[12,128,1,64]{1,3,2,0:T(8,128)}, f32[12,128,1]{1,0,2:T(8,128)}, s32[12]{0:T(128)}, bf16[1024,12,64]{0,2,1:T(8,128)(2,1)}, /*ind...) while((s32[]{:T(128)}, f32[12,128,1,64]{1,3,2,0:T(8,128)}, ...), condition=%wide.region_7.9_spmd, body=%wide.region_4.8_spmd.sunk | while | flops 34865028 | bytes 1907927 | solution.py:217
  821.1 18.0 gather_fusion.16
  849.6 24.2 gather_fusion.29
  882.8 8.1 multiply_convert_fusion.1
  916.5 6.4 fusion.423
  931.3 16.7 gather_fusion.34
  955.0 17.8 gather_fusion.35
  978.4 155.7 %while.119 = (s32[]{:T(128)}, f32[12,128,1,64]{1,3,2,0:T(8,128)}, f32[12,1024,1,64]{1,3,2,0:T(8,128)}, f32[12,1024,1,64]{1,3,2,0:T(8,128)}, s32[12]{0:T(128)}, /...) while((s32[]{:T(128)}, f32[12,128,1,64]{1,3,2,0:T(8,128)}, ...), condition=%wide.region_31.43_spmd, body=%wide.region_29.42_spmd.sunk | while | flops 85663616 | bytes 4971235 | solution.py:306
  1143.9 7.5 gather_fusion.37
  1153.1 7.7 gather_fusion.9
  1168.4 96.6 %while.120 = (s32[]{:T(128)}, f32[6,64,2,64]{1,3,2,0:T(8,128)}, f32[6,512,2,64]{1,3,2,0:T(8,128)}, f32[6,512,2,64]{1,3,2,0:T(8,128)}, s32[6]{0:T(128)}, /*index=...) while((s32[]{:T(128)}, f32[6,64,2,64]{1,3,2,0:T(8,128)}, ...), condition=%wide.region_35.47_spmd, body=%wide.region_33.46_spmd.sunk | while | flops 43132164 | bytes 4102423 | solution.py:306
  1301.2 43.2 %while.121 = (s32[]{:T(128)}, f32[3,32,4,64]{3,1,2,0:T(8,128)}, f32[3,256,4,64]{1,3,2,0:T(8,128)}, f32[3,256,4,64]{1,3,2,0:T(8,128)}, s32[3]{0:T(128)S(1)}, /*in...) while((s32[]{:T(128)}, f32[3,32,4,64]{3,1,2,0:T(8,128)}, ...), condition=%wide.region_39.51_spmd, body=%wide.region_37.50_spmd.sunk | while | flops 21603076 | bytes 2659607 | solution.py:306
  1361.8 7.0 gather_fusion.41
  1372.0 7.6 gather_fusion.11
  1384.9 29.6 %while.122 = (s32[]{:T(128)}, f32[2,22,6,64]{3,1,2,0:T(8,128)}, f32[2,176,6,64]{1,3,2,0:T(8,128)}, f32[2,176,6,64]{1,3,2,0:T(8,128)}, s32[2]{0:T(128)}, /*index=...) while((s32[]{:T(128)}, f32[2,22,6,64]{3,1,2,0:T(8,128)}, ...), condition=%wide.region_43.55_spmd, body=%wide.region_41.54_spmd.sunk | while | flops 15340076 | bytes 3140903 | solution.py:306
  1487.2 10.7 collective-permute-done.16
  1499.7 9.3 collective-permute-done.22
  1515.7 12.9 gather_fusion.44
  1535.2 24.1 gather_fusion.36
  1565.7 13.2 gather_fusion.38
  1583.4 13.1 gather_fusion.40
  1601.0 13.4 gather_fusion.42
  1625.8 13.7 reshape.3147
  1639.5 12.2 reshape.3148
  1661.0 13.0 gather_fusion.49
  1679.9 13.0 gather_fusion.54
  1704.4 13.2 gather_fusion.48
  1725.4 13.2 gather_fusion.53
  1750.3 13.1 gather_fusion.47
  1771.3 13.1 gather_fusion.52
  1794.3 13.2 gather_fusion.46
  1815.7 13.2 gather_fusion.51
  1837.5 24.1 gather_fusion.45
  1868.2 24.5 gather_fusion.50
  1908.7 9.4 reshape.3143
  1924.2 6.6 constant_dynamic-update-slice_fusion.23
  1935.0 8.6 constant_dynamic-update-slice_fusion.21
  1943.7 8.9 constant_dynamic-update-slice_fusion.20
  1952.5 80.2 %reshape.3149 = f32[7080960]{0:T(1024)} reshape(f32[4,1770240]{1,0:T(4,128)} %constant_dynamic-update-slice_fusion.20) | data formatting | bytes 56647680 | tf_op jit(solution)/shard_map/reshape | solution.py:362
  2032.7 454.3 %all-reduce.6 = bf16[7080960]{0:T(1024)(128)(2,1)} all-reduce(f32[7080960]{0:T(1024)} %reshape.3149), channel_id=2, replica_groups=mesh['row'=4,'seq'=8] {'row','seq'}, use_global_device_ids=true, to_apply=%region_52.64.clone | all-reduce | flops 7080960 | bytes 42485760
  2491.0 7.7 dynamic-update-slice
  2504.0 82.2 %all-reduce.5.cloned.1.call-done = bf16[1770240]{0:T(1024)(128)(2,1)} async-done(((bf16[1770240]{0:T(1024)(128)(2,1)}), bf16[1770240]{0:T(1024)(128)(2,1)}) %all-reduce.5.cloned.1.call-update) | async-done | bytes 3540496
  (1348 shorter events, 1248.5 us)
Async XLA Ops:
  7.2 2579.0 %all-reduce.5.cloned.1.call-start = ((), (), s32[]{:S(2)}) async-start(), calls=%async_computation | async-start | bytes 7081984
  9.3 66.7 %copy-start.92 = (s32[12]{0:T(128)}, s32[12]{0:T(128)S(1)}, u32[]{:S(2)}) copy-start(s32[12]{0:T(128)S(1)} %get-tuple-element.1336) | copy-start | bytes 148
  9.3 232.3 %copy-start.90 = (s32[12]{0:T(128)}, s32[12]{0:T(128)S(1)}, u32[]{:S(2)}) copy-start(s32[12]{0:T(128)S(1)} %get-tuple-element.1334) | copy-start | bytes 148
  9.3 233.6 %copy-start.91 = (s32[12]{0:T(128)}, s32[12]{0:T(128)S(1)}, u32[]{:S(2)}) copy-start(s32[12]{0:T(128)S(1)} %get-tuple-element.1333) | copy-start | bytes 148
  12.6 27.1 %copy-start.16 = (s32[132]{0:T(256)}, s32[132]{0:T(256)S(1)}, u32[]{:S(2)}) copy-start(s32[132]{0:T(256)S(1)} %reshape.3571) | copy-start | bytes 1588
  52.5 313.6 %collective-permute-start.12 = (bf16[2,1,11,768]{3,2,1,0:T(8,128)(2,1)}, bf16[2,1,11,768]{3,2,1,0:T(8,128)(2,1)}, u32[]{:S(2)}, u32[]{:S(2)}) collective-permute-start(bf16[2,1,11,768]{3,2,1,0:T(8,128)(2,1)} %constant_dynamic-update-slice_fusion.7), channel_id=1, source_target_pairs={{0,1},{1,0},{2,3},{3,2},{4,5},{5,4},{6,7},{7,6},{8,9},{9,8},{10,11... | collective-permute-start | bytes 101384 | tf_op jit(solution)/shard_map/ppermute | solution.py:18
  54.6 25.8 copy-start.14
  89.7 280.3 %collective-permute-start.9 = (bf16[2,1,22,768]{3,2,1,0:T(8,128)(2,1)}, bf16[2,1,22,768]{3,2,1,0:T(8,128)(2,1)}, u32[]{:S(2)}, u32[]{:S(2)}) collective-permute-start(bf16[2,1,22,768]{3,2,1,0:T(8,128)(2,1)} %constant_dynamic-update-slice_fusion.5), channel_id=1, source_target_pairs={{0,1},{1,0},{2,3},{3,2},{4,5},{5,4},{6,7},{7,6},{8,9},{9,8},{10,11... | collective-permute-start | bytes 202760 | tf_op jit(solution)/shard_map/ppermute | solution.py:18
  91.3 15.8 copy-start.13
  107.8 22.2 copy-start.117
  120.7 250.4 %collective-permute-start.6 = (bf16[2,1,32,768]{3,2,1,0:T(8,128)(2,1)}, bf16[2,1,32,768]{3,2,1,0:T(8,128)(2,1)}, u32[]{:S(2)}, u32[]{:S(2)}) collective-permute-start(bf16[2,1,32,768]{3,2,1,0:T(8,128)(2,1)} %constant_dynamic-update-slice_fusion.3), channel_id=1, source_target_pairs={{0,1},{1,0},{2,3},{3,2},{4,5},{5,4},{6,7},{7,6},{8,9},{9,8},{10,11... | collective-permute-start | bytes 294920 | tf_op jit(solution)/shard_map/ppermute | solution.py:18
  122.8 14.5 copy-start.12
  159.1 215.3 %collective-permute-start.3 = (bf16[2,1,64,768]{3,2,1,0:T(8,128)(2,1)}, bf16[2,1,64,768]{3,2,1,0:T(8,128)(2,1)}, u32[]{:S(2)}, u32[]{:S(2)}) collective-permute-start(bf16[2,1,64,768]{3,2,1,0:T(8,128)(2,1)} %constant_dynamic-update-slice_fusion.1), channel_id=1, source_target_pairs={{0,1},{1,0},{2,3},{3,2},{4,5},{5,4},{6,7},{7,6},{8,9},{9,8},{10,11... | collective-permute-start | bytes 589832 | tf_op jit(solution)/shard_map/ppermute | solution.py:18
  160.7 32.8 %copy-start.11 = (s32[1536]{0:T(1024)}, s32[1536]{0:T(1024)S(1)}, u32[]{:S(2)}) copy-start(s32[1536]{0:T(1024)S(1)} %reshape.3518) | copy-start | bytes 18436
  224.7 215.2 %collective-permute-start = (bf16[2,1,128,768]{2,3,1,0:T(8,128)(2,1)}, bf16[2,1,128,768]{2,3,1,0:T(8,128)(2,1)}, u32[]{:S(2)}, u32[]{:S(2)}) collective-permute-start(bf16[2,1,128,768]{2,3,1,0:T(8,128)(2,1)} %pad_maximum_fusion.8), channel_id=1, source_target_pairs={{0,1},{1,0},{2,3},{3,2},{4,5},{5,4},{6,7},{7,6},{8,9},{9,8},{10,11... | collective-permute-start | bytes 1179656 | tf_op jit(solution)/shard_map/ppermute | solution.py:18
  301.6 118.9 %copy-start.7 = (s32[1536]{0:T(1024)}, s32[1536]{0:T(1024)S(1)}, u32[]{:S(2)}) copy-start(s32[1536]{0:T(1024)S(1)} %reshape.3464) | copy-start | bytes 18436
  334.5 25.9 copy-start.139
  366.9 7.4 collective-permute-start.13
  371.0 5.4 collective-permute-start.10
  372.8 65.0 %collective-permute-start.7 = (bf16[2,2,32,768]{3,2,1,0:T(8,128)(2,1)}, bf16[2,2,32,768]{3,2,1,0:T(8,128)(2,1)}, u32[]{:S(2)}, u32[]{:S(2)}) collective-permute-start(bf16[2,2,32,768]{3,2,1,0:T(8,128)(2,1)} %pad_maximum_fusion.16), channel_id=1, source_target_pairs={{0,2},{1,3},{2,0},{3,1},{4,6},{5,7},{6,4},{7,5},{8,10},{9,11},{10,... | collective-permute-start | bytes 589832 | tf_op jit(solution)/shard_map/ppermute | solution.py:18
  374.3 9.4 collective-permute-start.14
  376.4 136.7 %collective-permute-start.4 = (bf16[2,2,64,768]{3,2,1,0:T(8,128)(2,1)}, bf16[2,2,64,768]{3,2,1,0:T(8,128)(2,1)}, u32[]{:S(2)}, u32[]{:S(2)}) collective-permute-start(bf16[2,2,64,768]{3,2,1,0:T(8,128)(2,1)} %pad_maximum_fusion.9), channel_id=1, source_target_pairs={{0,2},{1,3},{2,0},{3,1},{4,6},{5,7},{6,4},{7,5},{8,10},{9,11},{10,... | collective-permute-start | bytes 1179656 | tf_op jit(solution)/shard_map/ppermute | solution.py:18
  377.9 67.4 %collective-permute-start.11 = (bf16[2,4,22,768]{3,2,1,0:T(8,128)(2,1)}, bf16[2,4,22,768]{3,2,1,0:T(8,128)(2,1)}, u32[]{:S(2)}, u32[]{:S(2)}) collective-permute-start(bf16[2,4,22,768]{3,2,1,0:T(8,128)(2,1)} %pad_maximum_fusion.12), channel_id=1, source_target_pairs={{0,4},{1,5},{2,6},{3,7},{4,0},{5,1},{6,2},{7,3},{8,12},{9,13},{10,... | collective-permute-start | bytes 811016 | tf_op jit(solution)/shard_map/ppermute | solution.py:18
  439.9 75.6 %collective-permute-start.8 = (bf16[2,4,32,768]{3,2,1,0:T(8,128)(2,1)}, bf16[2,4,32,768]{3,2,1,0:T(8,128)(2,1)}, u32[]{:S(2)}, u32[]{:S(2)}) collective-permute-start(bf16[2,4,32,768]{3,2,1,0:T(8,128)(2,1)} %pad_maximum_fusion.10), channel_id=1, source_target_pairs={{0,4},{1,5},{2,6},{3,7},{4,0},{5,1},{6,2},{7,3},{8,12},{9,13},{10,... | collective-permute-start | bytes 1179656 | tf_op jit(solution)/shard_map/ppermute | solution.py:18
  442.2 146.9 %collective-permute-start.1 = (bf16[2,2,128,768]{2,3,1,0:T(8,128)(2,1)}, bf16[2,2,128,768]{2,3,1,0:T(8,128)(2,1)}, u32[]{:S(2)}, u32[]{:S(2)}) collective-permute-start(bf16[2,2,128,768]{2,3,1,0:T(8,128)(2,1)} %pad_maximum_fusion.4), channel_id=1, source_target_pairs={{0,2},{1,3},{2,0},{3,1},{4,6},{5,7},{6,4},{7,5},{8,10},{9,11},{10,... | collective-permute-start | bytes 2359304 | tf_op jit(solution)/shard_map/ppermute | solution.py:18
  472.4 17.1 copy-start.1
  515.4 79.1 %collective-permute-start.5 = (bf16[2,4,64,768]{3,2,1,0:T(8,128)(2,1)}, bf16[2,4,64,768]{3,2,1,0:T(8,128)(2,1)}, u32[]{:S(2)}, u32[]{:S(2)}) collective-permute-start(bf16[2,4,64,768]{3,2,1,0:T(8,128)(2,1)} %pad_maximum_fusion.5), channel_id=1, source_target_pairs={{0,4},{1,5},{2,6},{3,7},{4,0},{5,1},{6,2},{7,3},{8,12},{9,13},{10,... | collective-permute-start | bytes 2359304 | tf_op jit(solution)/shard_map/ppermute | solution.py:18
  548.4 17.1 copy-start.3
  592.2 99.8 %collective-permute-start.2 = (bf16[2,4,128,768]{2,3,1,0:T(8,128)(2,1)}, bf16[2,4,128,768]{2,3,1,0:T(8,128)(2,1)}, u32[]{:S(2)}, u32[]{:S(2)}) collective-permute-start(bf16[2,4,128,768]{2,3,1,0:T(8,128)(2,1)} %pad_maximum_fusion.2), channel_id=1, source_target_pairs={{0,4},{1,5},{2,6},{3,7},{4,0},{5,1},{6,2},{7,3},{8,12},{9,13},{10,... | collective-permute-start | bytes 4718600 | tf_op jit(solution)/shard_map/ppermute | solution.py:18
  882.5 12.7 copy-start.18
  1143.8 332.9 %collective-permute-start.15 = (bf16[2,4,128,768]{2,3,1,0:T(8,128)(2,1)}, bf16[2,4,128,768]{2,3,1,0:T(8,128)(2,1)}, u32[]{:S(2)}, u32[]{:S(2)}) collective-permute-start(bf16[2,4,128,768]{2,3,1,0:T(8,128)(2,1)} %select_convert_fusion), channel_id=1, source_target_pairs={{0,4},{1,5},{2,6},{3,7},{4,0},{5,1},{6,2},{7,3},{8,12},{9,13},{10,... | collective-permute-start | bytes 4718600 | tf_op jit(solution)/shard_map/ppermute | solution.py:18
  1281.3 204.0 %collective-permute-start.21 = (bf16[2,4,64,768]{3,2,1,0:T(8,128)(2,1)}, bf16[2,4,64,768]{3,2,1,0:T(8,128)(2,1)}, u32[]{:S(2)}, u32[]{:S(2)}) collective-permute-start(bf16[2,4,64,768]{3,2,1,0:T(8,128)(2,1)} %select_convert_fusion.1), channel_id=1, source_target_pairs={{0,4},{1,5},{2,6},{3,7},{4,0},{5,1},{6,2},{7,3},{8,12},{9,13},{10,... | collective-permute-start | bytes 2359304 | tf_op jit(solution)/shard_map/ppermute | solution.py:18
  1357.4 12.9 copy-start.124
  1361.7 101.5 %collective-permute-start.27 = (bf16[2,4,32,768]{3,2,1,0:T(8,128)(2,1)}, bf16[2,4,32,768]{3,2,1,0:T(8,128)(2,1)}, u32[]{:S(2)}, u32[]{:S(2)}) collective-permute-start(bf16[2,4,32,768]{3,2,1,0:T(8,128)(2,1)} %select_convert_fusion.3), channel_id=1, source_target_pairs={{0,4},{1,5},{2,6},{3,7},{4,0},{5,1},{6,2},{7,3},{8,12},{9,13},{10,... | collective-permute-start | bytes 1179656 | tf_op jit(solution)/shard_map/ppermute | solution.py:18
  1372.0 12.9 copy-start.2
  1435.1 10.7 collective-permute-start.39
  1446.9 29.8 %slice-start = ((s8[6291456]{0:T(1024)(128)(4,1)}), s8[4194304]{0:T(1024)(128)(4,1)S(1)}, s32[]{:S(2)}) async-start(s8[6291456]{0:T(1024)(128)(4,1)} %bitcast.701), calls=%async_computation.1 | async-start | bytes 8388608
  1447.0 3.5 collective-permute-start.40
  1447.2 14.2 collective-permute-start.33
  1450.6 10.7 collective-permute-start.41
  1456.2 20.5 slice-start.1
  1461.2 21.0 collective-permute-start.42
  1461.5 4.2 collective-permute-start.34
  1465.7 5.0 collective-permute-start.35
  1468.9 7.1 collective-permute-start.28
  1470.7 12.2 collective-permute-start.36
  1476.1 7.6 collective-permute-start.29
  1478.8 19.1 collective-permute-start.16
  1482.2 169.5 %collective-permute-start.43 = (bf16[2,1,11,768]{3,2,1,0:T(8,128)(2,1)}, bf16[2,1,11,768]{3,2,1,0:T(8,128)(2,1)}, u32[]{:S(2)}, u32[]{:S(2)}) collective-permute-start(bf16[2,1,11,768]{3,2,1,0:T(8,128)(2,1)} %collective-permute-done.42), channel_id=1, source_target_pairs={{0,2},{1,3},{2,0},{3,1},{4,6},{5,7},{6,4},{7,5},{8,10},{9,11},{10,... | collective-permute-start | bytes 101384 | tf_op jit(solution)/shard_map/ppermute | solution.py:18
  1483.0 171.0 %collective-permute-start.37 = (bf16[2,1,22,768]{3,2,1,0:T(8,128)(2,1)}, bf16[2,1,22,768]{3,2,1,0:T(8,128)(2,1)}, u32[]{:S(2)}, u32[]{:S(2)}) collective-permute-start(bf16[2,1,22,768]{3,2,1,0:T(8,128)(2,1)} %collective-permute-done.36), channel_id=1, source_target_pairs={{0,2},{1,3},{2,0},{3,1},{4,6},{5,7},{6,4},{7,5},{8,10},{9,11},{10,... | collective-permute-start | bytes 202760 | tf_op jit(solution)/shard_map/ppermute | solution.py:18
  1484.3 169.7 %collective-permute-start.30 = (bf16[2,1,32,768]{3,2,1,0:T(8,128)(2,1)}, bf16[2,1,32,768]{3,2,1,0:T(8,128)(2,1)}, u32[]{:S(2)}, u32[]{:S(2)}) collective-permute-start(bf16[2,1,32,768]{3,2,1,0:T(8,128)(2,1)} %add_convert_fusion.5), channel_id=1, source_target_pairs={{0,1},{1,0},{2,3},{3,2},{4,5},{5,4},{6,7},{7,6},{8,9},{9,8},{10,11... | collective-permute-start | bytes 294920 | tf_op jit(solution)/shard_map/ppermute | solution.py:18
  1486.7 22.3 collective-permute-start.22
  1498.3 12.6 collective-permute-start.17
  1509.9 145.6 %collective-permute-start.23 = (bf16[2,1,64,768]{3,2,1,0:T(8,128)(2,1)}, bf16[2,1,64,768]{3,2,1,0:T(8,128)(2,1)}, u32[]{:S(2)}, u32[]{:S(2)}) collective-permute-start(bf16[2,1,64,768]{3,2,1,0:T(8,128)(2,1)} %select_convert_fusion.9), channel_id=1, source_target_pairs={{0,1},{1,0},{2,3},{3,2},{4,5},{5,4},{6,7},{7,6},{8,9},{9,8},{10,11... | collective-permute-start | bytes 589832 | tf_op jit(solution)/shard_map/ppermute | solution.py:18
  1511.7 147.1 %collective-permute-start.18 = (bf16[2,1,128,768]{2,3,1,0:T(8,128)(2,1)}, bf16[2,1,128,768]{2,3,1,0:T(8,128)(2,1)}, u32[]{:S(2)}, u32[]{:S(2)}) collective-permute-start(bf16[2,1,128,768]{2,3,1,0:T(8,128)(2,1)} %add_convert_fusion.1), channel_id=1, source_target_pairs={{0,1},{1,0},{2,3},{3,2},{4,5},{5,4},{6,7},{7,6},{8,9},{9,8},{10,11... | collective-permute-start | bytes 1179656 | tf_op jit(solution)/shard_map/ppermute | solution.py:18
  1651.7 7.1 collective-permute-start.44
  1653.9 45.7 %collective-permute-start.38 = (bf16[2,1,22,768]{3,2,1,0:T(8,128)(2,1)}, bf16[2,1,22,768]{3,2,1,0:T(8,128)(2,1)}, u32[]{:S(2)}, u32[]{:S(2)}) collective-permute-start(bf16[2,1,22,768]{3,2,1,0:T(8,128)(2,1)} %collective-permute-done.37), channel_id=1, source_target_pairs={{0,4},{1,5},{2,6},{3,7},{4,0},{5,1},{6,2},{7,3},{8,12},{9,13},{10,... | collective-permute-start | bytes 202760 | tf_op jit(solution)/shard_map/ppermute | solution.py:18
  1654.0 43.3 %collective-permute-start.31 = (bf16[2,1,32,768]{3,2,1,0:T(8,128)(2,1)}, bf16[2,1,32,768]{3,2,1,0:T(8,128)(2,1)}, u32[]{:S(2)}, u32[]{:S(2)}) collective-permute-start(bf16[2,1,32,768]{3,2,1,0:T(8,128)(2,1)} %collective-permute-done.30), channel_id=1, source_target_pairs={{0,2},{1,3},{2,0},{3,1},{4,6},{5,7},{6,4},{7,5},{8,10},{9,11},{10,... | collective-permute-start | bytes 294920 | tf_op jit(solution)/shard_map/ppermute | solution.py:18
  1657.4 42.2 %collective-permute-start.24 = (bf16[2,1,64,768]{3,2,1,0:T(8,128)(2,1)}, bf16[2,1,64,768]{3,2,1,0:T(8,128)(2,1)}, u32[]{:S(2)}, u32[]{:S(2)}) collective-permute-start(bf16[2,1,64,768]{3,2,1,0:T(8,128)(2,1)} %add_convert_fusion.3), channel_id=1, source_target_pairs={{0,1},{1,0},{2,3},{3,2},{4,5},{5,4},{6,7},{7,6},{8,9},{9,8},{10,11... | collective-permute-start | bytes 589832 | tf_op jit(solution)/shard_map/ppermute | solution.py:18
  1658.8 85.8 %collective-permute-start.19 = (bf16[2,1,128,768]{2,3,1,0:T(8,128)(2,1)}, bf16[2,1,128,768]{2,3,1,0:T(8,128)(2,1)}, u32[]{:S(2)}, u32[]{:S(2)}) collective-permute-start(bf16[2,1,128,768]{2,3,1,0:T(8,128)(2,1)} %collective-permute-done.18), channel_id=1, source_target_pairs={{0,2},{1,3},{2,0},{3,1},{4,6},{5,7},{6,4},{7,5},{8,10},{9,11},{10,... | collective-permute-start | bytes 1179656 | tf_op jit(solution)/shard_map/ppermute | solution.py:18
  1697.4 48.0 %collective-permute-start.32 = (bf16[2,1,32,768]{3,2,1,0:T(8,128)(2,1)}, bf16[2,1,32,768]{3,2,1,0:T(8,128)(2,1)}, u32[]{:S(2)}, u32[]{:S(2)}) collective-permute-start(bf16[2,1,32,768]{3,2,1,0:T(8,128)(2,1)} %collective-permute-done.31), channel_id=1, source_target_pairs={{0,4},{1,5},{2,6},{3,7},{4,0},{5,1},{6,2},{7,3},{8,12},{9,13},{10,... | collective-permute-start | bytes 294920 | tf_op jit(solution)/shard_map/ppermute | solution.py:18
  1699.7 43.4 %collective-permute-start.25 = (bf16[2,1,64,768]{3,2,1,0:T(8,128)(2,1)}, bf16[2,1,64,768]{3,2,1,0:T(8,128)(2,1)}, u32[]{:S(2)}, u32[]{:S(2)}) collective-permute-start(bf16[2,1,64,768]{3,2,1,0:T(8,128)(2,1)} %collective-permute-done.24), channel_id=1, source_target_pairs={{0,2},{1,3},{2,0},{3,1},{4,6},{5,7},{6,4},{7,5},{8,10},{9,11},{10,... | collective-permute-start | bytes 589832 | tf_op jit(solution)/shard_map/ppermute | solution.py:18
  1743.1 45.8 %collective-permute-start.26 = (bf16[2,1,64,768]{3,2,1,0:T(8,128)(2,1)}, bf16[2,1,64,768]{3,2,1,0:T(8,128)(2,1)}, u32[]{:S(2)}, u32[]{:S(2)}) collective-permute-start(bf16[2,1,64,768]{3,2,1,0:T(8,128)(2,1)} %collective-permute-done.25), channel_id=1, source_target_pairs={{0,4},{1,5},{2,6},{3,7},{4,0},{5,1},{6,2},{7,3},{8,12},{9,13},{10,... | collective-permute-start | bytes 589832 | tf_op jit(solution)/shard_map/ppermute | solution.py:18
  1744.6 88.8 %collective-permute-start.20 = (bf16[2,1,128,768]{2,3,1,0:T(8,128)(2,1)}, bf16[2,1,128,768]{2,3,1,0:T(8,128)(2,1)}, u32[]{:S(2)}, u32[]{:S(2)}) collective-permute-start(bf16[2,1,128,768]{2,3,1,0:T(8,128)(2,1)} %collective-permute-done.19), channel_id=1, source_target_pairs={{0,4},{1,5},{2,6},{3,7},{4,0},{5,1},{6,2},{7,3},{8,12},{9,13},{10,... | collective-permute-start | bytes 1179656 | tf_op jit(solution)/shard_map/ppermute | solution.py:18
  (154 other events, 574.5 us)
Sparse Core Ops, SparseCore 0:
  2498.8 87.3 all-reduce.4
where the time goes:
time: 2650 us; the launch traced here: 2610 us
  local copies, waits for them, and re-layouts  1430 us (54%)
  blocking collectives  463 us (17%)
  matrix products  319 us (12%)
  other arithmetic  155 us (6%)
  waiting for transfers between devices  115 us (4%)
  loops' own time  62.2 us (2%)
  starting transfers between devices  49.6 us (2%)
    gather x106, local copies, waits for them, and re-layouts, take_slots(): return jnp.take_along_axis(array, index_table[:, :, None], axis=0)  596 us
    unnamed x1, blocking collectives  454 us
    gather x29, local copies, waits for them, and re-layouts, shards(): jnp.take_along_axis(lse_slots, token_slot, axis=0)  121 us
    unnamed x2, waiting for transfers between devices  82.3 us
    reshape x1, local copies, waits for them, and re-layouts, shards(): padded = flat_grads.reshape(-1)  80.2 us
    dot_general x47, matrix products, block_scores(): jnp.einsum('qhe,khe->hqk', query_part, key_part, preferred_element_type=j...  65.4 us
    unnamed x323, local copies, waits for them, and re-layouts  59.1 us
  transfers between devices with their start and end apart: 46, of which 7 were waited for; matrix products, arithmetic and copies ran while one was open for 47% of the time, Pallas kernels for 0%

commit v1 on v0

v1 whole, which is shorter than its diff:
```python
import functools

import jax
import jax.numpy as jnp
from jax import lax
from jax.experimental import pallas as pl
from jax.experimental.pallas import tpu as pltpu
from jax.sharding import PartitionSpec as P

reaches = (2048, 4096, 8192, 16384, 32768)
dilations = (1, 2, 4, 6, 12)
period = 12
doc_count = 4
epsilon = 1e-05
negative = -1e30
bf16 = jnp.bfloat16
f32 = jnp.float32


def layer_norm(values, gain_vec, shift_vec):
    centered = values - jnp.mean(values, axis=-1, keepdims=True)
    variance = jnp.mean(centered * centered, axis=-1, keepdims=True)
    return centered * lax.rsqrt(variance + epsilon) * gain_vec + shift_vec


def gelu_exact(values):
    return jax.nn.gelu(values, approximate=False)


def matmul(left, right):
    return jnp.dot(left, right, preferred_element_type=f32)


def matmul_t(left, right):
    return lax.dot_general(left, right, (((1,), (1,)), ((), ())), preferred_element_type=f32)


def token_sum(left, right):
    return lax.dot_general(left, right, (((0,), (0,)), ((), ())), preferred_element_type=f32)


def split3(values):
    first = lax.reduce_precision(values, 8, 7)
    rest = values - first
    second = lax.reduce_precision(rest, 8, 7)
    return first.astype(bf16), second.astype(bf16), (rest - second).astype(bf16)


def swap_seq(value, mask):
    count = lax.axis_size("seq")
    return lax.ppermute(value, "seq", [(s, s ^ mask) for s in range(count)])


def swap_row(value, even_mask, odd_mask):
    rows = lax.axis_size("row")
    count = lax.axis_size("seq")
    pairs = []
    for r in range(rows):
        for s in range(count):
            partner = r ^ (odd_mask if s % 2 else even_mask)
            pairs.append((r * count + s, partner * count + s))
    return lax.ppermute(value, ("row", "seq"), pairs)


def direct(count):
    return count <= 8


def gather_blocks(block):
    count = lax.axis_size("seq")
    if direct(count):
        parts = [block]
        for apart in range(1, count // 2):
            parts.append(swap_seq(block, 2 * apart))
        mine = jnp.stack(parts)
        other = swap_seq(mine, 1)
        return jnp.stack([mine, other], axis=1).reshape((count,) + block.shape)
    return lax.all_gather(block, "seq", axis=0)


def sum_chips(block):
    count = lax.axis_size("seq")
    chips = count // 2
    if not direct(count):
        groups = [list(range(0, count, 2)), list(range(1, count, 2))]
        return lax.psum(block.astype(f32), "seq", axis_index_groups=groups).astype(bf16)
    chip = lax.axis_index("seq") // 2
    height = block.shape[0] // chips
    total = lax.dynamic_slice_in_dim(block, chip * height, height, 0).astype(f32)
    for apart in range(1, chips):
        piece = lax.dynamic_slice_in_dim(block, (chip ^ apart) * height, height, 0)
        total = total + swap_seq(piece, 2 * apart).astype(f32)
    total = total.astype(bf16)
    parts = [total]
    for apart in range(1, chips):
        parts.append(swap_seq(total, 2 * apart))
    result = jnp.zeros_like(block)
    for apart in range(chips):
        result = lax.dynamic_update_slice_in_dim(result, parts[apart], (chip ^ apart) * height, 0)
    return result


def sum_rows(piece_of):
    rows = lax.axis_size("row")
    r = lax.axis_index("row")
    core = lax.axis_index("seq") % 2
    first = jnp.where(core == 0, 1, 2)
    second = jnp.where(core == 0, 2, 1)
    sent = jnp.concatenate([piece_of(r ^ first), piece_of(r ^ first ^ second)], axis=0)
    got = swap_row(sent.astype(bf16), 1, 2)
    height = got.shape[0] // 2
    onward = piece_of(r ^ second) + got[height:].astype(f32)
    got_two = swap_row(onward.astype(bf16), 2, 1)
    return (piece_of(r) + got[:height].astype(f32) + got_two.astype(f32)).astype(bf16)


def fold_pair(ref_value, head_bit, lanes):
    return jnp.where((lanes >= 64) == (head_bit == 1), ref_value, jnp.zeros_like(ref_value))


def forward_kernel(
    place_ref, q_ref, k_ref, v_ref, own_ref, all_ref, out_ref, lse_ref, bias_ref, *, tokens, chunk
):
    pairs = q_ref.shape[1] // 128
    length = k_ref.shape[0]
    chunks = length // chunk
    step = pl.program_id(0)
    me = place_ref[0]
    flip = place_ref[1]
    lanes = lax.broadcasted_iota(jnp.int32, (tokens, 128), 1)

    @pl.when(step == 0)
    def _():
        lse_ref[...] = jnp.zeros_like(lse_ref)
        row = lax.broadcasted_iota(jnp.int32, (tokens, tokens), 0)
        col = lax.broadcasted_iota(jnp.int32, (tokens, tokens), 1)
        for c in range(length // tokens):
            block = c ^ flip
            allowed = (block < me) | ((block == me) & (col <= row))
            bias_ref[:, c * tokens : (c + 1) * tokens] = jnp.where(allowed, 0.0, negative)

    def scores(left, pair, begin):
        right = jnp.concatenate(
            [k_ref[pl.ds(begin, chunk), pair * 128 : pair * 128 + 128], all_ref[pl.ds(begin, chunk), :]],
            axis=1,
        )
        return matmul_t(left, right)

    for pair in range(pairs):
        span = slice(pair * 128, pair * 128 + 128)
        q_pair = q_ref[:, span]
        outs = []
        for bit in range(2):
            left = jnp.concatenate([fold_pair(q_pair, bit, lanes), own_ref[pair * 2 + bit]], axis=1)

            def one(c, carry, left=left):
                top, total, acc = carry
                begin = c * chunk if isinstance(c, int) else pl.multiple_of(c * chunk, chunk)
                s = scores(left, pair, begin) + bias_ref[:, pl.ds(begin, chunk)]
                new_top = jnp.max(s, axis=1, keepdims=True)
                if top is not None:
                    new_top = jnp.maximum(top, new_top)
                p = jnp.exp(s - new_top)
                new_total = jnp.sum(p, axis=1, keepdims=True)
                new_acc = matmul(p.astype(bf16), v_ref[pl.ds(begin, chunk), span])
                if top is not None:
                    scale = jnp.exp(top - new_top)
                    new_total = new_total + scale * total
                    new_acc = new_acc + scale * acc
                return new_top, new_total, new_acc

            if chunks == 1:
                top, total, acc = one(0, (None, None, None))
            else:
                start = (
                    jnp.full((tokens, 1), 4 * negative, f32),
                    jnp.zeros((tokens, 1), f32),
                    jnp.zeros((tokens, 128), f32),
                )
                top, total, acc = lax.fori_loop(0, chunks, one, start)
            outs.append(acc / total)
            head = step * pairs * 2 + pair * 2 + bit
            lse_ref[...] = jnp.where(lanes == head, top + jnp.log(total), lse_ref[...])
        out_ref[:, span] = jnp.where(lanes < 64, outs[0], outs[1])


def backward_kernel(
    place_ref,
    q_own,
    k_own,
    v_own,
    d_own,
    q_all,
    k_all,
    v_all,
    d_all,
    own_q,
    own_d,
    own_k,
    own_v,
    feat_q,
    feat_k,
    dq_ref,
    dk_ref,
    dv_ref,
    left_a,
    left_b,
    left_c,
    left_d,
    acc_q,
    acc_k,
    acc_v,
    *,
    tokens,
):
    pairs = q_own.shape[1] // 128
    blocks = q_all.shape[0] // tokens
    me = place_ref[0]
    flip = place_ref[1]
    lanes = lax.broadcasted_iota(jnp.int32, (tokens, 128), 1)
    low = lanes < 64
    for pair in range(pairs):
        span = slice(pair * 128, pair * 128 + 128)
        for bit in range(2):
            rows = slice(bit * tokens, (bit + 1) * tokens)
            head = pair * 2 + bit
            left_a[pair, rows, :] = jnp.concatenate(
                [fold_pair(q_own[:, span], bit, lanes), own_q[head]], axis=1
            )
            left_b[pair, rows, :] = jnp.concatenate(
                [fold_pair(d_own[:, span], bit, lanes), own_d[head]], axis=1
            )
            left_c[pair, rows, :] = jnp.concatenate(
                [fold_pair(k_own[:, span], bit, lanes), own_k[head]], axis=1
            )
            left_d[pair, rows, :] = jnp.concatenate(
                [
                    fold_pair(v_own[:, span], bit, lanes),
                    jnp.broadcast_to(own_v[head], (tokens, own_v.shape[2])),
                ],
                axis=1,
            )
    acc_q[...] = jnp.zeros_like(acc_q)
    acc_k[...] = jnp.zeros_like(acc_k)
    acc_v[...] = jnp.zeros_like(acc_v)
    row = lax.broadcasted_iota(jnp.int32, (2 * tokens, tokens), 0) % tokens
    col = lax.broadcasted_iota(jnp.int32, (2 * tokens, tokens), 1)
    later_col = jnp.where(col <= row, 0.0, negative)
    later_row = jnp.where(row <= col, 0.0, negative)

    def select(both):
        return jnp.where(low, both[:tokens], both[tokens:])

    def query_step(j, _):
        begin = pl.multiple_of((j ^ flip) * tokens, tokens)
        at_diag = (j == me).astype(f32)
        feats = feat_k[pl.ds(begin, tokens), :]
        for pair in range(pairs):
            span = slice(pair * 128, pair * 128 + 128)
            k_blk = k_all[pl.ds(begin, tokens), span]
            v_blk = v_all[pl.ds(begin, tokens), span]
            s = matmul_t(left_a[pair], jnp.concatenate([k_blk, feats], axis=1))
            dp = matmul_t(left_b[pair], jnp.concatenate([v_blk, feats], axis=1))
            w = jnp.exp(s + later_col * at_diag)
            ds = (w * dp).astype(bf16)
            acc_q[:, span] += select(matmul(ds, k_blk))
        return 0

    def key_step(j, _):
        begin = pl.multiple_of((j ^ flip) * tokens, tokens)
        at_diag = (j == me).astype(f32)
        feats = feat_q[pl.ds(begin, tokens), :]
        for pair in range(pairs):
            span = slice(pair * 128, pair * 128 + 128)
            q_blk = q_all[pl.ds(begin, tokens), span]
            d_blk = d_all[pl.ds(begin, tokens), span]
            s = matmul_t(left_c[pair], jnp.concatenate([q_blk, feats], axis=1))
            dp = matmul_t(left_d[pair], jnp.concatenate([d_blk, feats], axis=1))
            w = jnp.exp(s + later_row * at_diag)
            ds = (w * dp).astype(bf16)
            acc_k[:, span] += select(matmul(ds, q_blk))
            acc_v[:, span] += select(matmul(w.astype(bf16), d_blk))
        return 0

    lax.fori_loop(0, me + 1, query_step, 0)
    lax.fori_loop(me, blocks, key_step, 0)
    dq_ref[...] = (acc_q[...] * 0.125).astype(bf16)
    dk_ref[...] = acc_k[...].astype(bf16)
    dv_ref[...] = acc_v[...].astype(bf16)


def attend(place, q, k_all, v_all, own, feats, group):
    tokens, width = q.shape
    length = k_all.shape[0]
    chunk = min(length, 1024)
    lanes = 128 * group
    steps = width // lanes
    feat = feats.shape[1]
    spec = pltpu.PrefetchScalarGridSpec(
        num_scalar_prefetch=1,
        grid=(steps,),
        in_specs=[
            pl.BlockSpec((tokens, lanes), lambda i, _: (0, i)),
            pl.BlockSpec((length, lanes), lambda i, _: (0, i)),
            pl.BlockSpec((length, lanes), lambda i, _: (0, i)),
            pl.BlockSpec((2 * group, tokens, feat), lambda i, _: (i, 0, 0)),
            pl.BlockSpec((length, feat), lambda i, _: (0, 0)),
        ],
        out_specs=[
            pl.BlockSpec((tokens, lanes), lambda i, _: (0, i)),
            pl.BlockSpec((tokens, 128), lambda i, _: (0, 0)),
        ],
        scratch_shapes=[pltpu.VMEM((tokens, length), f32)],
    )
    return pl.pallas_call(
        functools.partial(forward_kernel, tokens=tokens, chunk=chunk),
        grid_spec=spec,
        out_shape=[
            jax.ShapeDtypeStruct((tokens, width), f32),
            jax.ShapeDtypeStruct((tokens, 128), f32),
        ],
        name="attend",
    )(place, q, k_all, v_all, own, feats)


def attend_back(place, owns, alls, own_feats, feats, group):
    tokens, width = owns[0].shape
    length = alls[0].shape[0]
    lanes = 128 * group
    steps = width // lanes
    feat = feats[0].shape[1]
    full = 128 + feat
    own_spec = pl.BlockSpec((tokens, lanes), lambda i, _: (0, i))
    all_spec = pl.BlockSpec((length, lanes), lambda i, _: (0, i))
    head_spec = pl.BlockSpec((2 * group, tokens, feat), lambda i, _: (i, 0, 0))
    flat_spec = pl.BlockSpec((2 * group, 1, feat), lambda i, _: (i, 0, 0))
    feat_spec = pl.BlockSpec((length, feat), lambda i, _: (0, 0))
    spec = pltpu.PrefetchScalarGridSpec(
        num_scalar_prefetch=1,
        grid=(steps,),
        in_specs=[own_spec] * 4
        + [all_spec] * 4
        + [head_spec, head_spec, head_spec, flat_spec, feat_spec, feat_spec],
        out_specs=[own_spec] * 3,
        scratch_shapes=[pltpu.VMEM((group, 2 * tokens, full), bf16)] * 4
        + [pltpu.VMEM((tokens, lanes), f32)] * 3,
    )
    return pl.pallas_call(
        functools.partial(backward_kernel, tokens=tokens),
        grid_spec=spec,
        out_shape=[jax.ShapeDtypeStruct((tokens, width), bf16)] * 3,
        name="attend_back",
    )(place, *owns, *alls, *own_feats, *feats)


def log_counts(offsets, positions, row_len, spans, parts):
    heads = offsets.shape[1]
    finest = spans[0]
    classes = jnp.arange(period, dtype=jnp.int32)
    part_start = jnp.arange(parts, dtype=jnp.int32) * finest
    total = jnp.zeros((heads, positions.shape[0], parts, period), f32)
    for index, dilation in enumerate(dilations):
        offset = offsets[index][:, None]
        own_in = jnp.mod(positions[None, :] - offset, dilation) == 0
        key_in = jnp.mod(classes[None, :] - offset, dilation) == 0
        same = positions[:, None] // spans[index] == part_start[None, :] // spans[index]
        both = own_in[:, :, None, None] & key_in[:, None, None, :] & same[None, :, :, None]
        total = total + both.astype(f32)
    logs = jnp.where(total > 0, jnp.log(jnp.maximum(total, 1.0)), negative)
    logs = logs.reshape(heads, positions.shape[0], parts * period)
    high = lax.reduce_precision(logs, 8, 7)
    return high.astype(bf16), (logs - high).astype(bf16)


def shards(
    inputs,
    documents,
    offsets,
    ln1_gain,
    ln1_bias,
    qkv_weight,
    out_weight,
    ln2_gain,
    ln2_bias,
    up_weight,
    down_weight,
    cotangent,
):
    tokens = inputs.shape[1]
    width = inputs.shape[2]
    heads = offsets.shape[1]
    hidden_width = up_weight.shape[1]
    rows = lax.axis_size("row")
    share = width // rows
    count = lax.axis_size("seq")
    me = lax.axis_index("seq")
    core = me % 2
    row_len = tokens * count
    flip = me if direct(count) else jnp.zeros_like(me)
    place = jnp.stack([me, flip]).astype(jnp.int32)
    spans = [min(reach, row_len) for reach in reaches]
    parts = row_len // spans[0]
    group = width // 128 if row_len <= 1024 else 1

    x_low = inputs[0]
    doc_rows = jnp.zeros((16, width), bf16).at[0, :tokens].set(documents[0].astype(bf16))
    gathered = gather_blocks(jnp.concatenate([x_low, doc_rows], axis=0))
    x_all = gathered[:, :tokens].reshape(row_len, width)
    docs_all = gathered[:, tokens, :tokens].reshape(row_len).astype(jnp.int32)
    block_of = jnp.arange(count, dtype=jnp.int32) ^ flip
    pos_all = (block_of[:, None] * tokens + jnp.arange(tokens, dtype=jnp.int32)[None, :]).reshape(-1)
    pos_own = me * tokens + jnp.arange(tokens, dtype=jnp.int32)
    docs_own = documents[0]

    key_class = (pos_all // spans[0]) * period + pos_all % period
    class_hot = (key_class[:, None] == jnp.arange(parts * period)[None, :]).astype(bf16)
    doc_hot = (docs_all[:, None] == jnp.arange(doc_count)[None, :]).astype(bf16)
    ones_at = 2 * parts * period + doc_count
    lse_at = ones_at + 3
    delta_at = lse_at + 3 * heads
    used = delta_at + 3 * heads
    feat = -(-used // 128) * 128
    feat_base = jnp.concatenate(
        [
            class_hot,
            class_hot,
            doc_hot,
            jnp.ones((row_len, 3), bf16),
            jnp.zeros((row_len, feat - lse_at), bf16),
        ],
        axis=1,
    )
    high, low = log_counts(offsets, pos_own, row_len, spans, parts)
    doc_part = jnp.where(docs_own[:, None] == jnp.arange(doc_count)[None, :], 0.0, negative).astype(bf16)
    doc_part = jnp.broadcast_to(doc_part[None], (heads, tokens, doc_count))
    own_base = jnp.concatenate(
        [high, low, doc_part, jnp.zeros((heads, tokens, feat - ones_at), bf16)], axis=2
    )

    x_own = x_low.astype(f32)
    normed_one, norm_one_back = jax.vjp(layer_norm, x_own, ln1_gain, ln1_bias)
    normed_all = layer_norm(x_all.astype(f32), ln1_gain, ln1_bias).astype(bf16)
    q_all = (matmul(normed_all, qkv_weight[:, :width]) ).astype(bf16) * jnp.asarray(0.125, bf16)
    k_all = matmul(normed_all, qkv_weight[:, width : 2 * width]).astype(bf16)
    v_all = matmul(normed_all, qkv_weight[:, 2 * width :]).astype(bf16)
    own_at = (me ^ flip) * tokens

    def own_rows(value):
        if direct(count):
            return value[:tokens]
        return lax.dynamic_slice_in_dim(value, own_at, tokens, 0)

    q_own, k_own, v_own = own_rows(q_all), own_rows(k_all), own_rows(v_all)
    mixed, lse = attend(place, q_own, k_all, v_all, own_base, feat_base, group)
    lse = lse[:, :heads]

    attended = mixed.astype(bf16)
    middle = x_own + matmul(attended, out_weight)
    normed_two, norm_two_back = jax.vjp(layer_norm, middle, ln2_gain, ln2_bias)
    normed_two_low = normed_two.astype(bf16)
    hidden_pre = matmul(normed_two_low, up_weight)
    hidden, gelu_back = jax.vjp(gelu_exact, hidden_pre)
    hidden_low = hidden.astype(bf16)
    result = middle + matmul(hidden_low, down_weight)
    grad_result = cotangent[0]
    grad_hidden = matmul_t(grad_result, down_weight)
    grad_pre = gelu_back(grad_hidden)[0].astype(bf16)
    grad_normed_two = matmul_t(grad_pre, up_weight)
    grad_middle_part, grad_ln2_gain, grad_ln2_bias = norm_two_back(grad_normed_two)
    grad_middle = grad_result.astype(f32) + grad_middle_part
    grad_branch = grad_middle.astype(bf16)
    grad_mixed = matmul_t(grad_branch, out_weight)
    delta = jnp.sum((lax.reduce_precision(grad_mixed, 8, 7) * mixed).reshape(tokens, heads, width // heads), axis=-1)

    lse3 = jnp.stack(split3(lse), axis=2)
    delta3 = jnp.stack(split3(delta), axis=2)
    head_columns = jnp.concatenate(
        [lse3.reshape(tokens, 3 * heads), delta3.reshape(tokens, 3 * heads)], axis=1
    )
    head_columns = jnp.pad(head_columns, ((0, 0), (lse_at, feat - used)))
    grad_mixed_low = grad_mixed.astype(bf16)
    sent = jnp.concatenate([grad_mixed_low, head_columns], axis=1)
    gathered_back = gather_blocks(sent).reshape(row_len, width + feat)
    d_all = gathered_back[:, :width]
    feat_back = gathered_back[:, width:] + jnp.concatenate(
        [feat_base[:, :ones_at], jnp.zeros((row_len, feat - ones_at), bf16)], axis=1
    )
    own_q = own_base + jnp.pad(-jnp.moveaxis(lse3, 1, 0), ((0, 0), (0, 0), (ones_at, feat - lse_at)))
    own_d = jnp.pad(-jnp.moveaxis(delta3, 1, 0), ((0, 0), (0, 0), (ones_at, feat - lse_at)))
    column = jnp.arange(feat)[None, :]
    head = jnp.arange(heads)[:, None]
    pick_lse = jnp.where((column >= lse_at) & (column < delta_at) & ((column - lse_at) // 3 == head), -1.0, 0.0)
    pick_delta = jnp.where((column >= delta_at) & (column < used) & ((column - delta_at) // 3 == head), -1.0, 0.0)
    own_k = own_base + pick_lse[:, None, :].astype(bf16)
    own_v = pick_delta[:, None, :].astype(bf16)
    d_q, d_k, d_v = attend_back(
        place,
        (q_own, k_own, v_own, grad_mixed_low),
        (q_all, k_all, v_all, d_all),
        (own_q, own_d, own_k, own_v),
        (feat_back, feat_base),
        group,
    )
    grad_packed = jnp.concatenate([d_q, d_k, d_v], axis=1)
    grad_normed_one = matmul_t(grad_packed, qkv_weight)
    grad_source_part, grad_ln1_gain, grad_ln1_bias = norm_one_back(grad_normed_one)
    grad_inputs = (grad_middle + grad_source_part).astype(bf16)[None]

    def halves(value):
        half = value.shape[1] // 2
        mine = lax.dynamic_slice_in_dim(value, core * half, half, 1)
        theirs = lax.dynamic_slice_in_dim(value, (1 - core) * half, half, 1)
        return mine, theirs

    def stripes(value):
        cut = value.reshape(tokens, rows, 2, value.shape[1] // (2 * rows))
        mine = lax.dynamic_index_in_dim(cut, core, 2, keepdims=False)
        theirs = lax.dynamic_index_in_dim(cut, 1 - core, 2, keepdims=False)
        return mine.reshape(tokens, -1), theirs.reshape(tokens, -1)

    def pair_up(mine, theirs):
        got = swap_seq(jnp.concatenate(theirs, axis=1), 1)
        both = []
        cursor = 0
        for own, other in zip(mine, theirs):
            both.append(
                jnp.concatenate([own, got[:, cursor : cursor + other.shape[1]]], axis=0)
            )
            cursor += other.shape[1]
        return both

    def slice_of(value, index):
        extent = value.shape[1] // rows
        return lax.dynamic_slice_in_dim(value, index * extent, extent, 1)

    def vectors(first, second):
        return jnp.pad(jnp.stack([first, second], axis=1), ((0, 0), (0, 126)))

    pre_mine, pre_theirs = halves(grad_pre)
    branch_mine, branch_theirs = halves(grad_branch)
    hidden_mine, hidden_theirs = stripes(hidden_low)
    normed_two_pair, pre_pair, attended_pair, branch_pair, hidden_pair, result_pair = pair_up(
        (normed_two_low, pre_mine, attended, branch_mine, hidden_mine, grad_result),
        (normed_two_low, pre_theirs, attended, branch_theirs, hidden_theirs, grad_result),
    )
    ln2_vectors = vectors(grad_ln2_gain, grad_ln2_bias)

    def first_piece(index):
        up = token_sum(slice_of(normed_two_pair, index), pre_pair)
        out = token_sum(slice_of(attended_pair, index), branch_pair)
        down = token_sum(slice_of(hidden_pair, index), result_pair)
        vec = lax.dynamic_slice_in_dim(ln2_vectors, index * share, share, 0)
        folds = down.shape[0] // share
        return jnp.concatenate(
            [up, out] + [down[i * share : (i + 1) * share] for i in range(folds)] + [vec], axis=1
        )

    first_total = sum_chips(sum_rows(first_piece))

    packed_mine, packed_theirs = halves(grad_packed)
    (packed_pair,) = pair_up((packed_mine,), (packed_theirs,))
    if direct(count):
        normed_pair = normed_all[: 2 * tokens]
    else:
        normed_low = normed_one.astype(bf16)
        normed_pair = jnp.concatenate([normed_low, swap_seq(normed_low, 1)], axis=0)
    ln1_vectors = vectors(grad_ln1_gain, grad_ln1_bias)

    def second_piece(index):
        qkv = token_sum(slice_of(normed_pair, index), packed_pair)
        vec = lax.dynamic_slice_in_dim(ln1_vectors, index * share, share, 0)
        return jnp.concatenate([qkv, vec], axis=1)

    second_total = sum_chips(sum_rows(second_piece))

    def both_cores(mine):
        other = swap_seq(mine, 1)
        return jnp.where(core == 0, mine, other), jnp.where(core == 0, other, mine)

    even, odd = both_cores(first_total)
    up_half = hidden_width // 2
    out_half = width // 2
    up_end = up_half
    out_end = up_end + out_half
    folds = hidden_width // 2 // width
    down_end = out_end + folds * width
    grad_up = jnp.concatenate([even[:, :up_end], odd[:, :up_end]], axis=1).astype(f32)
    grad_out = jnp.concatenate([even[:, up_end:out_end], odd[:, up_end:out_end]], axis=1).astype(f32)
    grad_down = jnp.concatenate(
        [
            part[:, out_end + i * width : out_end + (i + 1) * width]
            for part in (even, odd)
            for i in range(folds)
        ],
        axis=0,
    ).astype(f32)
    ln2 = even[:, down_end : down_end + 2].astype(f32) + odd[:, down_end : down_end + 2].astype(f32)
    even, odd = both_cores(second_total)
    qkv_half = 3 * width // 2
    grad_qkv = jnp.concatenate([even[:, :qkv_half], odd[:, :qkv_half]], axis=1).astype(f32)
    ln1 = even[:, qkv_half : qkv_half + 2].astype(f32) + odd[:, qkv_half : qkv_half + 2].astype(f32)
    return (
        result.astype(bf16)[None],
        grad_inputs,
        ln1[:, 0],
        ln1[:, 1],
        grad_qkv,
        grad_out,
        ln2[:, 0],
        ln2[:, 1],
        grad_up,
        grad_down,
    )


def solution(mesh):
    placed = (
        P("row", "seq", None),
        P("row", "seq"),
        P(),
        P(),
        P(),
        P(),
        P(),
        P(),
        P(),
        P(),
        P(),
        P("row", "seq", None),
    )
    return jax.shard_map(
        shards,
        mesh=mesh,
        in_specs=placed,
        out_specs=(
            P("row", "seq", None),
            P("row", "seq", None),
            P("row"),
            P("row"),
            P("row", None),
            P("row", None),
            P("row"),
            P("row"),
            P("row", None),
            P("row", None),
        ),
        check_vma=False,
    )
```

time: 2650 us -> 310 us (0.12); the launches traced: 2610 us -> 305 us
  local copies, waits for them, and re-layouts: 1430 us -> 36.1 us
  blocking collectives: 463 us -> 0 us
  matrix products: 319 us -> 31.7 us
  other arithmetic: 155 us -> 31.7 us
  loops' own time: 62.2 us -> 0 us
  Pallas kernels: 0 us -> 37.2 us
    gather x158 -> x0, local copies, waits for them, and re-layouts: 797 us -> none  [the longest x106 596 us: take_slots(): return jnp.take_along_axis(array, index_table[:, :, None], axis=0)]
    unnamed x1 -> x0, blocking collectives: 454 us -> none
    dot_general x179 -> x26, matrix products: 319 us -> 31.7 us  [the longest x6 12.7 us: matmul(): return jnp.dot(left, right, preferred_element_type=f32)]
    reshape x19 -> x5, local copies, waits for them, and re-layouts: 141 us -> 0.88 us  [the longest x1 0.58 us: stripes(): cut = value.reshape(tokens, rows, 2, value.shape[1] // (2 * rows))]
    another operation x63 -> x11, local copies, waits for them, and re-layouts: 119 us -> 1.29 us  [the longest x6 0.97 us: vectors(): return jnp.pad(jnp.stack([first, second], axis=1), ((0, 0), (0, 126)))]
    ppermute x45 -> x28, waiting for transfers between devices: 32.5 us -> 138 us  [the longest x24 94 us: swap_seq(): return lax.ppermute(value, 'seq', [(s, s ^ mask) for s in range(count)])]
    unnamed x2 -> x0, waiting for transfers between devices: 82.3 us -> none
    dynamic_slice x79 -> x7, local copies, waits for them, and re-layouts: 75.6 us -> 8.34 us  [the longest x1 4.91 us: stripes(): mine = lax.dynamic_index_in_dim(cut, core, 2, keepdims=False)]
  transfers between devices with their start and end apart: 46 -> 28, of which waited for: 7 -> 14; matrix products, arithmetic and copies ran while one was open for 47% -> 16% of each run, Pallas kernels for 0% -> 9%
where the time goes in v1:
time: 310 us; the launch traced here: 305 us
  waiting for transfers between devices  138 us (45%)
  Pallas kernels  37.2 us (12%)
  local copies, waits for them, and re-layouts  36.1 us (12%)
  other arithmetic  31.7 us (10%)
  matrix products  31.7 us (10%)
  starting transfers between devices  28.1 us (9%)
    ppermute x24, waiting for transfers between devices, swap_seq(): return lax.ppermute(value, 'seq', [(s, s ^ mask) for s in range(count)])  94 us
    ppermute x4, waiting for transfers between devices, swap_row(): return lax.ppermute(value, ('row', 'seq'), pairs)  44 us
    pallas_call x1, Pallas kernels, attend_back(): pl.pallas_call(functools.partial(backward_kernel, tokens=tokens), grid_sp...  27.9 us
    ppermute x24, starting transfers between devices, swap_seq(): return lax.ppermute(value, 'seq', [(s, s ^ mask) for s in range(count)])  24.9 us
    dot_general x6, matrix products, matmul(): return jnp.dot(left, right, preferred_element_type=f32)  12.7 us
    dot_general x16, matrix products, token_sum(): lax.dot_general(left, right, (((0,), (0,)), ((), ())), preferred_element_...  10.6 us
    pallas_call x1, Pallas kernels, attend(): pl.pallas_call(functools.partial(forward_kernel, tokens=tokens, chunk=chu...  9.21 us
    dot_general x4, matrix products, matmul_t(): lax.dot_general(left, right, (((1,), (1,)), ((), ())), preferred_element_...  8.44 us
  transfers between devices with their start and end apart: 28, of which 14 were waited for; matrix products, arithmetic and copies ran while one was open for 16% of the time, Pallas kernels for 9%

profile of v1, /device:TPU:15, one launch (start us, length us, event | category | flops | bytes accessed | tf_op | source)
XLA Modules:
  0.0 304.8 jit_solution(10603060936320984415)
XLA Ops:
  1.4 1.0 fusion.169
  2.4 2.4 collective-permute-start.1
  5.1 1.0 convert_reduce_fusion
  9.3 5.7 %collective-permute-done.1 = bf16[144,768]{1,0:T(8,128)(2,1)S(1)} collective-permute-done((bf16[144,768]{1,0:T(8,128)(2,1)S(1)}, bf16[144,768]{1,0:T(8,128)(2,1)S(1)}, u32[]{:S(2)}, u32[]{:S(2)}) %collective-permute-start.1) | collective-permute-done | bytes 221216 | tf_op jit(solution)/shard_map/ppermute | solution.py:51
  15.0 9.0 %collective-permute-done.2 = bf16[144,768]{1,0:T(8,128)(2,1)S(1)} collective-permute-done((bf16[144,768]{1,0:T(8,128)(2,1)S(1)}, bf16[144,768]{1,0:T(8,128)(2,1)S(1)}, u32[]{:S(2)}, u32[]{:S(2)}) %collective-permute-start.2) | collective-permute-done | bytes 221216 | tf_op jit(solution)/shard_map/ppermute | solution.py:51
  24.0 1.1 fusion.171
  26.4 1.1 reduce-precision_convert_fusion
  27.6 1.3 broadcast_add_fusion
  28.9 1.3 pad_maximum_fusion.2
  33.8 1.4 convolution_convert_fusion.4.v_ref.v_all
  35.2 1.4 convolution_convert_fusion.5.k_ref.k_all
  36.6 1.4 fusion.12.q_all
  40.6 1.3 concatenate.100.all_ref.feat_k
  41.9 9.2 %attend.1 = (f32[128,768]{1,0:T(8,128)}, f32[128,128]{1,0:T(8,128)}) custom-call(s32[2]{0:T(128)} %pad_add_fusion.1.place_ref, bf16[128,768]{1,0:T(8,128)(2,1)} %slice.232.q_ref.q_own, bf16[1024,768]{1,0:T(8,128)(2,1)} %copy-done.4, bf16[1024,768]{1,0:T(8,128)(2,1)} %copy-done.3, bf16[12,128,128]{2,1,0:T(8,128)(2,1)} %get-tuple-element.53.own_ref, ...), custom_call_target="tpu_custom_call" | custom-call | tf_op jit(solution)/shard_map/attend/pallas_call | solution.py:315
  52.5 1.0 convert_element_type.281
  55.0 6.6 %multiply_convert_fusion = (bf16[128,3072]{1,0:T(8,128)(2,1)S(1)}, f32[128,3072]{1,0:T(8,128)S(1)}, f32[128,3072]{1,0:T(8,128)S(1)}) fusion(bf16[128,768]{1,0:T(8,128)(2,1)S(1)} %get-tuple-element.49, bf16[768,3072]{1,0:T(8,128)(2,1)} %param.23), kind=kOutput, calls=%fused_computation.26 | convolution fusion | flops 629538816 | bytes 8847360 | tf_op jit(solution)/shard_map/dot_general | solution.py:31
  61.7 1.9 add_convert_fusion.2
  63.7 1.8 multiply_reduce_fusion.1
  67.3 1.4 reduce-precision_multiply_fusion
  68.6 1.2 copy.127
  71.1 3.4 %collective-permute-start.4 = (bf16[128,896]{1,0:T(8,128)(2,1)}, bf16[128,896]{1,0:T(8,128)(2,1)}, u32[]{:S(2)}, u32[]{:S(2)}) collective-permute-start(bf16[128,896]{1,0:T(8,128)(2,1)} %get-tuple-element.96), channel_id=1, source_target_pairs={{0,2},{1,3},{2,0},{3,1},{4,6},{5,7},{6,4},{7,5},{8,10},{9,11},{10,... | collective-permute-start | bytes 688136 | tf_op jit(solution)/shard_map/ppermute | solution.py:51
  74.5 1.0 copy.132
  76.0 4.9 %dynamic-slice_reduce_fusion = (bf16[128,4,384]{2,1,0:T(4,128)(2,1)S(1)}, bf16[128,4,384]{2,1,0:T(4,128)(2,1)S(1)}) fusion(bf16[128,4,2,384]{3,2,1,0:T(2,128)(2,1)S(1)} %reshape.825, s32[]{:T(128)S(6)} %select_n.350, s32[]{:T(128)S(6)} %select_n.347), kind=kLoop, calls=%fused_computation.82 | loop fusion | bytes 1572872 | tf_op jit(solution)/shard_map/jit(dynamic_index_in_dim)/dynamic_slice | solution.py:517
  85.4 8.9 %collective-permute-done.6 = bf16[128,896]{1,0:T(8,128)(2,1)} collective-permute-done((bf16[128,896]{1,0:T(8,128)(2,1)}, bf16[128,896]{1,0:T(8,128)(2,1)}, u32[]{:S(2)}, u32[]{:S(2)}) %collective-permute-start.6) | collective-permute-done | bytes 229408 | tf_op jit(solution)/shard_map/ppermute | solution.py:51
  94.4 2.3 fusion.172
  97.5 1.7 constant_dynamic-slice_fusion.3
  99.2 1.8 constant_dynamic-update-slice_fusion.4
  101.7 0.9 pad_add_fusion.own_q
  102.7 1.4 pad_maximum_fusion.1
  105.0 1.1 fusion.41.feat_q
  106.1 1.4 slice.236.d_all
  107.4 27.9 %attend_back.1 = (bf16[128,768]{1,0:T(8,128)(2,1)}, bf16[128,768]{1,0:T(8,128)(2,1)}, bf16[128,768]{1,0:T(8,128)(2,1)}) custom-call(s32[2]{0:T(128)} %pad_add_fusion.1.place_ref, bf16[128,768]{1,0:T(8,128)(2,1)} %slice.232.q_ref.q_own, bf16[128,768]{1,0:T(8,128)(2,1)} %slice.234.k_own, bf16[128,768]{1,0:T(8,128)(2,1)} %slice.235.v_own, ...), custom_call_target="tpu_custom_call" | custom-call | tf_op jit(solution)/shard_map/attend_back/pallas_call | solution.py:348
  136.3 0.9 constant_dynamic-update-slice_fusion.1
  137.2 0.9 constant_dynamic-update-slice_fusion
  138.2 3.4 %fusion.35 = (f32[128]{0:T(128)S(1)}, f32[128]{0:T(128)S(1)}, f32[128,768]{1,0:T(8,128)S(1)}) fusion(f32[128]{0:T(128)S(1)} %copy-done.31, bf16[1,128,768]{2,1,0:T(8,128)(2,1)S(1)} %copy-done.5, f32[768]{0:T(1024)S(1)} %copy-done.28, bf16[128,2304]{1,0:T(8,128)(2,1)S(1)} %constant_dynamic-update-slice_fusion, bf16[768,2304]{1,0:T(8,128)(2,1)} %param.19), kind=kOutput, calls=%fused_computation.128 | convolution fusion | flops 453672704 | bytes 4723200 | tf_op jit(solution)/shard_map/dot_general | solution.py:35
  143.5 1.3 collective-permute-done.8
  144.7 1.5 convolution_convert_fusion.3
  146.2 1.5 convolution_convert_fusion.2
  147.7 1.2 fusion.175
  148.9 1.2 fusion.176
  154.3 1.3 collective-permute-start.9
  155.6 1.4 fusion.71
  157.0 1.4 fusion.75
  161.1 35.6 %collective-permute-done.9 = bf16[384,1280]{1,0:T(8,128)(2,1)S(1)} collective-permute-done((bf16[384,1280]{1,0:T(8,128)(2,1)S(1)}, bf16[384,1280]{1,0:T(8,128)(2,1)S(1)}, u32[]{:S(2)}, u32[]{:S(2)}) %collective-permute-start.9) | collective-permute-done | bytes 983072 | tf_op jit(solution)/shard_map/ppermute | solution.py:62
  197.4 1.3 collective-permute-start.20
  198.7 6.2 %collective-permute-done.10 = bf16[192,1280]{1,0:T(8,128)(2,1)S(1)} collective-permute-done((bf16[192,1280]{1,0:T(8,128)(2,1)S(1)}, bf16[192,1280]{1,0:T(8,128)(2,1)S(1)}, u32[]{:S(2)}, u32[]{:S(2)}) %collective-permute-start.10) | collective-permute-done | bytes 491552 | tf_op jit(solution)/shard_map/ppermute | solution.py:62
  205.2 3.5 %collective-permute-start.12 = (bf16[48,1280]{1,0:T(8,128)(2,1)S(1)}, bf16[48,1280]{1,0:T(8,128)(2,1)S(1)}, u32[]{:S(2)}, u32[]{:S(2)}) collective-permute-start(bf16[48,1280]{1,0:T(8,128)(2,1)S(1)} %get-tuple-element.84), channel_id=1, source_target_pairs={{0,4},{1,5},{2,6},{3,7},{4,0},{5,1},{6,2},{7,3},{8,12},{9,13},{10,... | collective-permute-start | bytes 368648 | tf_op jit(solution)/shard_map/ppermute | solution.py:51
  208.7 1.5 fusion.20
  210.2 6.0 %collective-permute-done.12 = bf16[48,1280]{1,0:T(8,128)(2,1)S(1)} collective-permute-done((bf16[48,1280]{1,0:T(8,128)(2,1)S(1)}, bf16[48,1280]{1,0:T(8,128)(2,1)S(1)}, u32[]{:S(2)}, u32[]{:S(2)}) %collective-permute-start.12) | collective-permute-done | bytes 122912 | tf_op jit(solution)/shard_map/ppermute | solution.py:51
  216.3 1.1 collective-permute-start.14
  217.4 2.2 collective-permute-done.20
  220.4 3.4 %collective-permute-start.22 = (bf16[48,3584]{1,0:T(8,128)(2,1)S(1)}, bf16[48,3584]{1,0:T(8,128)(2,1)S(1)}, u32[]{:S(2)}, u32[]{:S(2)}) collective-permute-start(bf16[48,3584]{1,0:T(8,128)(2,1)S(1)} %get-tuple-element.71), channel_id=1, source_target_pairs={{0,4},{1,5},{2,6},{3,7},{4,0},{5,1},{6,2},{7,3},{8,12},{9,13},{10,... | collective-permute-start | bytes 1032200 | tf_op jit(solution)/shard_map/ppermute | solution.py:51
  224.1 3.9 %collective-permute-done.21 = bf16[48,3584]{1,0:T(8,128)(2,1)S(1)} collective-permute-done((bf16[48,3584]{1,0:T(8,128)(2,1)S(1)}, bf16[48,3584]{1,0:T(8,128)(2,1)S(1)}, u32[]{:S(2)}, u32[]{:S(2)}) %collective-permute-start.21) | collective-permute-done | bytes 344096 | tf_op jit(solution)/shard_map/ppermute | solution.py:51
  228.0 25.4 %collective-permute-done.22 = bf16[48,3584]{1,0:T(8,128)(2,1)S(1)} collective-permute-done((bf16[48,3584]{1,0:T(8,128)(2,1)S(1)}, bf16[48,3584]{1,0:T(8,128)(2,1)S(1)}, u32[]{:S(2)}, u32[]{:S(2)}) %collective-permute-start.22) | collective-permute-done | bytes 344096 | tf_op jit(solution)/shard_map/ppermute | solution.py:51
  253.8 3.0 collective-permute-start.24
  256.8 3.4 %collective-permute-done.16 = bf16[48,1280]{1,0:T(8,128)(2,1)S(1)} collective-permute-done((bf16[48,1280]{1,0:T(8,128)(2,1)S(1)}, bf16[48,1280]{1,0:T(8,128)(2,1)S(1)}, u32[]{:S(2)}, u32[]{:S(2)}) %collective-permute-start.16) | collective-permute-done | bytes 122912 | tf_op jit(solution)/shard_map/ppermute | solution.py:51
  260.2 3.3 %collective-permute-start.17 = (bf16[192,1280]{1,0:T(8,128)(2,1)S(1)}, bf16[192,1280]{1,0:T(8,128)(2,1)S(1)}, u32[]{:S(2)}, u32[]{:S(2)}) collective-permute-start(bf16[192,1280]{1,0:T(8,128)(2,1)S(1)} %constant_dynamic-update-slice_fusion.13), channel_id=1, source_target_pairs={{0,1},{1,0},{2,3},{3,2},{4,5},{5,4},{6,7},{7,6},{8,9},{9,8},{10,11... | collective-permute-start | bytes 1474568 | tf_op jit(solution)/shard_map/ppermute | solution.py:51
  263.5 1.1 collective-permute-start.26
  264.7 21.2 %collective-permute-done.25 = bf16[48,3584]{1,0:T(8,128)(2,1)S(1)} collective-permute-done((bf16[48,3584]{1,0:T(8,128)(2,1)S(1)}, bf16[48,3584]{1,0:T(8,128)(2,1)S(1)}, u32[]{:S(2)}, u32[]{:S(2)}) %collective-permute-start.25) | collective-permute-done | bytes 344096 | tf_op jit(solution)/shard_map/ppermute | solution.py:51
  285.9 9.0 %collective-permute-done.26 = bf16[48,3584]{1,0:T(8,128)(2,1)S(1)} collective-permute-done((bf16[48,3584]{1,0:T(8,128)(2,1)S(1)}, bf16[48,3584]{1,0:T(8,128)(2,1)S(1)}, u32[]{:S(2)}, u32[]{:S(2)}) %collective-permute-start.26) | collective-permute-done | bytes 344096 | tf_op jit(solution)/shard_map/ppermute | solution.py:51
  294.9 1.0 collective-permute-start.27
  297.9 1.3 maximum_convert_fusion.2
  301.3 1.7 maximum_convert_fusion
  303.0 1.6 maximum_convert_fusion.1
  (261 shorter events, 41.2 us)
Async XLA Ops:
  0.6 52.8 %copy-start = (bf16[768,768]{1,0:T(8,128)(2,1)S(1)}, bf16[768,768]{1,0:T(8,128)(2,1)}, u32[]{:S(2)}) copy-start(bf16[768,768]{1,0:T(8,128)(2,1)} %param.20) | copy-start | bytes 3538948
  2.4 12.6 %collective-permute-start.1 = (bf16[144,768]{1,0:T(8,128)(2,1)S(1)}, bf16[144,768]{1,0:T(8,128)(2,1)S(1)}, u32[]{:S(2)}, u32[]{:S(2)}) collective-permute-start(bf16[144,768]{1,0:T(8,128)(2,1)S(1)} %get-tuple-element.98), channel_id=1, source_target_pairs={{0,4},{1,5},{2,6},{3,7},{4,0},{5,1},{6,2},{7,3},{8,12},{9,13},{10,... | collective-permute-start | bytes 663560 | tf_op jit(solution)/shard_map/ppermute | solution.py:51
  4.7 10.3 %collective-permute-start = (bf16[144,768]{1,0:T(8,128)(2,1)S(1)}, bf16[144,768]{1,0:T(8,128)(2,1)S(1)}, u32[]{:S(2)}, u32[]{:S(2)}) collective-permute-start(bf16[144,768]{1,0:T(8,128)(2,1)S(1)} %get-tuple-element.98), channel_id=1, source_target_pairs={{0,2},{1,3},{2,0},{3,1},{4,6},{5,7},{6,4},{7,5},{8,10},{9,11},{10,... | collective-permute-start | bytes 663560 | tf_op jit(solution)/shard_map/ppermute | solution.py:51
  4.9 19.1 %collective-permute-start.2 = (bf16[144,768]{1,0:T(8,128)(2,1)S(1)}, bf16[144,768]{1,0:T(8,128)(2,1)S(1)}, u32[]{:S(2)}, u32[]{:S(2)}) collective-permute-start(bf16[144,768]{1,0:T(8,128)(2,1)S(1)} %get-tuple-element.98), channel_id=1, source_target_pairs={{0,6},{1,7},{2,4},{3,5},{4,2},{5,3},{6,0},{7,1},{8,14},{9,15},{10,... | collective-permute-start | bytes 663560 | tf_op jit(solution)/shard_map/ppermute | solution.py:51
  25.1 3.9 %collective-permute-start.3 = (bf16[4,144,768]{2,1,0:T(8,128)(2,1)}, bf16[4,144,768]{2,1,0:T(8,128)(2,1)}, u32[]{:S(2)}, u32[]{:S(2)}) collective-permute-start(bf16[4,144,768]{2,1,0:T(8,128)(2,1)} %get-tuple-element.77), channel_id=1, source_target_pairs={{0,1},{1,0},{2,3},{3,2},{4,5},{5,4},{6,7},{7,6},{8,9},{9,8},{10,11... | collective-permute-start | bytes 2654216 | tf_op jit(solution)/shard_map/ppermute | solution.py:51
  31.7 2.1 copy-start.7
  35.2 3.0 copy-start.3
  36.6 3.3 %copy-start.4 = (bf16[1024,768]{1,0:T(8,128)(2,1)}, bf16[1024,768]{1,0:T(8,128)(2,1)S(1)}, u32[]{:S(2)}) copy-start(bf16[1024,768]{1,0:T(8,128)(2,1)S(1)} %convolution_convert_fusion.5.k_ref.k_all) | copy-start | bytes 4718596
  38.0 2.5 copy-start.19
  38.3 3.7 %copy-start.17 = (bf16[1024,4]{1,0:T(8,128)(2,1)}, bf16[1024,4]{1,0:T(8,128)(2,1)S(1)}, u32[]{:S(2)}) copy-start(bf16[1024,4]{1,0:T(8,128)(2,1)S(1)} %fusion.33) | copy-start | bytes 24580
  41.9 11.6 %copy-start.5 = (bf16[1,128,768]{2,1,0:T(8,128)(2,1)S(1)}, bf16[1,128,768]{2,1,0:T(8,128)(2,1)}, u32[]{:S(2)}) copy-start(bf16[1,128,768]{2,1,0:T(8,128)(2,1)} %param.14) | copy-start | bytes 589828
  52.1 2.0 copy-start.29
  52.1 2.0 copy-start.33
  53.5 10.1 %slice-start = ((s8[4718592]{0:T(1024)(128)(4,1)}), s8[4194304]{0:T(1024)(128)(4,1)S(1)}, s32[]{:S(2)}) async-start(s8[4718592]{0:T(1024)(128)(4,1)} %bitcast.151), calls=%async_computation | async-start | bytes 8388608
  54.0 7.7 %slice-start.2 = ((s8[4718592]{0:T(1024)(128)(4,1)}), s8[4194304]{0:T(1024)(128)(4,1)S(1)}, s32[]{:S(2)}) async-start(s8[4718592]{0:T(1024)(128)(4,1)} %bitcast.153), calls=%async_computation.2 | async-start | bytes 8388608
  55.0 6.7 %copy-start.20 = (bf16[128,768]{1,0:T(8,128)(2,1)}, bf16[128,768]{1,0:T(8,128)(2,1)S(1)}, u32[]{:S(2)}) copy-start(bf16[128,768]{1,0:T(8,128)(2,1)S(1)} %get-tuple-element.49) | copy-start | bytes 589828
  55.0 6.7 %copy-start.2 = (bf16[1,128,768]{2,1,0:T(8,128)(2,1)S(1)}, bf16[1,128,768]{2,1,0:T(8,128)(2,1)}, u32[]{:S(2)}) copy-start(bf16[1,128,768]{2,1,0:T(8,128)(2,1)} %param.25) | copy-start | bytes 589828
  55.0 6.7 %slice-start.3 = ((s8[4718592]{0:T(1024)(128)(4,1)}), s8[524288]{0:T(1024)(128)(4,1)S(1)}, s32[]{:S(2)}) async-start(s8[4718592]{0:T(1024)(128)(4,1)} %bitcast.153), calls=%async_computation.3 | async-start | bytes 1048576
  55.0 8.6 %slice-start.1 = ((s8[4718592]{0:T(1024)(128)(4,1)}), s8[524288]{0:T(1024)(128)(4,1)S(1)}, s32[]{:S(2)}) async-start(s8[4718592]{0:T(1024)(128)(4,1)} %bitcast.151), calls=%async_computation.1 | async-start | bytes 1048576
  61.7 13.8 %copy-start.11 = (bf16[128,3072]{1,0:T(8,128)(2,1)}, bf16[128,3072]{1,0:T(8,128)(2,1)S(1)}, u32[]{:S(2)}) copy-start(bf16[128,3072]{1,0:T(8,128)(2,1)S(1)} %get-tuple-element.56) | copy-start | bytes 2359300
  63.6 1.8 copy-start.13
  65.5 1.8 copy-start.6
  65.7 2.9 copy-start.34
  68.6 1.5 copy-start.23
  71.0 14.1 %collective-permute-start.5 = (bf16[128,896]{1,0:T(8,128)(2,1)}, bf16[128,896]{1,0:T(8,128)(2,1)}, u32[]{:S(2)}, u32[]{:S(2)}) collective-permute-start(bf16[128,896]{1,0:T(8,128)(2,1)} %get-tuple-element.96), channel_id=1, source_target_pairs={{0,4},{1,5},{2,6},{3,7},{4,0},{5,1},{6,2},{7,3},{8,12},{9,13},{10,... | collective-permute-start | bytes 688136 | tf_op jit(solution)/shard_map/ppermute | solution.py:51
  71.1 14.4 %collective-permute-start.4 = (bf16[128,896]{1,0:T(8,128)(2,1)}, bf16[128,896]{1,0:T(8,128)(2,1)}, u32[]{:S(2)}, u32[]{:S(2)}) collective-permute-start(bf16[128,896]{1,0:T(8,128)(2,1)} %get-tuple-element.96), channel_id=1, source_target_pairs={{0,2},{1,3},{2,0},{3,1},{4,6},{5,7},{6,4},{7,5},{8,10},{9,11},{10,... | collective-permute-start | bytes 688136 | tf_op jit(solution)/shard_map/ppermute | solution.py:51
  74.4 19.9 %collective-permute-start.6 = (bf16[128,896]{1,0:T(8,128)(2,1)}, bf16[128,896]{1,0:T(8,128)(2,1)}, u32[]{:S(2)}, u32[]{:S(2)}) collective-permute-start(bf16[128,896]{1,0:T(8,128)(2,1)} %get-tuple-element.96), channel_id=1, source_target_pairs={{0,6},{1,7},{2,4},{3,5},{4,2},{5,3},{6,0},{7,1},{8,14},{9,15},{10,... | collective-permute-start | bytes 688136 | tf_op jit(solution)/shard_map/ppermute | solution.py:51
  80.9 2.7 copy-start.14
  82.7 11.6 %copy-start.26 = (bf16[1,128,896]{2,1,0:T(8,128)(2,1)S(1)}, bf16[1,128,896]{2,1,0:T(8,128)(2,1)}, u32[]{:S(2)}) copy-start(bf16[1,128,896]{2,1,0:T(8,128)(2,1)} %get-tuple-element.95) | copy-start | bytes 688132
  84.5 12.8 %copy-start.30 = (f32[768,1]{0,1:T(1,128)S(1)}, f32[768,1]{0,1:T(1,128)}, u32[]{:S(2)}) copy-start(f32[768,1]{0,1:T(1,128)} %stack.118) | copy-start | bytes 9220
  96.7 5.1 %copy-start.8 = (bf16[12,128,128]{2,1,0:T(8,128)(2,1)S(1)}, bf16[12,128,128]{2,1,0:T(8,128)(2,1)}, u32[]{:S(2)}) copy-start(bf16[12,128,128]{2,1,0:T(8,128)(2,1)} %get-tuple-element.53.own_ref) | copy-start | bytes 1179652
  96.7 6.0 %collective-permute-start.7 = (bf16[4,128,896]{2,1,0:T(8,128)(2,1)}, bf16[4,128,896]{2,1,0:T(8,128)(2,1)}, u32[]{:S(2)}, u32[]{:S(2)}) collective-permute-start(bf16[4,128,896]{2,1,0:T(8,128)(2,1)} %get-tuple-element.75), channel_id=1, source_target_pairs={{0,1},{1,0},{2,3},{3,2},{4,5},{5,4},{6,7},{7,6},{8,9},{9,8},{10,11... | collective-permute-start | bytes 2752520 | tf_op jit(solution)/shard_map/ppermute | solution.py:51
  97.5 4.3 %copy-start.24 = (bf16[128,12,3]{2,0,1:T(8,128)(2,1)S(1)}, bf16[128,12,3]{2,0,1:T(8,128)(2,1)}, u32[]{:S(2)}) copy-start(bf16[128,12,3]{2,0,1:T(8,128)(2,1)} %copy.132) | copy-start | bytes 27652
  101.7 46.0 %collective-permute-start.18 = (bf16[128,5760]{1,0:T(8,128)(2,1)}, bf16[128,5760]{1,0:T(8,128)(2,1)}, u32[]{:S(2)}, u32[]{:S(2)}) collective-permute-start(bf16[128,5760]{1,0:T(8,128)(2,1)} %constant_dynamic-update-slice_fusion.3), channel_id=1, source_target_pairs={{0,1},{1,0},{2,3},{3,2},{4,5},{5,4},{6,7},{7,6},{8,9},{9,8},{10,11... | collective-permute-start | bytes 4423688 | tf_op jit(solution)/shard_map/ppermute | solution.py:51
  107.4 30.8 %copy-start.31 = (f32[128]{0:T(128)S(1)}, f32[128]{0:T(128)}, u32[]{:S(2)}) copy-start(f32[128]{0:T(128)} %broadcast_multiply_fusion.1) | copy-start | bytes 1540
  142.7 2.0 collective-permute-start.8
  147.7 2.4 copy-start.21
  151.1 1.7 copy-start.16
  151.1 1.7 copy-start.27
  153.9 1.7 copy-start.25
  153.9 43.2 %collective-permute-start.19 = (bf16[384,3584]{1,0:T(8,128)(2,1)S(1)}, bf16[384,3584]{1,0:T(8,128)(2,1)S(1)}, u32[]{:S(2)}, u32[]{:S(2)}) collective-permute-start(bf16[384,3584]{1,0:T(8,128)(2,1)S(1)} %pad_maximum_fusion), channel_id=1, source_target_pairs={{0,8},{1,17},{2,10},{3,19},{4,12},{5,21},{6,14},{7,23},{8,0},{9,25... | collective-permute-start | bytes 8257544 | tf_op jit(solution)/shard_map/ppermute | solution.py:62
  154.3 42.5 %collective-permute-start.9 = (bf16[384,1280]{1,0:T(8,128)(2,1)S(1)}, bf16[384,1280]{1,0:T(8,128)(2,1)S(1)}, u32[]{:S(2)}, u32[]{:S(2)}) collective-permute-start(bf16[384,1280]{1,0:T(8,128)(2,1)S(1)} %maximum_maximum_fusion), channel_id=1, source_target_pairs={{0,8},{1,17},{2,10},{3,19},{4,12},{5,21},{6,14},{7,23},{8,0},{9,25... | collective-permute-start | bytes 2949128 | tf_op jit(solution)/shard_map/ppermute | solution.py:62
  161.1 47.6 %slice-start.4 = ((s8[4718592]{0:T(1024)(128)(4,1)}), s8[4194304]{0:T(1024)(128)(4,1)S(1)}, s32[]{:S(2)}) async-start(s8[4718592]{0:T(1024)(128)(4,1)} %bitcast.155), calls=%async_computation.4 | async-start | bytes 8388608
  196.8 8.0 %collective-permute-start.10 = (bf16[192,1280]{1,0:T(8,128)(2,1)S(1)}, bf16[192,1280]{1,0:T(8,128)(2,1)S(1)}, u32[]{:S(2)}, u32[]{:S(2)}) collective-permute-start(bf16[192,1280]{1,0:T(8,128)(2,1)S(1)} %fusion.23), channel_id=1, source_target_pairs={{0,16},{1,9},{2,18},{3,11},{4,20},{5,13},{6,22},{7,15},{8,24},{9,1... | collective-permute-start | bytes 1474568 | tf_op jit(solution)/shard_map/ppermute | solution.py:62
  197.1 11.6 %slice-start.5 = ((s8[4718592]{0:T(1024)(128)(4,1)}), s8[524288]{0:T(1024)(128)(4,1)S(1)}, s32[]{:S(2)}) async-start(s8[4718592]{0:T(1024)(128)(4,1)} %bitcast.155), calls=%async_computation.5 | async-start | bytes 1048576
  197.4 22.2 %collective-permute-start.20 = (bf16[192,3584]{1,0:T(8,128)(2,1)S(1)}, bf16[192,3584]{1,0:T(8,128)(2,1)S(1)}, u32[]{:S(2)}, u32[]{:S(2)}) collective-permute-start(bf16[192,3584]{1,0:T(8,128)(2,1)S(1)} %add_convert_fusion.1), channel_id=1, source_target_pairs={{0,16},{1,9},{2,18},{3,11},{4,20},{5,13},{6,22},{7,15},{8,24},{9,1... | collective-permute-start | bytes 4128776 | tf_op jit(solution)/shard_map/ppermute | solution.py:62
  204.9 3.8 %copy-start.12 = (bf16[128,3072]{1,0:T(8,128)(2,1)S(1)}, bf16[128,3072]{1,0:T(8,128)(2,1)}, u32[]{:S(2)}) copy-start(bf16[128,3072]{1,0:T(8,128)(2,1)} %copy-done.11) | copy-start | bytes 2359300
  205.1 5.1 %collective-permute-start.11 = (bf16[48,1280]{1,0:T(8,128)(2,1)S(1)}, bf16[48,1280]{1,0:T(8,128)(2,1)S(1)}, u32[]{:S(2)}, u32[]{:S(2)}) collective-permute-start(bf16[48,1280]{1,0:T(8,128)(2,1)S(1)} %get-tuple-element.82), channel_id=1, source_target_pairs={{0,2},{1,3},{2,0},{3,1},{4,6},{5,7},{6,4},{7,5},{8,10},{9,11},{10,... | collective-permute-start | bytes 368648 | tf_op jit(solution)/shard_map/ppermute | solution.py:51
  205.2 5.0 %collective-permute-start.13 = (bf16[48,1280]{1,0:T(8,128)(2,1)S(1)}, bf16[48,1280]{1,0:T(8,128)(2,1)S(1)}, u32[]{:S(2)}, u32[]{:S(2)}) collective-permute-start(bf16[48,1280]{1,0:T(8,128)(2,1)S(1)} %get-tuple-element.83), channel_id=1, source_target_pairs={{0,6},{1,7},{2,4},{3,5},{4,2},{5,3},{6,0},{7,1},{8,14},{9,15},{10,... | collective-permute-start | bytes 368648 | tf_op jit(solution)/shard_map/ppermute | solution.py:51
  205.2 10.9 %collective-permute-start.12 = (bf16[48,1280]{1,0:T(8,128)(2,1)S(1)}, bf16[48,1280]{1,0:T(8,128)(2,1)S(1)}, u32[]{:S(2)}, u32[]{:S(2)}) collective-permute-start(bf16[48,1280]{1,0:T(8,128)(2,1)S(1)} %get-tuple-element.84), channel_id=1, source_target_pairs={{0,4},{1,5},{2,6},{3,7},{4,0},{5,1},{6,2},{7,3},{8,12},{9,13},{10,... | collective-permute-start | bytes 368648 | tf_op jit(solution)/shard_map/ppermute | solution.py:51
  216.3 7.5 %collective-permute-start.14 = (bf16[48,1280]{1,0:T(8,128)(2,1)S(1)}, bf16[48,1280]{1,0:T(8,128)(2,1)S(1)}, u32[]{:S(2)}, u32[]{:S(2)}) collective-permute-start(bf16[48,1280]{1,0:T(8,128)(2,1)S(1)} %get-tuple-element.51), channel_id=1, source_target_pairs={{0,2},{1,3},{2,0},{3,1},{4,6},{5,7},{6,4},{7,5},{8,10},{9,11},{10,... | collective-permute-start | bytes 368648 | tf_op jit(solution)/shard_map/ppermute | solution.py:51
  220.1 7.9 %collective-permute-start.21 = (bf16[48,3584]{1,0:T(8,128)(2,1)S(1)}, bf16[48,3584]{1,0:T(8,128)(2,1)S(1)}, u32[]{:S(2)}, u32[]{:S(2)}) collective-permute-start(bf16[48,3584]{1,0:T(8,128)(2,1)S(1)} %get-tuple-element.69), channel_id=1, source_target_pairs={{0,2},{1,3},{2,0},{3,1},{4,6},{5,7},{6,4},{7,5},{8,10},{9,11},{10,... | collective-permute-start | bytes 1032200 | tf_op jit(solution)/shard_map/ppermute | solution.py:51
  220.2 7.8 %collective-permute-start.23 = (bf16[48,3584]{1,0:T(8,128)(2,1)S(1)}, bf16[48,3584]{1,0:T(8,128)(2,1)S(1)}, u32[]{:S(2)}, u32[]{:S(2)}) collective-permute-start(bf16[48,3584]{1,0:T(8,128)(2,1)S(1)} %get-tuple-element.70), channel_id=1, source_target_pairs={{0,6},{1,7},{2,4},{3,5},{4,2},{5,3},{6,0},{7,1},{8,14},{9,15},{10,... | collective-permute-start | bytes 1032200 | tf_op jit(solution)/shard_map/ppermute | solution.py:51
  220.4 33.1 %collective-permute-start.22 = (bf16[48,3584]{1,0:T(8,128)(2,1)S(1)}, bf16[48,3584]{1,0:T(8,128)(2,1)S(1)}, u32[]{:S(2)}, u32[]{:S(2)}) collective-permute-start(bf16[48,3584]{1,0:T(8,128)(2,1)S(1)} %get-tuple-element.71), channel_id=1, source_target_pairs={{0,4},{1,5},{2,6},{3,7},{4,0},{5,1},{6,2},{7,3},{8,12},{9,13},{10,... | collective-permute-start | bytes 1032200 | tf_op jit(solution)/shard_map/ppermute | solution.py:51
  223.7 33.0 %collective-permute-start.15 = (bf16[48,1280]{1,0:T(8,128)(2,1)S(1)}, bf16[48,1280]{1,0:T(8,128)(2,1)S(1)}, u32[]{:S(2)}, u32[]{:S(2)}) collective-permute-start(bf16[48,1280]{1,0:T(8,128)(2,1)S(1)} %get-tuple-element.51), channel_id=1, source_target_pairs={{0,4},{1,5},{2,6},{3,7},{4,0},{5,1},{6,2},{7,3},{8,12},{9,13},{10,... | collective-permute-start | bytes 368648 | tf_op jit(solution)/shard_map/ppermute | solution.py:51
  223.8 36.4 %collective-permute-start.16 = (bf16[48,1280]{1,0:T(8,128)(2,1)S(1)}, bf16[48,1280]{1,0:T(8,128)(2,1)S(1)}, u32[]{:S(2)}, u32[]{:S(2)}) collective-permute-start(bf16[48,1280]{1,0:T(8,128)(2,1)S(1)} %get-tuple-element.51), channel_id=1, source_target_pairs={{0,6},{1,7},{2,4},{3,5},{4,2},{5,3},{6,0},{7,1},{8,14},{9,15},{10,... | collective-permute-start | bytes 368648 | tf_op jit(solution)/shard_map/ppermute | solution.py:51
  253.7 42.2 %copy-start.10 = (f32[128,768]{1,0:T(8,128)S(1)}, f32[128,768]{1,0:T(8,128)}, u32[]{:S(2)}) copy-start(f32[128,768]{1,0:T(8,128)} %copy-done.9) | copy-start | bytes 1179652
  253.7 42.2 %copy-start.35 = (f32[128]{0:T(128)S(1)}, f32[128]{0:T(128)}, u32[]{:S(2)}) copy-start(f32[128]{0:T(128)} %copy-done.34) | copy-start | bytes 1540
  253.8 10.9 %collective-permute-start.24 = (bf16[48,3584]{1,0:T(8,128)(2,1)S(1)}, bf16[48,3584]{1,0:T(8,128)(2,1)S(1)}, u32[]{:S(2)}, u32[]{:S(2)}) collective-permute-start(bf16[48,3584]{1,0:T(8,128)(2,1)S(1)} %get-tuple-element.47), channel_id=1, source_target_pairs={{0,2},{1,3},{2,0},{3,1},{4,6},{5,7},{6,4},{7,5},{8,10},{9,11},{10,... | collective-permute-start | bytes 1032200 | tf_op jit(solution)/shard_map/ppermute | solution.py:51
  260.2 36.7 %collective-permute-start.17 = (bf16[192,1280]{1,0:T(8,128)(2,1)S(1)}, bf16[192,1280]{1,0:T(8,128)(2,1)S(1)}, u32[]{:S(2)}, u32[]{:S(2)}) collective-permute-start(bf16[192,1280]{1,0:T(8,128)(2,1)S(1)} %constant_dynamic-update-slice_fusion.13), channel_id=1, source_target_pairs={{0,1},{1,0},{2,3},{3,2},{4,5},{5,4},{6,7},{7,6},{8,9},{9,8},{10,11... | collective-permute-start | bytes 1474568 | tf_op jit(solution)/shard_map/ppermute | solution.py:51
  263.5 22.3 %collective-permute-start.25 = (bf16[48,3584]{1,0:T(8,128)(2,1)S(1)}, bf16[48,3584]{1,0:T(8,128)(2,1)S(1)}, u32[]{:S(2)}, u32[]{:S(2)}) collective-permute-start(bf16[48,3584]{1,0:T(8,128)(2,1)S(1)} %get-tuple-element.47), channel_id=1, source_target_pairs={{0,4},{1,5},{2,6},{3,7},{4,0},{5,1},{6,2},{7,3},{8,12},{9,13},{10,... | collective-permute-start | bytes 1032200 | tf_op jit(solution)/shard_map/ppermute | solution.py:51
  263.5 31.4 %collective-permute-start.26 = (bf16[48,3584]{1,0:T(8,128)(2,1)S(1)}, bf16[48,3584]{1,0:T(8,128)(2,1)S(1)}, u32[]{:S(2)}, u32[]{:S(2)}) collective-permute-start(bf16[48,3584]{1,0:T(8,128)(2,1)S(1)} %get-tuple-element.47), channel_id=1, source_target_pairs={{0,6},{1,7},{2,4},{3,5},{4,2},{5,3},{6,0},{7,1},{8,14},{9,15},{10,... | collective-permute-start | bytes 1032200 | tf_op jit(solution)/shard_map/ppermute | solution.py:51
  294.9 4.3 %collective-permute-start.27 = (bf16[192,3584]{1,0:T(8,128)(2,1)S(1)}, bf16[192,3584]{1,0:T(8,128)(2,1)S(1)}, u32[]{:S(2)}, u32[]{:S(2)}) collective-permute-start(bf16[192,3584]{1,0:T(8,128)(2,1)S(1)} %constant_dynamic-update-slice_fusion.9), channel_id=1, source_target_pairs={{0,1},{1,0},{2,3},{3,2},{4,5},{5,4},{6,7},{7,6},{8,9},{9,8},{10,11... | collective-permute-start | bytes 4128776 | tf_op jit(solution)/shard_map/ppermute | solution.py:51
  303.0 1.7 copy-start.1
  (6 other events, 5.3 us)

commit v2 on v1

v2 whole, which is shorter than its diff:
```python
import functools

import jax
import jax.numpy as jnp
from jax import lax
from jax.experimental import pallas as pl
from jax.experimental.pallas import tpu as pltpu
from jax.sharding import PartitionSpec as P


reaches = (2048, 4096, 8192, 16384, 32768)
dilations = (1, 2, 4, 6, 12)
period = 12
doc_count = 4
epsilon = 1e-05
negative = -1e30
bf16 = jnp.bfloat16
f32 = jnp.float32


def layer_norm(values, gain_vec, shift_vec):
    centered = values - jnp.mean(values, axis=-1, keepdims=True)
    variance = jnp.mean(centered * centered, axis=-1, keepdims=True)
    return centered * lax.rsqrt(variance + epsilon) * gain_vec + shift_vec


def matmul(left, right):
    return jnp.dot(left, right, preferred_element_type=f32)


def matmul_t(left, right):
    return lax.dot_general(left, right, (((1,), (1,)), ((), ())), preferred_element_type=f32)


def token_sum(left, right):
    return lax.dot_general(left, right, (((0,), (0,)), ((), ())), preferred_element_type=f32)


def swap_seq(value, mask):
    count = lax.axis_size("seq")
    return lax.ppermute(value, "seq", [(s, s ^ mask) for s in range(count)])


def swap_row(value, even_mask, odd_mask):
    rows = lax.axis_size("row")
    count = lax.axis_size("seq")
    pairs = []
    for r in range(rows):
        for s in range(count):
            partner = r ^ (odd_mask if s % 2 else even_mask)
            pairs.append((r * count + s, partner * count + s))
    return lax.ppermute(value, ("row", "seq"), pairs)


def direct(count):
    return count == 8


def gather_blocks(block):
    count = lax.axis_size("seq")
    if not direct(count):
        return [[lax.all_gather(block, "seq", axis=0, tiled=True)]]
    mine = [block]
    for apart in range(1, count // 2):
        mine.append(swap_seq(block, 2 * apart))
    other = []
    for part in mine:
        other.append(swap_seq(part, 1))
    both = [part for pair in zip(mine, other) for part in pair]
    return [both[: count // 2], both[count // 2 :]]


def places(me, count):
    blocks = jnp.arange(count, dtype=jnp.int32)
    if not direct(count):
        return blocks
    return (blocks ^ me) % (count // 2)


def span_of(me, group, groups, blocks):
    size = blocks // groups
    return (me // size ^ group) * size, size


def sum_chips(block):
    count = lax.axis_size("seq")
    height = block.shape[0] // 2
    if not direct(count):
        groups = [list(range(0, count, 2)), list(range(1, count, 2))]
        total = lax.psum(block.astype(f32), "seq", axis_index_groups=groups).astype(bf16)
        return total[:height], total[height:], jnp.zeros((), jnp.int32)
    side = lax.axis_index("seq") // 2 % 2
    kept = lax.dynamic_slice_in_dim(block, side * height, height, 0)
    sent = lax.dynamic_slice_in_dim(block, (1 - side) * height, height, 0)
    part = (kept.astype(f32) + swap_seq(sent, 2).astype(f32)).astype(bf16)
    total = (part.astype(f32) + swap_seq(part, 4).astype(f32)).astype(bf16)
    other = swap_seq(total, 2)
    return total, other, side


def both_cores(halves, core):
    total, other, side = halves
    far_total = swap_seq(total, 1)
    far_other = swap_seq(other, 1)

    def pick(first, second, flag):
        return jnp.where(flag == 0, first, second), jnp.where(flag == 0, second, first)

    mine = jnp.concatenate(pick(total, other, side), axis=0)
    theirs = jnp.concatenate(pick(far_total, far_other, side), axis=0)
    return pick(mine, theirs, core)


def piece_kernel(*refs, count, windows, tokens, stripe):
    place_ref = refs[0]
    inputs = refs[1 : 1 + count]
    send_ref, onward_ref, own_ref = refs[1 + count : 4 + count]
    stripe_refs = refs[4 + count :]
    r, first, second = place_ref[0], place_ref[1], place_ref[2]
    share = own_ref.shape[0]

    def put(index, columns, value):
        apart = index ^ r

        @pl.when((apart == first) | (apart == 3))
        def _():
            slot = jnp.where(apart == 3, share, 0)
            send_ref[pl.ds(pl.multiple_of(slot, share), share), columns] = value.astype(bf16)

        @pl.when(apart == second)
        def _():
            onward_ref[:, columns] = value

        @pl.when(apart == 0)
        def _():
            own_ref[:, columns] = value

    for apart, target in enumerate(stripe_refs):
        begin, width = stripe
        lanes = pl.ds(pl.multiple_of(begin + (r ^ apart) * width, 128), width)
        target[:tokens, :] = inputs[0][:, lanes]
        target[tokens:, :] = inputs[1][:, lanes]
    at_column = 0
    for lefts, rights in windows:
        if rights is None:
            width = inputs[lefts].shape[1]
            for index in range(4):
                rows = slice(index * share, (index + 1) * share)
                put(index, slice(at_column, at_column + width), inputs[lefts][rows, :])
            at_column += width
            continue
        sources, begin, width = lefts
        left = jnp.concatenate([inputs[i][:, begin : begin + width] for i in sources], axis=0)
        sources, begin, width = rights
        for start in range(begin, begin + width, 384):
            right = jnp.concatenate([inputs[i][:, start : start + 384] for i in sources], axis=0)
            grads = token_sum(left, right)
            for index in range(4):
                rows = slice(index * share, (index + 1) * share)
                put(index, slice(at_column, at_column + 384), grads[rows])
            at_column += 384


def piece_call(inputs, windows, columns, share, tokens, stripe=None):
    r = lax.axis_index("row")
    core = lax.axis_index("seq") % 2
    place = jnp.stack([r, jnp.where(core == 0, 1, 2), jnp.where(core == 0, 2, 1)]).astype(jnp.int32)
    shape = jax.ShapeDtypeStruct
    outs = [shape((2 * share, columns), bf16)] + [shape((share, columns), f32)] * 2
    if stripe:
        outs += [shape((2 * tokens, stripe[1]), bf16)] * 4
    vmem = pl.BlockSpec(memory_space=pltpu.VMEM)
    return pl.pallas_call(
        functools.partial(
            piece_kernel, count=len(inputs), windows=windows, tokens=tokens, stripe=stripe
        ),
        in_specs=[pl.BlockSpec(memory_space=pltpu.SMEM)] + [vmem] * len(inputs),
        out_specs=[vmem] * len(outs),
        out_shape=outs,
        name="pieces",
        compiler_params=pltpu.CompilerParams(vmem_limit_bytes=20 << 20),
    )(place, *inputs)


def row_start(piece):
    send, onward, own = piece
    got = swap_row(send, 1, 2)
    height = onward.shape[0]
    return (onward + got[height:].astype(f32)).astype(bf16), own, got[:height]


def row_end(started):
    onward, own, got = [jnp.concatenate(items, axis=1) for items in zip(*started)]
    got_two = swap_row(onward, 2, 1)
    return (own + got.astype(f32) + got_two.astype(f32)).astype(bf16)


def when(condition):
    if isinstance(condition, bool):
        return lambda body: body() if condition else None
    return pl.when(condition)


def fold_pair(value, bit, lanes):
    return jnp.where((lanes >= 64) == (bit == 1), value, jnp.zeros_like(value))


def split_columns(column):
    first = column.astype(bf16).astype(f32)
    second = (column - first).astype(bf16).astype(f32)
    return first, second, column - first - second


def put_columns(array, lanes, at, columns, sign):
    for step, column in enumerate(columns):
        array = jnp.where(lanes == at + step, sign * column, array)
    return array


def vector_sums(upstream, z, lanes):
    ones = jnp.where(lanes == 0, 1.0, 0.0).astype(bf16)
    twos = jnp.where(lanes == 1, 1.0, 0.0).astype(bf16)
    return token_sum((upstream * z).astype(bf16), ones) + token_sum(upstream.astype(bf16), twos)


def project_kernel(*refs, tokens, partner):
    parts = refs[:-9] if partner else refs[:-8]
    gain_ref, shift_ref, weight_hbm, packed_ref, feats_ref = refs[len(parts) : len(parts) + 5]
    pair_ref, normed_ref, weight_ref, sems = refs[-4:]
    width = normed_ref.shape[1]
    copies = []
    for third in range(3):
        columns = pl.ds(third * width, width)
        copies.append(
            pltpu.make_async_copy(weight_hbm.at[:, columns], weight_ref.at[:, columns], sems.at[third])
        )
        copies[-1].start()
    for index, part in enumerate(parts):
        rows = slice(index * tokens, (index + 1) * tokens)
        x = part[:, :width].astype(f32)
        centered = x - jnp.mean(x, axis=1, keepdims=True)
        scale = lax.rsqrt(jnp.mean(centered * centered, axis=1, keepdims=True) + epsilon)
        normed = (centered * scale * gain_ref[...][None, :] + shift_ref[...][None, :]).astype(bf16)
        normed_ref[rows, :] = normed
        feats_ref[rows, :] = part[:, width:]
        if partner and index == 0:
            pair_ref[:tokens, :] = normed
        if partner and index == partner:
            pair_ref[tokens:, :] = normed
    for start in range(0, packed_ref.shape[1], 256):
        columns = slice(start, start + 256)
        if start % width == 0:
            copies[start // width].wait()
        packed_ref[:, columns] = matmul(normed_ref[...], weight_ref[:, columns]).astype(bf16)


def project_call(parts, gain, shift, weight, tokens, partner):
    count = len(parts)
    width, packed = weight.shape
    feat = parts[0].shape[1] - width
    shape = jax.ShapeDtypeStruct
    return pl.pallas_call(
        functools.partial(project_kernel, tokens=tokens, partner=partner),
        out_shape=[
            shape((count * tokens, packed), bf16),
            shape((count * tokens, feat), bf16),
        ]
        + ([shape((2 * tokens, width), bf16)] if partner else []),
        in_specs=[pl.BlockSpec(memory_space=pltpu.VMEM)] * (count + 2) + [pl.BlockSpec(memory_space=pl.ANY)],
        scratch_shapes=[
            pltpu.VMEM((count * tokens, width), bf16),
            pltpu.VMEM(weight.shape, bf16),
            pltpu.SemaphoreType.DMA((3,)),
        ],
        name="project",
        compiler_params=pltpu.CompilerParams(vmem_limit_bytes=16 << 20),
    )(*parts, gain, shift, weight)


def forward_kernel(*refs, tokens, chunk, groups, at, alone):
    place_ref, q_ref = refs[:2]
    k_refs = refs[2 : 2 + groups]
    v_refs = refs[2 + groups : 2 + 2 * groups]
    f_refs = refs[2 + 2 * groups : 2 + 3 * groups]
    own_ref, mine_ref, x_ref, cot_ref, gain_ref, shift_ref = refs[2 + 3 * groups : 8 + 3 * groups]
    out_hbm, up_hbm, down_hbm, result_ref, keep_ref, give_ref = refs[8 + 3 * groups : 14 + 3 * groups]
    middle_ref, send_ref, ownq_ref, ownd_ref, vec_ref = refs[14 + 3 * groups : 19 + 3 * groups]
    bias_ref, mixed_ref, cols_ref, out_w, up_w, down_w, sems = refs[19 + 3 * groups :]
    ones_at, lse_at, delta_at = at
    pairs = q_ref.shape[1] // 128
    length = k_refs[0].shape[0]
    chunks = length // chunk
    step, last = (0, 0) if alone else (pl.program_id(0), pl.num_programs(0) - 1)
    me = place_ref[0]
    core = me % 2
    feat = own_ref.shape[2]
    lanes = lax.broadcasted_iota(jnp.int32, (tokens, 128), 1)
    feat_lanes = lax.broadcasted_iota(jnp.int32, (tokens, feat), 1)
    copies = [
        pltpu.make_async_copy(out_hbm, out_w, sems.at[0]),
        pltpu.make_async_copy(up_hbm, up_w, sems.at[1]),
        pltpu.make_async_copy(down_hbm, down_w, sems.at[2]),
    ]

    @when(step == 0)
    def _():
        for copy in copies:
            copy.start()
        cols_ref[...] = mine_ref[...].astype(f32)
        row = lax.broadcasted_iota(jnp.int32, (tokens, tokens), 0)
        col = lax.broadcasted_iota(jnp.int32, (tokens, tokens), 1)
        blocks = groups * length // tokens
        for group in range(groups):
            begin, size = span_of(me, group, groups, blocks)
            for step_in in range(size):
                block = begin + step_in
                allowed = (block < me) | ((block == me) & (col <= row))
                place = pl.multiple_of(group * length + place_ref[1 + block] * tokens, tokens)
                bias_ref[:, pl.ds(place, tokens)] = jnp.where(allowed, 0.0, negative)

    for pair in range(pairs):
        span = slice(pair * 128, pair * 128 + 128)
        q_pair = q_ref[:, span] * jnp.asarray(0.125, bf16)
        outs = []
        for bit in range(2):
            left = jnp.concatenate([fold_pair(q_pair, bit, lanes), own_ref[pair * 2 + bit]], axis=1)

            def one(c, carry, left=left):
                top, total, acc = carry
                begin = c * chunk if isinstance(c, int) else pl.multiple_of(c * chunk, chunk)
                rows = pl.ds(begin, chunk)
                scores = []
                for group in range(groups):
                    right = jnp.concatenate([k_refs[group][rows, span], f_refs[group][rows, :]], axis=1)
                    shifted = pl.ds(group * length + begin, chunk)
                    scores.append(matmul_t(left, right) + bias_ref[:, shifted])
                tops = [jnp.max(s, axis=1, keepdims=True) for s in scores]
                new_top = functools.reduce(jnp.maximum, tops if top is None else [top] + tops)
                new_total = 0.0
                new_acc = 0.0
                for group, s in enumerate(scores):
                    p = jnp.exp(s - new_top)
                    new_total = new_total + jnp.sum(p, axis=1, keepdims=True)
                    new_acc = new_acc + matmul(p.astype(bf16), v_refs[group][rows, span])
                if top is not None:
                    scale = jnp.exp(top - new_top)
                    new_total = new_total + scale * total
                    new_acc = new_acc + scale * acc
                return new_top, new_total, new_acc

            if chunks == 1:
                top, total, acc = one(0, (None, None, None))
            else:
                start = (
                    jnp.full((tokens, 1), 4 * negative, f32),
                    jnp.zeros((tokens, 1), f32),
                    jnp.zeros((tokens, 128), f32),
                )
                top, total, acc = lax.fori_loop(0, chunks, one, start)
            outs.append(acc / total)
            head = step * pairs * 2 + pair * 2 + bit
            columns = split_columns(top + jnp.log(total))
            cols_ref[...] = put_columns(cols_ref[...], feat_lanes, lse_at + 3 * head, columns, 1.0)
            ownq_ref[pair * 2 + bit] = put_columns(
                own_ref[pair * 2 + bit].astype(f32), feat_lanes, ones_at, columns, -1.0
            ).astype(bf16)
        where = span
        if pairs * 128 < mixed_ref.shape[1]:
            where = pl.ds(pl.multiple_of(step * (pairs * 128) + pair * 128, 128), 128)
        mixed_ref[:, where] = jnp.where(lanes < 64, outs[0], outs[1])

    @when(step == last)
    def _():
        width = mixed_ref.shape[1]
        half = width // 2
        pieces = up_w.shape[1] // width
        up_half = up_w.shape[1] // 2
        cot = cot_ref[...]
        attended = mixed_ref[...].astype(bf16)
        copies[0].wait()
        middle = x_ref[...].astype(f32) + matmul(attended, out_w[...])
        centered = middle - jnp.mean(middle, axis=1, keepdims=True)
        scale = lax.rsqrt(jnp.mean(centered * centered, axis=1, keepdims=True) + epsilon)
        z = centered * scale
        normed = (z * gain_ref[...][None, :] + shift_ref[...][None, :]).astype(bf16)
        dU_at, att_at = width, width + up_half
        dB_at, hid_at = att_at + width, att_at + width + half
        cot_at = hid_at + up_half
        for ref in (keep_ref, give_ref):
            ref[:, :width] = normed
            ref[:, att_at : att_at + width] = attended
            ref[:, cot_at : cot_at + width] = cot
        copies[1].wait()
        copies[2].wait()
        y = middle
        grad_normed = jnp.zeros_like(middle)
        for c in range(pieces):
            cut = slice(c * width, (c + 1) * width)
            u = matmul(normed, up_w[:, cut])
            cdf = 0.5 + 0.5 * lax.erf(u * (0.5**0.5))
            hidden = (u * cdf).astype(bf16)
            slope = cdf + u * (jnp.exp(-0.5 * u * u) * 0.3989422804014327)
            grad_u = (matmul_t(cot, down_w[cut, :]) * slope).astype(bf16)
            y = y + matmul(hidden, down_w[cut, :])
            grad_normed = grad_normed + matmul_t(grad_u, up_w[:, cut])
            inner = slice(dU_at + (c % (pieces // 2)) * width, dU_at + (c % (pieces // 2) + 1) * width)
            stripe = slice(hid_at + c * half, hid_at + (c + 1) * half)

            @pl.when(core == c // (pieces // 2))
            def _(grad_u=grad_u, inner=inner):
                keep_ref[:, inner] = grad_u

            @pl.when(core != c // (pieces // 2))
            def _(grad_u=grad_u, inner=inner):
                give_ref[:, inner] = grad_u

            @pl.when(core == 0)
            def _(hidden=hidden, stripe=stripe):
                keep_ref[:, stripe] = hidden[:, :half]
                give_ref[:, stripe] = hidden[:, half:]

            @pl.when(core == 1)
            def _(hidden=hidden, stripe=stripe):
                keep_ref[:, stripe] = hidden[:, half:]
                give_ref[:, stripe] = hidden[:, :half]

        result_ref[...] = y.astype(bf16)
        vec_ref[...] = vector_sums(grad_normed, z, lanes)
        t = grad_normed * gain_ref[...][None, :]
        t_z = jnp.mean(t * z, axis=1, keepdims=True)
        grad_middle = cot.astype(f32) + scale * (t - jnp.mean(t, axis=1, keepdims=True) - z * t_z)
        middle_ref[...] = grad_middle
        branch = grad_middle.astype(bf16)
        grad_mixed = matmul_t(branch, out_w[...]).astype(bf16)
        send_ref[:, :width] = grad_mixed

        @pl.when(core == 0)
        def _():
            keep_ref[:, dB_at : dB_at + half] = branch[:, :half]
            give_ref[:, dB_at : dB_at + half] = branch[:, half:]

        @pl.when(core == 1)
        def _():
            keep_ref[:, dB_at : dB_at + half] = branch[:, half:]
            give_ref[:, dB_at : dB_at + half] = branch[:, :half]

        columns_all = cols_ref[...]
        for pair in range(width // 128):
            span = slice(pair * 128, pair * 128 + 128)
            product = grad_mixed[:, span].astype(f32) * mixed_ref[:, span]
            for bit in range(2):
                head = pair * 2 + bit
                delta = jnp.sum(fold_pair(product, bit, lanes), axis=1, keepdims=True)
                columns = split_columns(delta)
                columns_all = put_columns(columns_all, feat_lanes, delta_at + 3 * head, columns, 1.0)
                ownd_ref[head] = put_columns(
                    jnp.zeros((tokens, feat), f32), feat_lanes, ones_at, columns, -1.0
                ).astype(bf16)
        send_ref[:, width:] = columns_all.astype(bf16)


def stack_left(target, pair, value, bit, lanes, features):
    tokens = value.shape[0]
    target[pair, bit * tokens : (bit + 1) * tokens, :] = jnp.concatenate(
        [fold_pair(value, bit, lanes), features], axis=1
    )


def own_first(place_ref, me):
    return (place_ref[1 + me] < place_ref[1 + (me ^ 1)]).astype(jnp.int32)


def pair_rows(place_ref, j, tokens):
    first = jnp.minimum(place_ref[1 + 2 * j], place_ref[2 + 2 * j])
    return pl.ds(pl.multiple_of(first * tokens, 2 * tokens), 2 * tokens)


def pair_mask(tokens, me, swapped, first_own):
    shape = (2 * tokens, 2 * tokens)
    row = lax.broadcasted_iota(jnp.int32, shape, 0) % tokens
    col = lax.broadcasted_iota(jnp.int32, shape, 1)
    own_block = (col < tokens) == (first_own == 1)
    col = col % tokens
    if swapped:
        inside, beyond = row <= col, me % 2 == 0
    else:
        inside, beyond = col <= row, me % 2 == 1
    allowed = (own_block & inside) | (jnp.logical_not(own_block) & beyond)
    return jnp.where(allowed, 0.0, negative)


def query_kernel(*refs, tokens, groups, alone):
    place_ref, q_own, d_own, own_q, own_d = refs[:5]
    k_refs = refs[5 : 5 + groups]
    v_refs = refs[5 + groups : 5 + 2 * groups]
    f_refs = refs[5 + 2 * groups : 5 + 3 * groups]
    dq_ref, left_a, left_b, acc_q = refs[5 + 3 * groups :]
    pairs = q_own.shape[1] // 128
    blocks = groups * k_refs[0].shape[0] // tokens
    me = place_ref[0]
    lanes = lax.broadcasted_iota(jnp.int32, (tokens, 128), 1)
    low = lanes < 64
    for pair in range(pairs):
        span = slice(pair * 128, pair * 128 + 128)
        for bit in range(2):
            head = pair * 2 + bit
            stack_left(left_a, pair, q_own[:, span] * jnp.asarray(0.125, bf16), bit, lanes, own_q[head])
            stack_left(left_b, pair, d_own[:, span], bit, lanes, own_d[head])
    acc_q[...] = jnp.zeros_like(acc_q)
    later = pair_mask(tokens, me, False, own_first(place_ref, me))
    for group in range(groups):
        k_all, v_all, feat_k = k_refs[group], v_refs[group], f_refs[group]

        def query_step(j, _, k_all=k_all, v_all=v_all, feat_k=feat_k):
            rows = pair_rows(place_ref, j, tokens)
            at_diag = (j == me // 2).astype(f32)
            feats = feat_k[rows, :]
            for pair in range(pairs):
                span = slice(pair * 128, pair * 128 + 128)
                k_blk = k_all[rows, span]
                s = matmul_t(left_a[pair], jnp.concatenate([k_blk, feats], axis=1))
                dp = matmul_t(left_b[pair], jnp.concatenate([v_all[rows, span], feats], axis=1))
                ds = (jnp.exp(s + later * at_diag) * dp).astype(bf16)
                both = matmul(ds, k_blk)
                acc_q[:, span] += jnp.where(low, both[:tokens], both[tokens:])
            return 0

        begin, size = span_of(me, group, groups, blocks)
        end = jnp.minimum(begin + size, me // 2 * 2 + 2)
        lax.fori_loop(begin // 2, end // 2, query_step, 0)
    dq_ref[...] = (acc_q[...] * 0.125).astype(bf16)


def key_kernel(*refs, tokens, at, parts, group, groups, alone):
    final = group == groups - 1
    place_ref, k_own, v_own, q_all, own_base = refs[:5]
    given = refs[5 : 5 + parts]
    refs = refs[5 + parts :]
    if group > 0:
        k_before, v_before = refs[:2]
        refs = refs[2:]
    if final:
        wkv_hbm, start_ref, x_ref, gain_ref, middle_ref = refs[:5]
        keep_ref, give_ref, grad_ref, vec_ref = refs[5:9]
        acc_k, acc_v, wkv, sem, left_c, left_d = refs[9:15]
        refs = refs[15:]
    else:
        acc_k, acc_v, left_c, left_d = refs[:4]
        refs = refs[4:]
    _, lse_at, delta_at = at
    pairs = k_own.shape[1] // 128
    blocks = groups * q_all.shape[0] // tokens
    feat = own_base.shape[2]
    width = acc_k.shape[1]
    step, last = (0, 0) if alone else (pl.program_id(0), pl.num_programs(0) - 1)
    me = place_ref[0]
    core = me % 2
    lanes = lax.broadcasted_iota(jnp.int32, (tokens, 128), 1)
    feat_lanes = lax.broadcasted_iota(jnp.int32, (tokens, feat), 1)
    low = lanes < 64
    if final:
        copy = pltpu.make_async_copy(wkv_hbm.at[:, pl.ds(width, 2 * width)], wkv, sem)

        @when(step == 0)
        def _():
            copy.start()

    if parts == 2:
        d_all, feat_q = given
    else:
        d_all, feat_q = refs
        for index, part in enumerate(given):
            rows = slice(index * tokens, (index + 1) * tokens)
            d_all[rows, :] = part[:, :width]
            feat_q[rows, :] = part[:, width:]
    for pair in range(pairs):
        span = slice(pair * 128, pair * 128 + 128)
        for bit in range(2):
            head = pair * 2 + bit
            number = step * pairs * 2 + head
            minus = (jnp.full((tokens, 1), -1.0, f32),) * 3
            k_feats = put_columns(
                own_base[head].astype(f32), feat_lanes, lse_at + 3 * number, minus, 1.0
            ).astype(bf16)
            v_feats = put_columns(
                jnp.zeros((tokens, feat), f32), feat_lanes, delta_at + 3 * number, minus, 1.0
            ).astype(bf16)
            stack_left(left_c, pair, k_own[:, span] * jnp.asarray(0.125, bf16), bit, lanes, k_feats)
            stack_left(left_d, pair, v_own[:, span], bit, lanes, v_feats)

    def where(pair):
        if pairs * 128 == width:
            return slice(pair * 128, pair * 128 + 128)
        return pl.ds(pl.multiple_of(step * (pairs * 128) + pair * 128, 128), 128)

    for pair in range(pairs):
        if group > 0:
            acc_k[:, where(pair)] = k_before[:, where(pair)]
            acc_v[:, where(pair)] = v_before[:, where(pair)]
        else:
            acc_k[:, where(pair)] = jnp.zeros((tokens, 128), f32)
            acc_v[:, where(pair)] = jnp.zeros((tokens, 128), f32)
    later = pair_mask(tokens, me, True, own_first(place_ref, me))

    def key_step(j, _):
        rows = pair_rows(place_ref, j, tokens)
        at_diag = (j == me // 2).astype(f32)
        feats = feat_q[rows, :]
        for pair in range(pairs):
            span = slice(pair * 128, pair * 128 + 128)
            q_blk = q_all[rows, span]
            d_blk = d_all[rows, span]
            s = matmul_t(left_c[pair], jnp.concatenate([q_blk, feats], axis=1))
            dp = matmul_t(left_d[pair], jnp.concatenate([d_blk, feats], axis=1))
            w = jnp.exp(s + later * at_diag)
            both = matmul((w * dp).astype(bf16), q_blk)
            acc_k[:, where(pair)] += jnp.where(low, both[:tokens], both[tokens:])
            both = matmul(w.astype(bf16), d_blk)
            acc_v[:, where(pair)] += jnp.where(low, both[:tokens], both[tokens:])
        return 0

    begin, size = span_of(me, group, groups, blocks)
    lax.fori_loop(jnp.maximum(begin // 2, me // 2), (begin + size) // 2, key_step, 0)
    if not final:
        return

    @when(step == last)
    def _():
        d_k = (acc_k[...] * 0.125).astype(bf16)
        d_v = acc_v[...].astype(bf16)

        @pl.when(core == 0)
        def _():
            keep_ref[...] = d_k
            give_ref[...] = d_v

        @pl.when(core == 1)
        def _():
            keep_ref[...] = d_v
            give_ref[...] = d_k

        copy.wait()
        upstream = start_ref[...] + matmul_t(d_k, wkv[:, :width]) + matmul_t(d_v, wkv[:, width:])
        x = x_ref[...].astype(f32)
        centered = x - jnp.mean(x, axis=1, keepdims=True)
        scale = lax.rsqrt(jnp.mean(centered * centered, axis=1, keepdims=True) + epsilon)
        z = centered * scale
        vec_ref[...] = vector_sums(upstream, z, lanes)
        t = upstream * gain_ref[...][None, :]
        t_z = jnp.mean(t * z, axis=1, keepdims=True)
        grad = middle_ref[...] + scale * (t - jnp.mean(t, axis=1, keepdims=True) - z * t_z)
        grad_ref[...] = grad.astype(bf16)


class Plan:
    def __init__(self, tokens, length, width, feat, group):
        self.tokens, self.length, self.width, self.feat = tokens, length, width, feat
        self.lanes = 128 * group
        self.heads = 2 * group
        self.steps = width // self.lanes
        self.alone = self.steps == 1

    def own(self, third):
        block = (self.tokens, self.lanes)
        return block, lambda i, place: (place[1 + place[0]], third * self.steps + i), third * self.width

    def part(self):
        return (self.tokens, self.lanes), lambda i, place: (0, i), 0

    def all(self, third):
        block = (self.length, self.lanes)
        return block, lambda i, place: (0, third * self.steps + i), third * self.width

    def head(self):
        return (self.heads, self.tokens, self.feat), lambda i, place: (i, 0, 0), None

    def features(self):
        return (self.length, self.feat), lambda i, place: (0, 0), 0

    def own_features(self):
        return (self.tokens, self.feat), lambda i, place: (place[1 + place[0]], 0), 0

    def call(self, kernel, ins, outs, shapes, scratch, room):
        if not self.alone:
            kernel = functools.partial(kernel, alone=False)

            def spec(item):
                return pl.BlockSpec(item[0], item[1]) if isinstance(item, tuple) else item

            return pl.pallas_call(
                kernel,
                grid_spec=pltpu.PrefetchScalarGridSpec(
                    num_scalar_prefetch=1,
                    grid=(self.steps,),
                    in_specs=[spec(item) for item in ins],
                    out_specs=[spec(item) for item in outs],
                    scratch_shapes=scratch,
                ),
                out_shape=shapes,
            )

        vmem = pl.BlockSpec(memory_space=pltpu.VMEM)

        def run(place, *arrays):
            distinct, numbers, specs = [], [], []
            for item, array in zip(ins, arrays):
                same = [n for n, other in enumerate(distinct) if other is array]
                if not same:
                    same = [len(distinct)]
                    distinct.append(array)
                    specs.append(vmem if isinstance(item, tuple) else item)
                numbers.append(same[0])

            def body(place_ref, *refs):
                views = [place_ref]
                for item, number in zip(ins, numbers):
                    ref = refs[number]
                    if isinstance(item, tuple) and item[2] is not None:
                        block, _, begin = item
                        ref = ref.at[: block[0], begin : begin + block[1]]
                    views.append(ref)
                kernel(*views, *refs[len(distinct) :], alone=True)

            return pl.pallas_call(
                body,
                in_specs=[pl.BlockSpec(memory_space=pltpu.SMEM)] + specs,
                out_specs=[vmem] * len(outs),
                out_shape=shapes,
                scratch_shapes=scratch,
                compiler_params=pltpu.CompilerParams(vmem_limit_bytes=room << 20),
            )(place, *distinct)

        return run


def whole_spec(*shape):
    return shape, lambda i, place: (0,) * len(shape), None


def forward_call(plan, at, place, packed, own_base, feats, x, cot, gain, shift, weights):
    tokens, width, feat, groups = plan.tokens, plan.width, plan.feat, len(packed)
    out_weight, up_weight, down_weight = weights
    hidden = up_weight.shape[1]
    kept = 3 * width + width // 2 + hidden
    heads = plan.steps * plan.heads
    anywhere = pl.BlockSpec(memory_space=pl.ANY)
    shape = jax.ShapeDtypeStruct
    call = plan.call(
        functools.partial(
            forward_kernel, tokens=tokens, chunk=min(plan.length, 1024), groups=groups, at=at
        ),
        [plan.own(0)]
        + [plan.all(1)] * groups
        + [plan.all(2)] * groups
        + [plan.features()] * groups
        + [plan.head(), plan.own_features()]
        + [whole_spec(tokens, width)] * 2
        + [whole_spec(width)] * 2
        + [anywhere] * 3,
        [
            whole_spec(tokens, width),
            whole_spec(tokens, kept),
            whole_spec(tokens, kept),
            whole_spec(tokens, width),
            whole_spec(tokens, width + feat),
            plan.head(),
            whole_spec(heads, tokens, feat),
            whole_spec(width, 128),
        ],
        [
            shape((tokens, width), bf16),
            shape((tokens, kept), bf16),
            shape((tokens, kept), bf16),
            shape((tokens, width), f32),
            shape((tokens, width + feat), bf16),
            shape((heads, tokens, feat), bf16),
            shape((heads, tokens, feat), bf16),
            shape((width, 128), f32),
        ],
        [
            pltpu.VMEM((tokens, groups * plan.length), f32),
            pltpu.VMEM((tokens, width), f32),
            pltpu.VMEM((tokens, feat), f32),
            pltpu.VMEM(out_weight.shape, bf16),
            pltpu.VMEM(up_weight.shape, bf16),
            pltpu.VMEM(down_weight.shape, bf16),
            pltpu.SemaphoreType.DMA((3,)),
        ],
        30,
    )
    return call(
        place,
        packed[0],
        *packed,
        *packed,
        *feats,
        own_base,
        feats[0],
        x,
        cot,
        gain,
        shift,
        *weights,
    )


def query_call(plan, place, packed, sent, own_q, own_d, feats):
    tokens, lanes, full, groups = plan.tokens, plan.lanes, 128 + plan.feat, len(packed)
    group = plan.heads // 2
    call = plan.call(
        functools.partial(query_kernel, tokens=tokens, groups=groups),
        [plan.own(0), plan.part(), plan.head(), plan.head()]
        + [plan.all(1)] * groups
        + [plan.all(2)] * groups
        + [plan.features()] * groups,
        [plan.part()],
        [jax.ShapeDtypeStruct((tokens, plan.width), bf16)],
        [pltpu.VMEM((group, 2 * tokens, full), bf16)] * 2 + [pltpu.VMEM((tokens, lanes), f32)],
        14,
    )
    return call(place, packed[0], sent, own_q, own_d, *packed, *packed, *feats)[0]


def key_call(plan, at, place, packed, parts, own_base, group, groups, before, closing):
    tokens, width, full = plan.tokens, plan.width, 128 + plan.feat
    pairs = plan.heads // 2
    final = group == groups - 1
    shape = jax.ShapeDtypeStruct
    flat = whole_spec(tokens, width)
    left = [pltpu.VMEM((pairs, 2 * tokens, full), bf16)] * 2
    if len(parts) == 1:
        column = width // plan.feat
        features = ((plan.length, plan.feat), lambda i, place: (0, column), width)
        given, specs, more = parts * 2, [plan.all(0), features], []
    else:
        given, specs = parts, [whole_spec(tokens, width + plan.feat)] * len(parts)
        more = [pltpu.VMEM((plan.length, width), bf16), pltpu.VMEM((plan.length, plan.feat), bf16)]
    specs += [flat] * len(before)
    if final:
        specs += [pl.BlockSpec(memory_space=pl.ANY), flat, flat, whole_spec(width), flat]
        outs = [flat] * 3 + [whole_spec(width, 128)]
        shapes = [shape((tokens, width), bf16)] * 3 + [shape((width, 128), f32)]
        scratch = [pltpu.VMEM((tokens, width), f32)] * 2
        scratch += [pltpu.VMEM((width, 2 * width), bf16), pltpu.SemaphoreType.DMA]
    else:
        outs = [flat] * 2
        shapes = [shape((tokens, width), f32)] * 2
        scratch = []
    call = plan.call(
        functools.partial(
            key_kernel, tokens=tokens, at=at, parts=len(given), group=group, groups=groups
        ),
        [plan.own(1), plan.own(2), plan.all(0), plan.head()] + specs,
        outs,
        shapes,
        scratch + left + more,
        20,
    )
    return call(place, packed[0], packed[0], packed[group], own_base, *given, *before, *closing)


def log_counts(offsets, positions, spans, parts):
    heads = offsets.shape[1]
    finest = spans[0]
    classes = jnp.arange(period, dtype=jnp.int32)
    part_start = jnp.arange(parts, dtype=jnp.int32) * finest
    total = jnp.zeros((heads, positions.shape[0], parts, period), f32)
    for index, dilation in enumerate(dilations):
        offset = offsets[index][:, None]
        own_in = jnp.mod(positions[None, :] - offset, dilation) == 0
        key_in = jnp.mod(classes[None, :] - offset, dilation) == 0
        same = positions[:, None] // spans[index] == part_start[None, :] // spans[index]
        both = own_in[:, :, None, None] & key_in[:, None, None, :] & same[None, :, :, None]
        total = total + both.astype(f32)
    logs = jnp.where(total > 0, jnp.log(jnp.maximum(total, 1.0)), negative)
    logs = logs.reshape(heads, positions.shape[0], parts * period)
    high = lax.reduce_precision(logs, 8, 7)
    return high.astype(bf16), (logs - high).astype(bf16)


def shards(
    inputs,
    documents,
    offsets,
    ln1_gain,
    ln1_bias,
    qkv_weight,
    out_weight,
    ln2_gain,
    ln2_bias,
    up_weight,
    down_weight,
    cotangent,
):
    tokens = inputs.shape[1]
    width = inputs.shape[2]
    heads = offsets.shape[1]
    hidden_width = up_weight.shape[1]
    rows = lax.axis_size("row")
    share = width // rows
    count = lax.axis_size("seq")
    me = lax.axis_index("seq")
    core = me % 2
    row_len = tokens * count
    place = jnp.concatenate([me[None], places(me, count)]).astype(jnp.int32)
    spans = [min(reach, row_len) for reach in reaches]
    parts = row_len // spans[0]

    pos_own = me * tokens + jnp.arange(tokens, dtype=jnp.int32)
    docs_own = documents[0]
    ones_at = 2 * parts * period + doc_count
    lse_at = ones_at + 3
    delta_at = lse_at + 3 * heads
    used = delta_at + 3 * heads
    feat = -(-used // 128) * 128
    at = (ones_at, lse_at, delta_at)
    x_low = inputs[0]
    key_class = ((pos_own // spans[0]) * period + pos_own % period)[:, None]
    column = jnp.arange(feat, dtype=jnp.int32)[None, :]
    in_class = (column == key_class) | (column == key_class + parts * period)
    in_doc = column == docs_own[:, None] + 2 * parts * period
    hot = in_class | in_doc | ((column >= ones_at) & (column < lse_at))
    sent_first = jnp.concatenate([x_low, hot.astype(bf16)], axis=1)
    gathered = gather_blocks(sent_first)
    same_doc = docs_own[:, None] == jnp.arange(doc_count)[None, :]
    high, low = log_counts(offsets, pos_own, spans, parts)
    doc_part = jnp.where(same_doc, 0.0, negative).astype(bf16)
    doc_part = jnp.broadcast_to(doc_part[None], (heads, tokens, doc_count))
    own_base = jnp.concatenate(
        [high, low, doc_part, jnp.zeros((heads, tokens, feat - ones_at), bf16)], axis=2
    )

    cot = cotangent[0]
    cot_mine = [cot]
    for apart in range(1, rows):
        cot_mine.append(swap_row(cot, apart, apart))
    cot_other = swap_seq(jnp.concatenate(cot_mine, axis=0), 1)
    cot_all = jnp.concatenate(
        [
            part
            for apart, mine in enumerate(cot_mine)
            for part in (mine, cot_other[apart * tokens : (apart + 1) * tokens])
        ],
        axis=0,
    )

    if direct(count):
        packed_near, feats_near, normed_pair = project_call(
            gathered[0], ln1_gain, ln1_bias, qkv_weight, tokens, 1
        )
        packed_far, feats_far = project_call(gathered[1], ln1_gain, ln1_bias, qkv_weight, tokens, 0)
        packed, feats = [packed_near, packed_far], [feats_near, feats_far]
    else:
        ((joined,),) = gathered
        normed_all = layer_norm(joined[:, :width].astype(f32), ln1_gain, ln1_bias).astype(bf16)
        packed = [matmul(normed_all, qkv_weight).astype(bf16)]
        feats = [joined[:, width:]]
        normed_low = lax.dynamic_slice_in_dim(normed_all, me * tokens, tokens, 0)
        normed_pair = jnp.concatenate([normed_low, swap_seq(normed_low, 1)], axis=0)
    groups = len(packed)
    plan = Plan(tokens, row_len // groups, width, feat, width // 128 if row_len <= 1024 else 1)
    result, kept, given, grad_middle, sent, own_q, own_d, ln2_vectors = forward_call(
        plan,
        at,
        place,
        packed,
        own_base,
        feats,
        x_low,
        cot,
        ln2_gain,
        ln2_bias,
        (out_weight, up_weight, down_weight),
    )
    gathered_back = gather_blocks(sent)

    half = width // 2
    folds = hidden_width // 2 // width
    got = swap_seq(given, 1)
    up_half = hidden_width // 2
    attended_at = width + up_half
    branch_at = attended_at + width
    hidden_at = branch_at + half
    up_columns = up_half + half + 128
    pieces = piece_call(
        [kept, got, ln2_vectors],
        (
            (((0, 1), 0, width), ((0, 1), width, up_half)),
            (((0, 1), attended_at, width), ((0, 1), branch_at, half)),
            (2, None),
        ),
        up_columns,
        share,
        tokens,
        (hidden_at, half),
    )
    up_piece, stripes = pieces[:3], list(pieces[3:])
    for apart in range(1, rows):
        stripes[apart] = swap_row(stripes[apart], apart, apart)
    down = token_sum(jnp.concatenate(stripes, axis=0), cot_all)
    down = jnp.concatenate([down[i * share : (i + 1) * share] for i in range(folds)], axis=1)
    down_total = both_cores(sum_chips(down.astype(bf16)), core)

    up_started = row_start(up_piece)

    d_q = query_call(plan, place, packed, sent, own_q, own_d, feats)
    q_mine = lax.dynamic_slice_in_dim(d_q, core * half, half, 1)
    q_theirs = lax.dynamic_slice_in_dim(d_q, (1 - core) * half, half, 1)
    q_got = swap_seq(q_theirs, 1)
    start = matmul_t(d_q, qkv_weight[:, :width])
    query_piece = piece_call(
        [q_mine, q_got, normed_pair],
        ((((2,), 0, width), ((0, 1), 0, half)),),
        half,
        share,
        tokens,
    )
    query_started = row_start(query_piece)
    up_total = both_cores(sum_chips(row_end([up_started, query_started])), core)

    before = ()
    for group in range(groups):
        closing = ()
        if group == groups - 1:
            closing = (qkv_weight, start, x_low, ln1_gain, grad_middle)
        before = key_call(
            plan,
            at,
            place,
            packed,
            gathered_back[group],
            own_base,
            group,
            groups,
            tuple(before),
            closing,
        )
    kv_mine, kv_theirs, grad_inputs, ln1_vectors = before
    kv_got = swap_seq(kv_theirs, 1)
    kv_piece = piece_call(
        [kv_mine, kv_got, normed_pair, ln1_vectors],
        ((((2,), 0, width), ((0, 1), 0, width)), (3, None)),
        width + 128,
        share,
        tokens,
    )
    kv_total = both_cores(sum_chips(row_end([row_start(kv_piece)])), core)

    def columns(pair, begin, end):
        return jnp.concatenate([part[:, begin:end] for part in pair], axis=1).astype(f32)

    def vector(pair, at_column):
        first, second = [part[:, at_column : at_column + 2].astype(f32) for part in pair]
        return first + second

    grad_down = jnp.concatenate(
        [part[:, i * width : (i + 1) * width] for part in down_total for i in range(folds)], axis=0
    ).astype(f32)
    up_end = hidden_width // 2
    out_end = up_end + half
    vec_end = out_end + 128
    grad_up = columns(up_total, 0, up_end)
    grad_out = columns(up_total, up_end, out_end)
    ln2 = vector(up_total, out_end)
    grad_qkv = jnp.concatenate(
        [columns(up_total, vec_end, vec_end + half), columns(kv_total, 0, width)], axis=1
    )
    ln1 = vector(kv_total, width)
    return (
        result[None],
        grad_inputs[None],
        ln1[:, 0],
        ln1[:, 1],
        grad_qkv,
        grad_out,
        ln2[:, 0],
        ln2[:, 1],
        grad_up,
        grad_down,
    )


def solution(mesh):
    placed = (
        P("row", "seq", None),
        P("row", "seq"),
        P(),
        P(),
        P(),
        P(),
        P(),
        P(),
        P(),
        P(),
        P(),
        P("row", "seq", None),
    )

    return jax.shard_map(
        shards,
        mesh=mesh,
        in_specs=placed,
        out_specs=(
            P("row", "seq", None),
            P("row", "seq", None),
            P("row"),
            P("row"),
            P("row", None),
            P("row", None),
            P("row"),
            P("row"),
            P("row", None),
            P("row", None),
        ),
        check_vma=False,
    )
```

time: 310 us -> 226 us (0.73)
  the two profiles are of different devices: /device:TPU:15 before, /device:TPU:0 now
where the time goes in v2:
time: 226 us
  waiting for transfers between devices  119 us (53%)
  Pallas kernels  42.9 us (19%)
  starting transfers between devices  34.6 us (15%)
  other arithmetic  14.6 us (6%)
  local copies, waits for them, and re-layouts  11.7 us (5%)
    ppermute x33, waiting for transfers between devices, swap_seq(): return lax.ppermute(value, 'seq', [(s, s ^ mask) for s in range(count)])  103 us
    pallas_call x4, Pallas kernels, run(): pl.pallas_call(body, in_specs=[pl.BlockSpec(memory_space=pltpu.SMEM)] + s...  27.2 us
    ppermute x33, starting transfers between devices, swap_seq(): return lax.ppermute(value, 'seq', [(s, s ^ mask) for s in range(count)])  21.4 us
    ppermute x11, waiting for transfers between devices, swap_row(): return lax.ppermute(value, ('row', 'seq'), pairs)  16.5 us
    ppermute x11, starting transfers between devices, swap_row(): return lax.ppermute(value, ('row', 'seq'), pairs)  13.2 us
    pallas_call x2, Pallas kernels, project_call(): pl.pallas_call(functools.partial(project_kernel, tokens=tokens, partner=p...  9.78 us
    unnamed x45, local copies, waits for them, and re-layouts  7.72 us
    pallas_call x3, Pallas kernels, piece_call(): pl.pallas_call(functools.partial(piece_kernel, count=len(inputs), windows...  5.95 us
  transfers between devices with their start and end apart: 44, of which 21 were waited for; matrix products, arithmetic and copies ran while one was open for 7% of the time, Pallas kernels for 19%

profile of v2, /device:TPU:0, one launch (start us, length us, event | category | flops | bytes accessed | tf_op | source)
XLA Modules:
  0.0 225.8 jit_solution(12104039879298451006)
XLA Ops:
  0.7 0.7 broadcast_add_fusion
  1.5 1.7 pad_maximum_fusion.8.refs_0_
  3.2 3.1 %collective-permute-start.1 = (bf16[128,896]{1,0:T(8,128)(2,1)}, bf16[128,896]{1,0:T(8,128)(2,1)}, u32[]{:S(2)}, u32[]{:S(2)}) collective-permute-start(bf16[128,896]{1,0:T(8,128)(2,1)} %pad_maximum_fusion.8.refs_0_), channel_id=1, source_target_pairs={{0,2},{1,3},{2,0},{3,1},{4,6},{5,7},{6,4},{7,5},{8,10},{9,11},{10,... | collective-permute-start | bytes 688136 | tf_op jit(solution)/shard_map/ppermute | solution.py:41
  6.2 2.6 %collective-permute-start.3 = (bf16[128,896]{1,0:T(8,128)(2,1)}, bf16[128,896]{1,0:T(8,128)(2,1)}, u32[]{:S(2)}, u32[]{:S(2)}) collective-permute-start(bf16[128,896]{1,0:T(8,128)(2,1)} %pad_maximum_fusion.8.refs_0_), channel_id=1, source_target_pairs={{0,4},{1,5},{2,6},{3,7},{4,0},{5,1},{6,2},{7,3},{8,12},{9,13},{10,... | collective-permute-start | bytes 688136 | tf_op jit(solution)/shard_map/ppermute | solution.py:41
  8.8 2.7 %collective-permute-start.37 = (bf16[128,768]{1,0:T(8,128)(2,1)}, bf16[128,768]{1,0:T(8,128)(2,1)S(1)}, u32[]{:S(2)}, u32[]{:S(2)}) collective-permute-start(bf16[128,768]{1,0:T(8,128)(2,1)} %bitcast.21), channel_id=1, source_target_pairs={{0,24},{1,25},{2,26},{3,27},{4,28},{5,29},{6,30},{7,31},{8,16},{9,... | collective-permute-start | bytes 589832 | tf_op jit(solution)/shard_map/ppermute | solution.py:52
  12.0 0.8 slice_bitcast_fusion.3
  13.2 1.1 reduce-precision_convert_fusion
  14.3 0.7 select_convert_fusion
  15.0 1.1 collective-permute-done.37
  16.1 1.5 collective-permute-start.35
  17.7 1.1 maximum_maximum_fusion.refs_4_.refs_1_.refs_2_
  18.8 1.4 collective-permute-done.36
  20.7 5.0 %collective-permute-done.3.refs_0_ = bf16[128,896]{1,0:T(8,128)(2,1)} collective-permute-done((bf16[128,896]{1,0:T(8,128)(2,1)}, bf16[128,896]{1,0:T(8,128)(2,1)}, u32[]{:S(2)}, u32[]{:S(2)}) %collective-permute-start.3) | collective-permute-done | bytes 229408 | tf_op jit(solution)/shard_map/ppermute | solution.py:41
  26.2 0.9 pad_maximum_fusion.3
  27.4 4.8 %project.2 = (bf16[512,2304]{1,0:T(8,128)(2,1)S(1)}, bf16[512,128]{1,0:T(8,128)(2,1)S(1)}, bf16[256,768]{1,0:T(8,128)(2,1)S(1)}) custom-call(bf16[128,896]{1,0:T(8,128)(2,1)} %pad_maximum_fusion.8.refs_0_, bf16[128,896]{1,0:T(8,128)(2,1)} %collective-permute-done.refs_1_, bf16[128,896]{1,0:T(8,128)(2,1)} %collective-permute-done.1.refs_2_, ...), custom_call_target="tpu_custom_call" | custom-call | tf_op jit(solution)/shard_map/project/pallas_call | solution.py:262
  32.3 4.9 %project.3 = (bf16[512,2304]{1,0:T(8,128)(2,1)S(1)}, bf16[512,128]{1,0:T(8,128)(2,1)S(1)}) custom-call(bf16[128,896]{1,0:T(8,128)(2,1)} %collective-permute-done.3.refs_0_, bf16[128,896]{1,0:T(8,128)(2,1)} %collective-permute-done.4.refs_1_, bf16[128,896]{1,0:T(8,128)(2,1)} %collective-permute-done.5.refs_2_, ...), custom_call_target="tpu_custom_call" | custom-call | tf_op jit(solution)/shard_map/project/pallas_call | solution.py:262
  37.3 2.3 %copy-done.2 = bf16[768,3072]{1,0:T(8,128)(2,1)S(1)} copy-done((bf16[768,3072]{1,0:T(8,128)(2,1)S(1)}, bf16[768,3072]{1,0:T(8,128)(2,1)}, u32[]{:S(2)}) %copy-start.2) | copy-done | bytes 4718616
  39.6 2.3 %copy-done.3 = bf16[3072,768]{1,0:T(8,128)(2,1)S(1)} copy-done((bf16[3072,768]{1,0:T(8,128)(2,1)S(1)}, bf16[3072,768]{1,0:T(8,128)(2,1)}, u32[]{:S(2)}) %copy-start.3) | copy-done | bytes 4718616
  42.0 14.3 %shard_map.195 = (bf16[128,768]{1,0:T(8,128)(2,1)}, bf16[128,5760]{1,0:T(8,128)(2,1)S(1)}, bf16[128,5760]{1,0:T(8,128)(2,1)S(1)}, f32[128,768]{1,0:T(8,128)S(1)}...) custom-call(s32[9]{0:T(128)S(1)} %pad_add_fusion.place_ref, ...), custom_call_target="tpu_custom_call" | custom-call | tf_op jit(solution)/shard_map/pallas_call | solution.py:724
  56.3 2.6 %shard_map.197 = bf16[128,768]{1,0:T(8,128)(2,1)S(1)} custom-call(s32[9]{0:T(128)S(1)} %pad_add_fusion.place_ref, bf16[512,2304]{1,0:T(8,128)(2,1)S(1)} %get-tuple-element.42.refs_0_, bf16[128,896]{1,0:T(8,128)(2,1)S(1)} %get-tuple-element.47.refs_2_.refs_1_, bf16[12,128,128]{2,1,0:T(8,128)(2,1)S(1)} %get-tuple-element.50.refs_2_, ...), custom_call_target="tpu_custom_call" | custom-call | tf_op jit(solution)/shard_map/pallas_call | solution.py:724
  58.9 0.6 collective-permute-start.23
  59.6 7.6 %collective-permute-start.7 = (bf16[128,896]{1,0:T(8,128)(2,1)S(1)}, bf16[128,896]{1,0:T(8,128)(2,1)S(1)}, u32[]{:S(2)}, u32[]{:S(2)}) collective-permute-start(bf16[128,896]{1,0:T(8,128)(2,1)S(1)} %get-tuple-element.47.refs_2_.refs_1_), channel_id=1, source_target_pairs={{0,4},{1,5},{2,6},{3,7},{4,0},{5,1},{6,2},{7,3},{8,12},{9,13},{10,... | collective-permute-start | bytes 688136 | tf_op jit(solution)/shard_map/ppermute | solution.py:41
  67.4 0.6 collective-permute-start.12
  68.1 14.9 %collective-permute-done.7.refs_3_ = bf16[128,896]{1,0:T(8,128)(2,1)S(1)} collective-permute-done((bf16[128,896]{1,0:T(8,128)(2,1)S(1)}, bf16[128,896]{1,0:T(8,128)(2,1)S(1)}, u32[]{:S(2)}, u32[]{:S(2)}) %collective-permute-start.7) | collective-permute-done | bytes 229408 | tf_op jit(solution)/shard_map/ppermute | solution.py:41
  83.6 1.4 collective-permute-done.12.refs_4_
  85.5 1.1 pieces.5
  86.6 0.7 collective-permute-done.13.refs_5_
  87.2 1.5 collective-permute-start.25
  88.7 4.0 %shard_map.196 = (f32[128,768]{1,0:T(8,128)S(1)}, f32[128,768]{1,0:T(8,128)S(1)}) custom-call(s32[9]{0:T(128)S(1)} %pad_add_fusion.place_ref, bf16[512,2304]{1,0:T(8,128)(2,1)S(1)} %get-tuple-element.42.refs_0_, bf16[12,128,128]{2,1,0:T(8,128)(2,1)S(1)} %copy-done.1, bf16[128,896]{1,0:T(8,128)(2,1)S(1)} %get-tuple-element.47.refs_2_.refs_1_, ...), custom_call_target="tpu_custom_call" | custom-call | tf_op jit(solution)/shard_map/pallas_call | solution.py:724
  92.8 6.2 %shard_map.198 = (bf16[128,768]{1,0:T(8,128)(2,1)S(1)}, bf16[128,768]{1,0:T(8,128)(2,1)S(1)}, bf16[128,768]{1,0:T(8,128)(2,1)}, f32[768,128]{1,0:T(8,128)S(1)}) custom-call(s32[9]{0:T(128)S(1)} %pad_add_fusion.place_ref, bf16[512,2304]{1,0:T(8,128)(2,1)S(1)} %get-tuple-element.42.refs_0_, bf16[512,2304]{1,0:T(8,128)(2,1)S(1)} %get-tuple-element.43.refs_1_.refs_4_, ...), custom_call_target="tpu_custom_call" | custom-call | tf_op jit(solution)/shard_map/pallas_call | solution.py:724
  99.2 1.0 slice_dynamic-update-slice_fusion.3
  100.2 0.9 slice_dynamic-update-slice_fusion.2
  101.2 1.6 pieces.3
  102.8 1.3 collective-permute-start.15
  104.1 0.9 slice_dynamic-update-slice_fusion.1
  105.1 0.9 slice_dynamic-update-slice_fusion
  106.1 3.3 %pieces.4 = (bf16[384,2048]{1,0:T(8,128)(2,1)S(1)}, f32[192,2048]{1,0:T(8,128)S(1)}, f32[192,2048]{1,0:T(8,128)S(1)}, bf16[256,384]{1,0:T(8,128)(2,1)S(1)}, bf16...) custom-call(s32[3]{0:T(128)S(1)} %pad_add_fusion.1.refs_0_, ...), custom_call_target="tpu_custom_call" | custom-call | tf_op jit(solution)/shard_map/pieces/pallas_call | solution.py:173
  109.4 1.8 collective-permute-start.34
  111.7 1.3 collective-permute-start.32
  112.9 2.3 %collective-permute-done.15 = bf16[384,896]{1,0:T(8,128)(2,1)S(1)} collective-permute-done((bf16[384,896]{1,0:T(8,128)(2,1)S(1)}, bf16[384,896]{1,0:T(8,128)(2,1)S(1)}, u32[]{:S(2)}, u32[]{:S(2)}) %collective-permute-start.15) | collective-permute-done | bytes 688160 | tf_op jit(solution)/shard_map/ppermute | solution.py:52
  115.3 1.6 collective-permute-start.16
  116.9 3.5 %collective-permute-done.34 = bf16[256,384]{1,0:T(8,128)(2,1)S(1)} collective-permute-done((bf16[256,384]{1,0:T(8,128)(2,1)S(1)}, bf16[256,384]{1,0:T(8,128)(2,1)S(1)}, u32[]{:S(2)}, u32[]{:S(2)}) %collective-permute-start.34) | collective-permute-done | bytes 196640 | tf_op jit(solution)/shard_map/ppermute | solution.py:52
  120.9 1.5 collective-permute-done.33
  122.4 1.2 collective-permute-done.32
  123.7 0.8 convolution_convert_fusion
  124.5 5.3 %collective-permute-done.16 = bf16[192,896]{1,0:T(8,128)(2,1)S(1)} collective-permute-done((bf16[192,896]{1,0:T(8,128)(2,1)S(1)}, bf16[192,896]{1,0:T(8,128)(2,1)S(1)}, u32[]{:S(2)}, u32[]{:S(2)}) %collective-permute-start.16) | collective-permute-done | bytes 344096 | tf_op jit(solution)/shard_map/ppermute | solution.py:52
  130.0 2.0 collective-permute-start.17
  132.2 7.0 %collective-permute-done.17 = bf16[96,896]{1,0:T(8,128)(2,1)S(1)} collective-permute-done((bf16[96,896]{1,0:T(8,128)(2,1)S(1)}, bf16[96,896]{1,0:T(8,128)(2,1)S(1)}, u32[]{:S(2)}, u32[]{:S(2)}) %collective-permute-start.17) | collective-permute-done | bytes 172064 | tf_op jit(solution)/shard_map/ppermute | solution.py:41
  139.3 8.5 %collective-permute-done.18 = bf16[96,896]{1,0:T(8,128)(2,1)S(1)} collective-permute-done((bf16[96,896]{1,0:T(8,128)(2,1)S(1)}, bf16[96,896]{1,0:T(8,128)(2,1)S(1)}, u32[]{:S(2)}, u32[]{:S(2)}) %collective-permute-start.18) | collective-permute-done | bytes 172064 | tf_op jit(solution)/shard_map/ppermute | solution.py:41
  148.0 0.9 collective-permute-start.40
  148.9 6.6 %collective-permute-done.19 = bf16[96,896]{1,0:T(8,128)(2,1)S(1)} collective-permute-done((bf16[96,896]{1,0:T(8,128)(2,1)S(1)}, bf16[96,896]{1,0:T(8,128)(2,1)S(1)}, u32[]{:S(2)}, u32[]{:S(2)}) %collective-permute-start.19) | collective-permute-done | bytes 172064 | tf_op jit(solution)/shard_map/ppermute | solution.py:41
  155.9 3.7 %collective-permute-done.40 = bf16[96,1536]{1,0:T(8,128)(2,1)S(1)} collective-permute-done((bf16[96,1536]{1,0:T(8,128)(2,1)S(1)}, bf16[96,1536]{1,0:T(8,128)(2,1)S(1)}, u32[]{:S(2)}, u32[]{:S(2)}) %collective-permute-start.40) | collective-permute-done | bytes 294944 | tf_op jit(solution)/shard_map/ppermute | solution.py:41
  160.2 0.8 slice_reduce_fusion.2
  161.0 8.3 %collective-permute-done.41 = bf16[96,1536]{1,0:T(8,128)(2,1)S(1)} collective-permute-done((bf16[96,1536]{1,0:T(8,128)(2,1)S(1)}, bf16[96,1536]{1,0:T(8,128)(2,1)S(1)}, u32[]{:S(2)}, u32[]{:S(2)}) %collective-permute-start.41) | collective-permute-done | bytes 294944 | tf_op jit(solution)/shard_map/ppermute | solution.py:41
  170.1 12.8 %collective-permute-done.27 = bf16[96,2432]{1,0:T(8,128)(2,1)S(1)} collective-permute-done((bf16[96,2432]{1,0:T(8,128)(2,1)S(1)}, bf16[96,2432]{1,0:T(8,128)(2,1)S(1)}, u32[]{:S(2)}, u32[]{:S(2)}) %collective-permute-start.27) | collective-permute-done | bytes 466976 | tf_op jit(solution)/shard_map/ppermute | solution.py:41
  183.0 1.5 collective-permute-start.28
  184.7 21.3 %collective-permute-done.28 = bf16[96,2432]{1,0:T(8,128)(2,1)S(1)} collective-permute-done((bf16[96,2432]{1,0:T(8,128)(2,1)S(1)}, bf16[96,2432]{1,0:T(8,128)(2,1)S(1)}, u32[]{:S(2)}, u32[]{:S(2)}) %collective-permute-start.28) | collective-permute-done | bytes 466976 | tf_op jit(solution)/shard_map/ppermute | solution.py:41
  206.3 1.6 maximum_convert_fusion.1
  207.9 10.8 %collective-permute-done.29 = bf16[96,2432]{1,0:T(8,128)(2,1)S(1)} collective-permute-done((bf16[96,2432]{1,0:T(8,128)(2,1)S(1)}, bf16[96,2432]{1,0:T(8,128)(2,1)S(1)}, u32[]{:S(2)}, u32[]{:S(2)}) %collective-permute-start.29) | collective-permute-done | bytes 466976 | tf_op jit(solution)/shard_map/ppermute | solution.py:41
  218.9 1.7 collective-permute-done.31
  221.2 0.8 slice_reduce_fusion
  222.0 0.9 maximum_convert_fusion.3
  222.8 1.7 maximum_convert_fusion
  224.5 1.3 maximum_convert_fusion.2
  (147 shorter events, 8.7 us)
Async XLA Ops:
  1.5 24.8 %copy-start.4 = (bf16[1,128,768]{2,1,0:T(8,128)(2,1)S(1)}, bf16[1,128,768]{2,1,0:T(8,128)(2,1)}, u32[]{:S(2)}) copy-start(bf16[1,128,768]{2,1,0:T(8,128)(2,1)} %param.23) | copy-start | bytes 589828
  3.2 17.2 %collective-permute-start.1 = (bf16[128,896]{1,0:T(8,128)(2,1)}, bf16[128,896]{1,0:T(8,128)(2,1)}, u32[]{:S(2)}, u32[]{:S(2)}) collective-permute-start(bf16[128,896]{1,0:T(8,128)(2,1)} %pad_maximum_fusion.8.refs_0_), channel_id=1, source_target_pairs={{0,2},{1,3},{2,0},{3,1},{4,6},{5,7},{6,4},{7,5},{8,10},{9,11},{10,... | collective-permute-start | bytes 688136 | tf_op jit(solution)/shard_map/ppermute | solution.py:41
  6.2 19.5 %collective-permute-start.3 = (bf16[128,896]{1,0:T(8,128)(2,1)}, bf16[128,896]{1,0:T(8,128)(2,1)}, u32[]{:S(2)}, u32[]{:S(2)}) collective-permute-start(bf16[128,896]{1,0:T(8,128)(2,1)} %pad_maximum_fusion.8.refs_0_), channel_id=1, source_target_pairs={{0,4},{1,5},{2,6},{3,7},{4,0},{5,1},{6,2},{7,3},{8,12},{9,13},{10,... | collective-permute-start | bytes 688136 | tf_op jit(solution)/shard_map/ppermute | solution.py:41
  8.8 16.9 %collective-permute-start.5 = (bf16[128,896]{1,0:T(8,128)(2,1)}, bf16[128,896]{1,0:T(8,128)(2,1)}, u32[]{:S(2)}, u32[]{:S(2)}) collective-permute-start(bf16[128,896]{1,0:T(8,128)(2,1)} %pad_maximum_fusion.8.refs_0_), channel_id=1, source_target_pairs={{0,6},{1,7},{2,4},{3,5},{4,2},{5,3},{6,0},{7,1},{8,14},{9,15},{10,... | collective-permute-start | bytes 688136 | tf_op jit(solution)/shard_map/ppermute | solution.py:41
  8.8 7.3 %collective-permute-start.37 = (bf16[128,768]{1,0:T(8,128)(2,1)}, bf16[128,768]{1,0:T(8,128)(2,1)S(1)}, u32[]{:S(2)}, u32[]{:S(2)}) collective-permute-start(bf16[128,768]{1,0:T(8,128)(2,1)} %bitcast.21), channel_id=1, source_target_pairs={{0,24},{1,25},{2,26},{3,27},{4,28},{5,29},{6,30},{7,31},{8,16},{9,... | collective-permute-start | bytes 589832 | tf_op jit(solution)/shard_map/ppermute | solution.py:52
  11.5 8.7 %collective-permute-start.36 = (bf16[128,768]{1,0:T(8,128)(2,1)}, bf16[128,768]{1,0:T(8,128)(2,1)S(1)}, u32[]{:S(2)}, u32[]{:S(2)}) collective-permute-start(bf16[128,768]{1,0:T(8,128)(2,1)} %bitcast.22), channel_id=1, source_target_pairs={{0,16},{1,17},{2,18},{3,19},{4,20},{5,21},{6,22},{7,23},{8,24},{9,... | collective-permute-start | bytes 589832 | tf_op jit(solution)/shard_map/ppermute | solution.py:52
  16.1 11.1 %copy-start.12 = (bf16[128,768]{1,0:T(8,128)(2,1)}, bf16[128,768]{1,0:T(8,128)(2,1)S(1)}, u32[]{:S(2)}) copy-start(bf16[128,768]{1,0:T(8,128)(2,1)S(1)} %collective-permute-done.37) | copy-start | bytes 589828
  16.1 10.2 %collective-permute-start.35 = (bf16[128,768]{1,0:T(8,128)(2,1)}, bf16[128,768]{1,0:T(8,128)(2,1)S(1)}, u32[]{:S(2)}, u32[]{:S(2)}) collective-permute-start(bf16[128,768]{1,0:T(8,128)(2,1)} %bitcast.23), channel_id=1, source_target_pairs={{0,8},{1,9},{2,10},{3,11},{4,12},{5,13},{6,14},{7,15},{8,0},{9,1},... | collective-permute-start | bytes 589832 | tf_op jit(solution)/shard_map/ppermute | solution.py:52
  17.6 9.7 %copy-start = (bf16[768,2304]{1,0:T(8,128)(2,1)S(1)}, bf16[768,2304]{1,0:T(8,128)(2,1)}, u32[]{:S(2)}) copy-start(bf16[768,2304]{1,0:T(8,128)(2,1)} %refs_9_.3) | copy-start | bytes 10616836
  17.7 9.7 %copy-start.8 = (f32[768]{0:T(1024)S(1)}, f32[768]{0:T(1024)}, u32[]{:S(2)}) copy-start(f32[768]{0:T(1024)} %refs_12_.1) | copy-start | bytes 9220
  17.7 9.7 %copy-start.9 = (f32[768]{0:T(1024)S(1)}, f32[768]{0:T(1024)}, u32[]{:S(2)}) copy-start(f32[768]{0:T(1024)} %refs_5_.3) | copy-start | bytes 9220
  20.2 7.0 %copy-start.14 = (bf16[128,768]{1,0:T(8,128)(2,1)}, bf16[128,768]{1,0:T(8,128)(2,1)S(1)}, u32[]{:S(2)}) copy-start(bf16[128,768]{1,0:T(8,128)(2,1)S(1)} %collective-permute-done.36) | copy-start | bytes 589828
  20.2 7.1 %collective-permute-start = (bf16[128,896]{1,0:T(8,128)(2,1)}, bf16[128,896]{1,0:T(8,128)(2,1)}, u32[]{:S(2)}, u32[]{:S(2)}) collective-permute-start(bf16[128,896]{1,0:T(8,128)(2,1)} %pad_maximum_fusion.8.refs_0_), channel_id=1, source_target_pairs={{0,1},{1,0},{2,3},{3,2},{4,5},{5,4},{6,7},{7,6},{8,9},{9,8},{10,11... | collective-permute-start | bytes 688136 | tf_op jit(solution)/shard_map/ppermute | solution.py:41
  20.3 7.0 %collective-permute-start.2 = (bf16[128,896]{1,0:T(8,128)(2,1)}, bf16[128,896]{1,0:T(8,128)(2,1)}, u32[]{:S(2)}, u32[]{:S(2)}) collective-permute-start(bf16[128,896]{1,0:T(8,128)(2,1)} %collective-permute-done.1.refs_2_), channel_id=1, source_target_pairs={{0,1},{1,0},{2,3},{3,2},{4,5},{5,4},{6,7},{7,6},{8,9},{9,8},{10,11... | collective-permute-start | bytes 688136 | tf_op jit(solution)/shard_map/ppermute | solution.py:41
  25.7 6.5 %collective-permute-start.4 = (bf16[128,896]{1,0:T(8,128)(2,1)}, bf16[128,896]{1,0:T(8,128)(2,1)}, u32[]{:S(2)}, u32[]{:S(2)}) collective-permute-start(bf16[128,896]{1,0:T(8,128)(2,1)} %collective-permute-done.3.refs_0_), channel_id=1, source_target_pairs={{0,1},{1,0},{2,3},{3,2},{4,5},{5,4},{6,7},{7,6},{8,9},{9,8},{10,11... | collective-permute-start | bytes 688136 | tf_op jit(solution)/shard_map/ppermute | solution.py:41
  25.7 6.6 %collective-permute-start.6 = (bf16[128,896]{1,0:T(8,128)(2,1)}, bf16[128,896]{1,0:T(8,128)(2,1)}, u32[]{:S(2)}, u32[]{:S(2)}) collective-permute-start(bf16[128,896]{1,0:T(8,128)(2,1)} %collective-permute-done.5.refs_2_), channel_id=1, source_target_pairs={{0,1},{1,0},{2,3},{3,2},{4,5},{5,4},{6,7},{7,6},{8,9},{9,8},{10,11... | collective-permute-start | bytes 688136 | tf_op jit(solution)/shard_map/ppermute | solution.py:41
  26.2 1.0 copy-start.16
  27.2 72.0 %collective-permute-start.38 = (bf16[512,768]{1,0:T(8,128)(2,1)}, bf16[512,768]{1,0:T(8,128)(2,1)}, u32[]{:S(2)}, u32[]{:S(2)}) collective-permute-start(bf16[512,768]{1,0:T(8,128)(2,1)} %pad_maximum_fusion.3), channel_id=1, source_target_pairs={{0,1},{1,0},{2,3},{3,2},{4,5},{5,4},{6,7},{7,6},{8,9},{9,8},{10,11... | collective-permute-start | bytes 2359304 | tf_op jit(solution)/shard_map/ppermute | solution.py:41
  32.2 5.0 %copy-start.1 = (bf16[12,128,128]{2,1,0:T(8,128)(2,1)S(1)}, bf16[12,128,128]{2,1,0:T(8,128)(2,1)}, u32[]{:S(2)}) copy-start(bf16[12,128,128]{2,1,0:T(8,128)(2,1)} %maximum_maximum_fusion.refs_4_.refs_1_.refs_2_) | copy-start | bytes 1179652
  32.2 5.0 %copy-start.5 = (bf16[1,128,768]{2,1,0:T(8,128)(2,1)S(1)}, bf16[1,128,768]{2,1,0:T(8,128)(2,1)}, u32[]{:S(2)}) copy-start(bf16[1,128,768]{2,1,0:T(8,128)(2,1)} %param.23) | copy-start | bytes 589828
  32.2 5.0 %copy-start.6 = (bf16[1,128,768]{2,1,0:T(8,128)(2,1)S(1)}, bf16[1,128,768]{2,1,0:T(8,128)(2,1)}, u32[]{:S(2)}) copy-start(bf16[1,128,768]{2,1,0:T(8,128)(2,1)} %param.12) | copy-start | bytes 589828
  32.2 5.0 %copy-start.7 = (bf16[768,768]{1,0:T(8,128)(2,1)S(1)}, bf16[768,768]{1,0:T(8,128)(2,1)}, u32[]{:S(2)}) copy-start(bf16[768,768]{1,0:T(8,128)(2,1)} %refs_9_.2) | copy-start | bytes 3538948
  32.2 5.0 %copy-start.10 = (f32[768]{0:T(1024)S(1)}, f32[768]{0:T(1024)}, u32[]{:S(2)}) copy-start(f32[768]{0:T(1024)} %refs_7_.1) | copy-start | bytes 9220
  32.3 5.0 %copy-start.11 = (f32[768]{0:T(1024)S(1)}, f32[768]{0:T(1024)}, u32[]{:S(2)}) copy-start(f32[768]{0:T(1024)} %refs_8_.1) | copy-start | bytes 9220
  37.3 2.3 %copy-start.2 = (bf16[768,3072]{1,0:T(8,128)(2,1)S(1)}, bf16[768,3072]{1,0:T(8,128)(2,1)}, u32[]{:S(2)}) copy-start(bf16[768,3072]{1,0:T(8,128)(2,1)} %refs_10_.1) | copy-start | bytes 14155780
  39.6 2.3 %copy-start.3 = (bf16[3072,768]{1,0:T(8,128)(2,1)S(1)}, bf16[3072,768]{1,0:T(8,128)(2,1)}, u32[]{:S(2)}) copy-start(bf16[3072,768]{1,0:T(8,128)(2,1)} %refs_11_.1) | copy-start | bytes 14155780
  58.9 8.5 %collective-permute-start.23 = (bf16[128,384]{1,0:T(8,128)(2,1)S(1)}, bf16[128,384]{1,0:T(8,128)(2,1)S(1)}, u32[]{:S(2)}, u32[]{:S(2)}) collective-permute-start(bf16[128,384]{1,0:T(8,128)(2,1)S(1)} %get-tuple-element.106), channel_id=1, source_target_pairs={{0,1},{1,0},{2,3},{3,2},{4,5},{5,4},{6,7},{7,6},{8,9},{9,8},{10,11... | collective-permute-start | bytes 294920 | tf_op jit(solution)/shard_map/ppermute | solution.py:41
  59.6 23.4 %collective-permute-start.7 = (bf16[128,896]{1,0:T(8,128)(2,1)S(1)}, bf16[128,896]{1,0:T(8,128)(2,1)S(1)}, u32[]{:S(2)}, u32[]{:S(2)}) collective-permute-start(bf16[128,896]{1,0:T(8,128)(2,1)S(1)} %get-tuple-element.47.refs_2_.refs_1_), channel_id=1, source_target_pairs={{0,4},{1,5},{2,6},{3,7},{4,0},{5,1},{6,2},{7,3},{8,12},{9,13},{10,... | collective-permute-start | bytes 688136 | tf_op jit(solution)/shard_map/ppermute | solution.py:41
  67.2 15.8 %collective-permute-start.9 = (bf16[128,896]{1,0:T(8,128)(2,1)S(1)}, bf16[128,896]{1,0:T(8,128)(2,1)S(1)}, u32[]{:S(2)}, u32[]{:S(2)}) collective-permute-start(bf16[128,896]{1,0:T(8,128)(2,1)S(1)} %get-tuple-element.47.refs_2_.refs_1_), channel_id=1, source_target_pairs={{0,6},{1,7},{2,4},{3,5},{4,2},{5,3},{6,0},{7,1},{8,14},{9,15},{10,... | collective-permute-start | bytes 688136 | tf_op jit(solution)/shard_map/ppermute | solution.py:41
  67.2 16.3 %collective-permute-start.11 = (bf16[128,896]{1,0:T(8,128)(2,1)S(1)}, bf16[128,896]{1,0:T(8,128)(2,1)S(1)}, u32[]{:S(2)}, u32[]{:S(2)}) collective-permute-start(bf16[128,896]{1,0:T(8,128)(2,1)S(1)} %get-tuple-element.47.refs_2_.refs_1_), channel_id=1, source_target_pairs={{0,1},{1,0},{2,3},{3,2},{4,5},{5,4},{6,7},{7,6},{8,9},{9,8},{10,11... | collective-permute-start | bytes 688136 | tf_op jit(solution)/shard_map/ppermute | solution.py:41
  67.4 17.5 %collective-permute-start.12 = (bf16[128,896]{1,0:T(8,128)(2,1)S(1)}, bf16[128,896]{1,0:T(8,128)(2,1)S(1)}, u32[]{:S(2)}, u32[]{:S(2)}) collective-permute-start(bf16[128,896]{1,0:T(8,128)(2,1)S(1)} %get-tuple-element.47.refs_2_.refs_1_), channel_id=1, source_target_pairs={{0,2},{1,3},{2,0},{3,1},{4,6},{5,7},{6,4},{7,5},{8,10},{9,11},{10,... | collective-permute-start | bytes 688136 | tf_op jit(solution)/shard_map/ppermute | solution.py:41
  83.0 23.1 %collective-permute-start.22 = (bf16[128,5760]{1,0:T(8,128)(2,1)S(1)}, bf16[128,5760]{1,0:T(8,128)(2,1)S(1)}, u32[]{:S(2)}, u32[]{:S(2)}) collective-permute-start(bf16[128,5760]{1,0:T(8,128)(2,1)S(1)} %get-tuple-element.62), channel_id=1, source_target_pairs={{0,1},{1,0},{2,3},{3,2},{4,5},{5,4},{6,7},{7,6},{8,9},{9,8},{10,11... | collective-permute-start | bytes 4423688 | tf_op jit(solution)/shard_map/ppermute | solution.py:41
  83.0 9.7 %collective-permute-start.8 = (bf16[128,896]{1,0:T(8,128)(2,1)S(1)}, bf16[128,896]{1,0:T(8,128)(2,1)S(1)}, u32[]{:S(2)}, u32[]{:S(2)}) collective-permute-start(bf16[128,896]{1,0:T(8,128)(2,1)S(1)} %collective-permute-done.7.refs_3_), channel_id=1, source_target_pairs={{0,1},{1,0},{2,3},{3,2},{4,5},{5,4},{6,7},{7,6},{8,9},{9,8},{10,11... | collective-permute-start | bytes 688136 | tf_op jit(solution)/shard_map/ppermute | solution.py:41
  83.5 9.3 %collective-permute-start.10 = (bf16[128,896]{1,0:T(8,128)(2,1)S(1)}, bf16[128,896]{1,0:T(8,128)(2,1)S(1)}, u32[]{:S(2)}, u32[]{:S(2)}) collective-permute-start(bf16[128,896]{1,0:T(8,128)(2,1)S(1)} %collective-permute-done.9.refs_5_), channel_id=1, source_target_pairs={{0,1},{1,0},{2,3},{3,2},{4,5},{5,4},{6,7},{7,6},{8,9},{9,8},{10,11... | collective-permute-start | bytes 688136 | tf_op jit(solution)/shard_map/ppermute | solution.py:41
  85.0 2.3 %collective-permute-start.13 = (bf16[128,896]{1,0:T(8,128)(2,1)S(1)}, bf16[128,896]{1,0:T(8,128)(2,1)S(1)}, u32[]{:S(2)}, u32[]{:S(2)}) collective-permute-start(bf16[128,896]{1,0:T(8,128)(2,1)S(1)} %collective-permute-done.12.refs_4_), channel_id=1, source_target_pairs={{0,1},{1,0},{2,3},{3,2},{4,5},{5,4},{6,7},{7,6},{8,9},{9,8},{10,11... | collective-permute-start | bytes 688136 | tf_op jit(solution)/shard_map/ppermute | solution.py:41
  87.2 52.0 %collective-permute-start.25 = (bf16[384,384]{1,0:T(8,128)(2,1)S(1)}, bf16[384,384]{1,0:T(8,128)(2,1)S(1)}, u32[]{:S(2)}, u32[]{:S(2)}) collective-permute-start(bf16[384,384]{1,0:T(8,128)(2,1)S(1)} %get-tuple-element.67), channel_id=1, source_target_pairs={{0,8},{1,17},{2,10},{3,19},{4,12},{5,21},{6,14},{7,23},{8,0},{9,25... | collective-permute-start | bytes 884744 | tf_op jit(solution)/shard_map/ppermute | solution.py:52
  92.8 7.4 %copy-start.17 = (bf16[128,768]{1,0:T(8,128)(2,1)S(1)}, bf16[128,768]{1,0:T(8,128)(2,1)}, u32[]{:S(2)}) copy-start(bf16[128,768]{1,0:T(8,128)(2,1)} %copy-done.16) | copy-start | bytes 589828
  99.0 5.0 %copy-start.15 = (bf16[128,768]{1,0:T(8,128)(2,1)S(1)}, bf16[128,768]{1,0:T(8,128)(2,1)}, u32[]{:S(2)}) copy-start(bf16[128,768]{1,0:T(8,128)(2,1)} %copy-done.14) | copy-start | bytes 589828
  99.1 6.0 %copy-start.13 = (bf16[128,768]{1,0:T(8,128)(2,1)S(1)}, bf16[128,768]{1,0:T(8,128)(2,1)}, u32[]{:S(2)}) copy-start(bf16[128,768]{1,0:T(8,128)(2,1)} %copy-done.12) | copy-start | bytes 589828
  99.1 2.1 collective-permute-start.14
  102.8 12.4 %collective-permute-start.15 = (bf16[384,896]{1,0:T(8,128)(2,1)S(1)}, bf16[384,896]{1,0:T(8,128)(2,1)S(1)}, u32[]{:S(2)}, u32[]{:S(2)}) collective-permute-start(bf16[384,896]{1,0:T(8,128)(2,1)S(1)} %get-tuple-element.59), channel_id=1, source_target_pairs={{0,8},{1,17},{2,10},{3,19},{4,12},{5,21},{6,14},{7,23},{8,0},{9,25... | collective-permute-start | bytes 2064392 | tf_op jit(solution)/shard_map/ppermute | solution.py:52
  109.4 11.1 %collective-permute-start.34 = (bf16[256,384]{1,0:T(8,128)(2,1)S(1)}, bf16[256,384]{1,0:T(8,128)(2,1)S(1)}, u32[]{:S(2)}, u32[]{:S(2)}) collective-permute-start(bf16[256,384]{1,0:T(8,128)(2,1)S(1)} %get-tuple-element.73), channel_id=1, source_target_pairs={{0,24},{1,25},{2,26},{3,27},{4,28},{5,29},{6,30},{7,31},{8,16},{9,... | collective-permute-start | bytes 589832 | tf_op jit(solution)/shard_map/ppermute | solution.py:52
  111.1 11.3 %collective-permute-start.33 = (bf16[256,384]{1,0:T(8,128)(2,1)S(1)}, bf16[256,384]{1,0:T(8,128)(2,1)S(1)}, u32[]{:S(2)}, u32[]{:S(2)}) collective-permute-start(bf16[256,384]{1,0:T(8,128)(2,1)S(1)} %get-tuple-element.72), channel_id=1, source_target_pairs={{0,16},{1,17},{2,18},{3,19},{4,20},{5,21},{6,22},{7,23},{8,24},{9,... | collective-permute-start | bytes 589832 | tf_op jit(solution)/shard_map/ppermute | solution.py:52
  111.7 12.0 %collective-permute-start.32 = (bf16[256,384]{1,0:T(8,128)(2,1)S(1)}, bf16[256,384]{1,0:T(8,128)(2,1)S(1)}, u32[]{:S(2)}, u32[]{:S(2)}) collective-permute-start(bf16[256,384]{1,0:T(8,128)(2,1)S(1)} %get-tuple-element.71), channel_id=1, source_target_pairs={{0,8},{1,9},{2,10},{3,11},{4,12},{5,13},{6,14},{7,15},{8,0},{9,1},... | collective-permute-start | bytes 589832 | tf_op jit(solution)/shard_map/ppermute | solution.py:52
  115.3 14.5 %collective-permute-start.16 = (bf16[192,896]{1,0:T(8,128)(2,1)S(1)}, bf16[192,896]{1,0:T(8,128)(2,1)S(1)}, u32[]{:S(2)}, u32[]{:S(2)}) collective-permute-start(bf16[192,896]{1,0:T(8,128)(2,1)S(1)} %add_convert_fusion.4), channel_id=1, source_target_pairs={{0,16},{1,9},{2,18},{3,11},{4,20},{5,13},{6,22},{7,15},{8,24},{9,1... | collective-permute-start | bytes 1032200 | tf_op jit(solution)/shard_map/ppermute | solution.py:52
  120.4 35.1 %collective-permute-start.24 = (bf16[384,2048]{1,0:T(8,128)(2,1)S(1)}, bf16[384,2048]{1,0:T(8,128)(2,1)S(1)}, u32[]{:S(2)}, u32[]{:S(2)}) collective-permute-start(bf16[384,2048]{1,0:T(8,128)(2,1)S(1)} %get-tuple-element.66), channel_id=1, source_target_pairs={{0,8},{1,17},{2,10},{3,19},{4,12},{5,21},{6,14},{7,23},{8,0},{9,25... | collective-permute-start | bytes 4718600 | tf_op jit(solution)/shard_map/ppermute | solution.py:52
  130.0 9.2 %collective-permute-start.17 = (bf16[96,896]{1,0:T(8,128)(2,1)S(1)}, bf16[96,896]{1,0:T(8,128)(2,1)S(1)}, u32[]{:S(2)}, u32[]{:S(2)}) collective-permute-start(bf16[96,896]{1,0:T(8,128)(2,1)S(1)} %constant_dynamic-slice_fusion.3), channel_id=1, source_target_pairs={{0,2},{1,3},{2,0},{3,1},{4,6},{5,7},{6,4},{7,5},{8,10},{9,11},{10,... | collective-permute-start | bytes 516104 | tf_op jit(solution)/shard_map/ppermute | solution.py:41
  132.0 15.9 %collective-permute-start.39 = (bf16[96,1536]{1,0:T(8,128)(2,1)S(1)}, bf16[96,1536]{1,0:T(8,128)(2,1)S(1)}, u32[]{:S(2)}, u32[]{:S(2)}) collective-permute-start(bf16[96,1536]{1,0:T(8,128)(2,1)S(1)} %fusion.12), channel_id=1, source_target_pairs={{0,2},{1,3},{2,0},{3,1},{4,6},{5,7},{6,4},{7,5},{8,10},{9,11},{10,... | collective-permute-start | bytes 884744 | tf_op jit(solution)/shard_map/ppermute | solution.py:41
  139.2 8.6 %collective-permute-start.18 = (bf16[96,896]{1,0:T(8,128)(2,1)S(1)}, bf16[96,896]{1,0:T(8,128)(2,1)S(1)}, u32[]{:S(2)}, u32[]{:S(2)}) collective-permute-start(bf16[96,896]{1,0:T(8,128)(2,1)S(1)} %add_convert_fusion.8), channel_id=1, source_target_pairs={{0,4},{1,5},{2,6},{3,7},{4,0},{5,1},{6,2},{7,3},{8,12},{9,13},{10,... | collective-permute-start | bytes 516104 | tf_op jit(solution)/shard_map/ppermute | solution.py:41
  139.3 16.3 %copy-start.18 = (bf16[384,384]{1,0:T(8,128)(2,1)}, bf16[384,384]{1,0:T(8,128)(2,1)S(1)}, u32[]{:S(2)}) copy-start(bf16[384,384]{1,0:T(8,128)(2,1)S(1)} %collective-permute-done.25) | copy-start | bytes 884740
  147.9 7.7 %collective-permute-start.19 = (bf16[96,896]{1,0:T(8,128)(2,1)S(1)}, bf16[96,896]{1,0:T(8,128)(2,1)S(1)}, u32[]{:S(2)}, u32[]{:S(2)}) collective-permute-start(bf16[96,896]{1,0:T(8,128)(2,1)S(1)} %add_convert_fusion.7), channel_id=1, source_target_pairs={{0,2},{1,3},{2,0},{3,1},{4,6},{5,7},{6,4},{7,5},{8,10},{9,11},{10,... | collective-permute-start | bytes 516104 | tf_op jit(solution)/shard_map/ppermute | solution.py:41
  148.0 11.6 %collective-permute-start.40 = (bf16[96,1536]{1,0:T(8,128)(2,1)S(1)}, bf16[96,1536]{1,0:T(8,128)(2,1)S(1)}, u32[]{:S(2)}, u32[]{:S(2)}) collective-permute-start(bf16[96,1536]{1,0:T(8,128)(2,1)S(1)} %add_convert_fusion.6), channel_id=1, source_target_pairs={{0,4},{1,5},{2,6},{3,7},{4,0},{5,1},{6,2},{7,3},{8,12},{9,13},{10,... | collective-permute-start | bytes 884744 | tf_op jit(solution)/shard_map/ppermute | solution.py:41
  148.9 11.0 %collective-permute-start.20 = (bf16[96,896]{1,0:T(8,128)(2,1)S(1)}, bf16[96,896]{1,0:T(8,128)(2,1)S(1)}, u32[]{:S(2)}, u32[]{:S(2)}) collective-permute-start(bf16[96,896]{1,0:T(8,128)(2,1)S(1)} %add_convert_fusion.7), channel_id=1, source_target_pairs={{0,1},{1,0},{2,3},{3,2},{4,5},{5,4},{6,7},{7,6},{8,9},{9,8},{10,11... | collective-permute-start | bytes 516104 | tf_op jit(solution)/shard_map/ppermute | solution.py:41
  155.5 4.4 %collective-permute-start.21 = (bf16[96,896]{1,0:T(8,128)(2,1)S(1)}, bf16[96,896]{1,0:T(8,128)(2,1)S(1)}, u32[]{:S(2)}, u32[]{:S(2)}) collective-permute-start(bf16[96,896]{1,0:T(8,128)(2,1)S(1)} %collective-permute-done.19), channel_id=1, source_target_pairs={{0,1},{1,0},{2,3},{3,2},{4,5},{5,4},{6,7},{7,6},{8,9},{9,8},{10,11... | collective-permute-start | bytes 516104 | tf_op jit(solution)/shard_map/ppermute | solution.py:41
  155.8 13.6 %collective-permute-start.26 = (bf16[192,2432]{1,0:T(8,128)(2,1)S(1)}, bf16[192,2432]{1,0:T(8,128)(2,1)S(1)}, u32[]{:S(2)}, u32[]{:S(2)}) collective-permute-start(bf16[192,2432]{1,0:T(8,128)(2,1)S(1)} %pad_maximum_fusion), channel_id=1, source_target_pairs={{0,16},{1,9},{2,18},{3,11},{4,20},{5,13},{6,22},{7,15},{8,24},{9,1... | collective-permute-start | bytes 2801672 | tf_op jit(solution)/shard_map/ppermute | solution.py:52
  159.7 24.7 %collective-permute-start.42 = (bf16[96,1536]{1,0:T(8,128)(2,1)S(1)}, bf16[96,1536]{1,0:T(8,128)(2,1)S(1)}, u32[]{:S(2)}, u32[]{:S(2)}) collective-permute-start(bf16[96,1536]{1,0:T(8,128)(2,1)S(1)} %add_convert_fusion.5), channel_id=1, source_target_pairs={{0,1},{1,0},{2,3},{3,2},{4,5},{5,4},{6,7},{7,6},{8,9},{9,8},{10,11... | collective-permute-start | bytes 884744 | tf_op jit(solution)/shard_map/ppermute | solution.py:41
  159.8 9.4 %collective-permute-start.41 = (bf16[96,1536]{1,0:T(8,128)(2,1)S(1)}, bf16[96,1536]{1,0:T(8,128)(2,1)S(1)}, u32[]{:S(2)}, u32[]{:S(2)}) collective-permute-start(bf16[96,1536]{1,0:T(8,128)(2,1)S(1)} %add_convert_fusion.5), channel_id=1, source_target_pairs={{0,2},{1,3},{2,0},{3,1},{4,6},{5,7},{6,4},{7,5},{8,10},{9,11},{10,... | collective-permute-start | bytes 884744 | tf_op jit(solution)/shard_map/ppermute | solution.py:41
  160.1 9.4 %slice-start = ((bf16[384,384]{1,0:T(8,128)(2,1)}), bf16[192,384]{1,0:T(8,128)(2,1)S(1)}, s32[]{:S(2)}) async-start(bf16[384,384]{1,0:T(8,128)(2,1)} %copy-done.18), calls=%async_computation | async-start | bytes 294912 | tf_op jit(solution)/shard_map/slice | solution.py:189
  169.2 15.2 %collective-permute-start.43 = (bf16[96,1536]{1,0:T(8,128)(2,1)S(1)}, bf16[96,1536]{1,0:T(8,128)(2,1)S(1)}, u32[]{:S(2)}, u32[]{:S(2)}) collective-permute-start(bf16[96,1536]{1,0:T(8,128)(2,1)S(1)} %collective-permute-done.41), channel_id=1, source_target_pairs={{0,1},{1,0},{2,3},{3,2},{4,5},{5,4},{6,7},{7,6},{8,9},{9,8},{10,11... | collective-permute-start | bytes 884744 | tf_op jit(solution)/shard_map/ppermute | solution.py:41
  169.9 13.0 %collective-permute-start.27 = (bf16[96,2432]{1,0:T(8,128)(2,1)S(1)}, bf16[96,2432]{1,0:T(8,128)(2,1)S(1)}, u32[]{:S(2)}, u32[]{:S(2)}) collective-permute-start(bf16[96,2432]{1,0:T(8,128)(2,1)S(1)} %constant_dynamic-slice_fusion), channel_id=1, source_target_pairs={{0,2},{1,3},{2,0},{3,1},{4,6},{5,7},{6,4},{7,5},{8,10},{9,11},{10,... | collective-permute-start | bytes 1400840 | tf_op jit(solution)/shard_map/ppermute | solution.py:41
  183.0 23.1 %collective-permute-start.28 = (bf16[96,2432]{1,0:T(8,128)(2,1)S(1)}, bf16[96,2432]{1,0:T(8,128)(2,1)S(1)}, u32[]{:S(2)}, u32[]{:S(2)}) collective-permute-start(bf16[96,2432]{1,0:T(8,128)(2,1)S(1)} %add_convert_fusion.2), channel_id=1, source_target_pairs={{0,4},{1,5},{2,6},{3,7},{4,0},{5,1},{6,2},{7,3},{8,12},{9,13},{10,... | collective-permute-start | bytes 1400840 | tf_op jit(solution)/shard_map/ppermute | solution.py:41
  206.2 12.6 %collective-permute-start.29 = (bf16[96,2432]{1,0:T(8,128)(2,1)S(1)}, bf16[96,2432]{1,0:T(8,128)(2,1)S(1)}, u32[]{:S(2)}, u32[]{:S(2)}) collective-permute-start(bf16[96,2432]{1,0:T(8,128)(2,1)S(1)} %add_convert_fusion.1), channel_id=1, source_target_pairs={{0,2},{1,3},{2,0},{3,1},{4,6},{5,7},{6,4},{7,5},{8,10},{9,11},{10,... | collective-permute-start | bytes 1400840 | tf_op jit(solution)/shard_map/ppermute | solution.py:41
  207.9 10.9 %collective-permute-start.30 = (bf16[96,2432]{1,0:T(8,128)(2,1)S(1)}, bf16[96,2432]{1,0:T(8,128)(2,1)S(1)}, u32[]{:S(2)}, u32[]{:S(2)}) collective-permute-start(bf16[96,2432]{1,0:T(8,128)(2,1)S(1)} %add_convert_fusion.1), channel_id=1, source_target_pairs={{0,1},{1,0},{2,3},{3,2},{4,5},{5,4},{6,7},{7,6},{8,9},{9,8},{10,11... | collective-permute-start | bytes 1400840 | tf_op jit(solution)/shard_map/ppermute | solution.py:41
  218.7 1.8 collective-permute-start.31
